TPU v7x, 32 devices: a whole 2x2x4 slice. The times are simulated.
32 devices in a mesh: member: 2 (over y), domain: 4 (over z), role: 4 (over x, core).
Axes of the slice: x: 2, y: 2, z: 4, core: 2. Of those that a mesh axis runs over, the one named last changes fastest.
Arguments:
- ensemble: float32 [256, 32, 512], P('member', 'domain', 'role'), may hold values from -6 to 6
- diffusion: float32 [32, 512], P('domain', 'role'), may hold values from 0.02 to 0.1
- drift_rows: float32 [32, 512], P('domain', 'role'), may hold values from 0.05 to 0.3
- drift_cols: float32 [32, 512], P('domain', 'role'), may hold values from 0.05 to 0.3
- observed_cells: int32 [4, 1024], P('domain'), may hold values from 0 to 4095
- observed_count: int32 [4], P('domain'), may hold values from 256 to 1024
- observed_values: float32 [4, 1024], P('domain'), may hold values from -6 to 6
- observed_weights: float32 [4, 1024], P('domain'), may hold values from 0.5 to 4
Outputs:
- analysis: float32 [256, 32, 512], P('member', 'domain', 'role')
All inputs are finite; a program needn't handle non-finite values.
Results may differ from a plain program's by a relative error of at most 0.0003.
Values sent between devices are 32-bit elements; how exact they have to be, the bound alone decides.
No kernel may reach another device: no remote copies, remote signals or barrier semaphores. Data moves between devices by JAX's collectives and lax.ppermute only.
A program may use at most 64 MiB of HBM per device.

v0:
```python
import functools

import jax
import jax.numpy as jnp
from jax import lax
from jax.experimental import pallas as pl
from jax.experimental.pallas import tpu as pltpu
from jax.sharding import PartitionSpec as P


STEPS = 4
ITERS = 6
LEAD = 16


VMEM = pl.BlockSpec(memory_space=pltpu.VMEM)
SMEM = pl.BlockSpec(memory_space=pltpu.SMEM)
ROOM = 1 << 20


def struct(*shape, kind=jnp.float32):
    return jax.ShapeDtypeStruct(shape, kind)


def near(shape, kind):
    size = jnp.dtype(kind).itemsize
    for place, extent in enumerate(shape[::-1]):
        unit = (128, 32 // jnp.dtype(kind).itemsize, 1)[min(place, 2)]
        size *= -(-extent // unit) * unit
    return size <= ROOM


def call(body, outs, *args, scratch=(), scalars=0, raw=0, result=False):
    placed = list(args[: scalars + raw])
    for value in args[scalars + raw :]:
        if near(value.shape, value.dtype):
            value = pltpu.with_memory_space_constraint(value, pltpu.VMEM)
        placed.append(value)
    if not result:
        outs = jax.tree.map(
            lambda s: pltpu.VMEM(s.shape, s.dtype) if near(s.shape, s.dtype) else s, outs
        )
    return pl.pallas_call(
        body,
        out_shape=outs,
        in_specs=[SMEM] * scalars + [VMEM] * (len(args) - scalars),
        out_specs=tuple(VMEM for _ in outs) if isinstance(outs, tuple) else VMEM,
        scratch_shapes=scratch,
    )(*placed)


def halves(value):
    upper = value.astype(jnp.bfloat16)
    lower = (value - upper.astype(jnp.float32)).astype(jnp.bfloat16)
    return upper, lower


def dot(a, b, dims=((1,), (0,))):
    return lax.dot_general(a, b, (dims, ((), ())), preferred_element_type=jnp.float32)


def dot3(a, b, dims=((1,), (0,))):
    return dot(a[0], b[0], dims) + (dot(a[0], b[1], dims) + dot(a[1], b[0], dims))


def loop(count, body):
    if count <= 16:
        for i in range(count):
            body(i)
    else:
        lax.fori_loop(0, count, lambda i, c: (body(i), c)[1], 0)


def parted(cols):
    cut = (cols // 2 + 16) // 8 * 8
    return cut, 8, cut - 8


def parity(axis):
    return lax.rem(lax.axis_index(axis), 2)


def pack_kernel(axis, ens, diffusion, drift_rows, drift_cols, field, kept, early, late, left, right):
    odd = parity(axis)
    rows, cols, members = field.shape
    width = STEPS
    cut = parted(cols)[0]
    lanes = pl.ds(0, members)
    for r in range(rows):
        turned = ens[pl.ds(r, members, stride=rows)].T
        field[r] = turned
        part = pl.ds(r * width, width)
        left[part, lanes] = turned[:width]
        right[part, lanes] = turned[cols - width :]
    for i in range(width):
        part = pl.ds(i * cut, cut)
        early[part, lanes] = field[i + odd * (rows - width), pl.ds(0, cut)]
        late[part, lanes] = field[i + (1 - odd) * (rows - width), pl.ds(0, cut)]
    near_edge = jnp.zeros((rows, cols), jnp.float32)
    far_edge = near_edge
    lane = lax.broadcasted_iota(jnp.int32, (rows, cols), 1)
    for k, part in enumerate((diffusion, drift_rows, drift_cols)):
        at = pl.ds(width * cut + k * width, width)
        top, bottom = part[:width], part[rows - width :]
        early[at, pl.ds(0, cols)] = jnp.where(odd == 0, top, bottom)
        late[at, pl.ds(0, cols)] = jnp.where(odd == 0, bottom, top)
        value = part[...]
        kept[k] = value
        mine = (lane >= k * width) & (lane < (k + 1) * width)
        if k:
            near_edge = jnp.where(mine, pltpu.roll(value, k * width, 1), near_edge)
        else:
            near_edge = jnp.where(mine, value, near_edge)
        far_edge = jnp.where(mine, pltpu.roll(value, (k + 1) * width, 1), far_edge)
    left[pl.ds(rows * width, rows), pl.ds(0, cols)] = near_edge
    right[pl.ds(rows * width, rows), pl.ds(0, cols)] = far_edge


def turn_kernel(axis, field, left, right, after, early, late):
    rows, cols, members = field.shape
    odd = parity(axis)
    width = STEPS
    area = width * width
    cut = parted(cols)[0]
    size = cols - cut
    lanes = pl.ds(0, members)
    for i in range(width):
        at = pl.ds(i * size, size)
        early[at, lanes] = field[i + odd * (rows - width), pl.ds(cut, size)]
        late[at, lanes] = field[i + (1 - odd) * (rows - width), pl.ds(cut, size)]
    base = width * size
    for i, side in enumerate((left, right)):
        at = pl.ds(base + i * area, area)
        top, bottom = side[pl.ds(0, area)], side[pl.ds((rows - width) * width, area)]
        early[at] = jnp.where(odd == 0, top, bottom)
        late[at] = jnp.where(odd == 0, bottom, top)
        at = pl.ds(base + 2 * area + i * width, width)
        top = side[pl.ds(rows * width, width)]
        bottom = side[pl.ds(rows * width + rows - width, width)]
        early[at] = jnp.where(odd == 0, top, bottom)
        late[at] = jnp.where(odd == 0, bottom, top)


def widen(write, line, columns, members):
    for at, parts in columns:
        size = parts[0].shape[0]
        diffusion, rowwise, colwise = (
            jnp.broadcast_to(p[:, line : line + 1], (size, members)) for p in parts
        )
        here = pl.ds(at, size)
        write(0, here, 1.0 - 4.0 * diffusion - rowwise - colwise)
        write(1, here, diffusion)
        write(2, here, diffusion + rowwise)
        write(3, here, diffusion + colwise)


def spread_rows(spread, lines, columns, members):
    for line, row in lines:

        def write(k, here, value, row=row):
            spread[k, row, here] = value

        widen(write, line, columns, members)


def march(rows, even, odd, spread, ranges, finals, store):
    width = STEPS
    source, target = even, odd
    for step in range(1, STEPS + 1):
        last = step == STEPS

        def advance(r, source=source, target=target, last=last):
            for at, size in finals if last else ranges:
                here = pl.ds(at, size)
                value = (
                    spread[0, r, here] * source[r, here]
                    + spread[1, r, here] * (source[r + 1, here] + source[r, pl.ds(at + 1, size)])
                    + spread[2, r, here] * source[r - 1, here]
                    + spread[3, r, here] * source[r, pl.ds(at - 1, size)]
                )
                if last:
                    store(r - width, at, value)
                else:
                    target[r, here] = value

        loop(rows + 2 * width - 2 * step, lambda i: advance(i + step))
        source, target = target, source


def coefficient_rows(odd, kept, early, late, stage, cut):
    rows, cols = kept.shape[1:]
    width = STEPS
    for k in range(3):
        at = pl.ds(width * cut + k * width, width), pl.ds(0, cols)
        stage[k, pl.ds(0, width)] = jnp.where(odd == 0, early[at], late[at])
        stage[k, pl.ds(width, width)] = jnp.where(odd == 0, late[at], early[at])
    lines = [(i, i) for i in range(1, width)]
    lines += [(width + i, width + rows + i) for i in range(width - 1)]
    inside = [(r, width + r) for r in range(rows)]
    return [kept[k].T for k in range(3)], inside, [stage[k].T for k in range(3)], lines


def middle_kernel(axis, field, kept, early, late, out, one, two, spread, stage):
    rows, cols, members = field.shape
    width = STEPS
    cut, low, high = parted(cols)
    lanes = pl.ds(0, members)
    odd = parity(axis)
    own, inside, beyond, lines = coefficient_rows(odd, kept, early, late, stage, cut)
    for parts, places in ((beyond, lines), (own, inside)):
        spread_rows(spread, places, [(LEAD, [p[:cut] for p in parts])], members)
    here = pl.ds(LEAD, cut)
    for i in range(width):
        part = pl.ds(i * cut, cut)
        one[i + odd * (rows + width), here] = early[part, lanes]
        one[i + (1 - odd) * (rows + width), here] = late[part, lanes]
    for r in range(rows):
        one[width + r, here] = field[r, pl.ds(0, cut)]

    def store(r, at, value):
        out[r] = value

    march(rows, one, two, spread, [(LEAD, cut)], [(LEAD + low, high - low)], store)


def sides_kernel(
    axis,
    field,
    kept,
    early,
    late,
    left,
    right,
    early_rest,
    late_rest,
    out,
    one,
    two,
    spread,
    stage,
):
    rows, cols, members = field.shape
    width = STEPS
    area = width * width
    cut, low, high = parted(cols)
    first, second = low + 8, high - 8
    size = cols - cut
    base = width * size
    lanes = pl.ds(0, members)
    odd = parity(axis)
    own, inside, beyond, lines = coefficient_rows(odd, kept, early, late, stage, cut)
    for side in range(2):
        at = pl.ds(base + 2 * area + side * width, width), pl.ds(0, cols)
        stage[3 + side, pl.ds(0, width)] = jnp.where(odd == 0, early_rest[at], late_rest[at])
        stage[3 + side, pl.ds(width, width)] = jnp.where(odd == 0, late_rest[at], early_rest[at])
    edge = pl.ds(rows * width, rows), pl.ds(0, cols)
    for parts, near_part, far_part, places in (
        (beyond, stage[3].T, stage[4].T, lines),
        (own, left[edge].T, right[edge].T, inside),
    ):
        halo = [slice(k * width, (k + 1) * width) for k in range(3)]
        columns = [
            (LEAD - width, [near_part[h] for h in halo]),
            (LEAD, [p[:first] for p in parts]),
            (LEAD + second, [p[second:] for p in parts]),
            (LEAD + cols, [far_part[h] for h in halo]),
        ]
        spread_rows(spread, places, columns, members)
    before = pl.ds(LEAD - width, width)
    after = pl.ds(LEAD + cols, width)
    for i in range(width):
        for j, strip, rest in (
            (i + odd * (rows + width), early, early_rest),
            (i + (1 - odd) * (rows + width), late, late_rest),
        ):
            one[j, before] = rest[pl.ds(base + i * width, width), lanes]
            one[j, pl.ds(LEAD, first)] = strip[pl.ds(i * cut, first), lanes]
            one[j, pl.ds(LEAD + second, cut - second)] = strip[
                pl.ds(i * cut + second, cut - second), lanes
            ]
            one[j, pl.ds(LEAD + cut, size)] = rest[pl.ds(i * size, size), lanes]
            one[j, after] = rest[pl.ds(base + area + i * width, width), lanes]
    for r in range(rows):
        part = pl.ds(r * width, width)
        one[width + r, before] = left[part, lanes]
        one[width + r, pl.ds(LEAD, first)] = field[r, pl.ds(0, first)]
        one[width + r, pl.ds(LEAD + second, cols - second)] = field[
            r, pl.ds(second, cols - second)
        ]
        one[width + r, after] = right[part, lanes]

    def store(r, at, value):
        if at == LEAD:
            out[r, pl.ds(cols - high, low)] = value
        else:
            out[r, pl.ds(0, cols - high)] = value

    march(
        rows,
        one,
        two,
        spread,
        [(LEAD + second, cols - second + 8), (LEAD - 8, first + 8)],
        [(LEAD + high, cols - high), (LEAD, low)],
        store,
    )


def weight_kernel(axis, count, cells, values, weights, out):
    cols, twice = out.shape
    rows = twice // 2
    slots = cells.shape[1]
    full = cols * lax.axis_size(axis)
    cell = cells[...]
    if full & (full - 1):
        row_of = lax.div(cell, full)
    else:
        row_of = lax.shift_right_logical(cell, full.bit_length() - 1)
    col_of = cell - row_of * full - lax.axis_index(axis) * cols
    slot = lax.broadcasted_iota(jnp.int32, (1, slots), 1)
    plain = jnp.where(slot < count[...], weights[...], 0.0)
    valued = plain * values[...]
    here = lax.broadcasted_iota(jnp.int32, (cols, slots), 0) == col_of
    here = jnp.where(here, 1.0, 0.0).astype(jnp.bfloat16)
    line = lax.broadcasted_iota(jnp.int32, (rows, slots), 0) == row_of
    value = jnp.concatenate([jnp.where(line, plain, 0.0), jnp.where(line, valued, 0.0)], axis=0)
    total = jnp.zeros((cols, twice), jnp.float32)
    for _ in range(3):
        part = value.astype(jnp.bfloat16)
        value = value - part.astype(jnp.float32)
        total = total + dot(here, part, ((1,), (1,)))
    out[...] = total


def cell_weights(rows, pieces, weight, b, many):
    plain, valued = [], []
    for i in range(many):
        r = b * many + i
        for start, column, length in pieces:
            source = weight[pl.ds(column, length)]
            line = lax.broadcasted_iota(jnp.int32, source.shape, 1)
            plain.append(jnp.sum(jnp.where(line == r, source, 0.0), axis=1, keepdims=True))
            valued.append(jnp.sum(jnp.where(line == r + rows, source, 0.0), axis=1, keepdims=True))
    return jnp.concatenate(plain, axis=0), jnp.concatenate(valued, axis=0)


def lay_rows(pieces, column_of, size, centre, b, many):
    cols = centre.shape[1]
    for i in range(many):
        row = jnp.zeros((1, cols), jnp.float32)
        for start, column, length in pieces:
            place = lax.broadcasted_iota(jnp.int32, (length, cols), 0) + column
            here = place == lax.broadcasted_iota(jnp.int32, (length, cols), 1)
            part = column_of[i * size + start : i * size + start + length]
            row = row + jnp.sum(jnp.where(here, part, 0.0), axis=0, keepdims=True)
        centre[pl.ds(b * many + i, 1)] = row


def grouping(rows):
    return next(n for n in (4, 2, 1) if rows % n == 0)


def cells_of(ref, b, many, start=0):
    value = ref[pl.ds(start + b * many, many)]
    return value.reshape(many * value.shape[1], value.shape[2])


def lane_mean(value):
    return jnp.sum(value, axis=1, keepdims=True) * (1.0 / value.shape[1])


def wide(parts):
    return jnp.concatenate(parts, axis=1)


def dot_wide(a, both, size):
    value = dot(a[0], both)
    return value[:, :size] + value[:, size:] + dot(a[1], both[:, :size])


def gram_kernel(groups, pieces, own, others, weight, upper, lower, centre, total, tilt):
    rows, size, _ = own.shape
    many = grouping(rows)
    depth = many * size

    def block(b):
        parts = [cells_of(own, b, many)]
        parts += [cells_of(others, b, many, g * rows) for g in range(groups - 1)]
        value = wide(parts) if groups > 1 else parts[0]
        mean = lane_mean(value)
        deviation = value - mean
        plain, valued = cell_weights(rows, pieces, weight, b, many)
        lay_rows(pieces, mean, size, centre, b, many)
        high, low = halves(deviation)
        at = pl.ds(b * depth, depth)
        upper[at] = high
        lower[at] = low
        turned = (deviation * plain).T
        total[...] += dot3(halves(turned), (high, low))
        tilt[...] += jnp.sum(deviation * (valued - plain * mean), axis=0, keepdims=True)

    loop(rows // many, block)


def own_gram_kernel(layout, middle, sides, weight, total, left, right, spread):
    local = total.shape[0]
    total[...] = jnp.zeros_like(total)
    for pieces, own in zip(layout, (middle, sides)):
        rows, size, _ = own.shape
        many = grouping(rows)
        depth = many * size

        def block(b, pieces=pieces, own=own, rows=rows, many=many, depth=depth):
            value = cells_of(own, b, many)
            mean = lane_mean(value)
            deviation = value - mean
            plain, valued = cell_weights(rows, pieces, weight, b, many)
            turned = halves((deviation * plain).T)
            total[...] += dot_wide(turned, wide(halves(deviation)), local)
            if own is sides:
                at = pl.ds(b * depth, depth)
                left[:, at], right[:, at] = turned
                lane = lax.broadcasted_iota(jnp.int32, (depth, local), 1)
                spread[at] = jnp.where(lane == 0, plain, jnp.where(lane == 1, valued, mean))

        loop(rows // many, block)


def tally(total, local, value, partner, plain, valued, mean_own):
    mean_partner = lane_mean(partner)
    counter = partner - mean_partner
    mean = 0.5 * (mean_own + mean_partner)
    apart = 0.5 * (mean_own - mean_partner)
    deviation = value - mean
    pull = valued - plain * mean
    tie = plain * apart

    def add(row, columns):
        total[pl.ds(local + row, 1)] += jnp.sum(columns, axis=0, keepdims=True)

    add(0, deviation * pull)
    add(1, (partner - mean) * pull)
    add(2, deviation * tie)
    add(3, (mean - partner) * tie)
    add(4, jnp.broadcast_to(tie * apart, deviation.shape))
    return counter


def part_deviations(pieces, value, partner, size, upper, lower, centre, b, many):
    value = wide([value, partner])
    mean = lane_mean(value)
    lay_rows(pieces, mean, size, centre, b, many)
    at = pl.ds(b * many * size, many * size)
    upper[at], lower[at] = halves(value - mean)


def first_cross_kernel(pieces, own, other, weight, after, upper, lower, centre, total):
    total[...] = jnp.zeros_like(total)
    rows, size, local = own.shape
    many = grouping(rows)

    def block(b):
        value, partner = cells_of(own, b, many), cells_of(other, b, many)
        mean = lane_mean(value)
        plain, valued = cell_weights(rows, pieces, weight, b, many)
        counter = tally(total, local, value, partner, plain, valued, mean)
        part_deviations(pieces, value, partner, size, upper, lower, centre, b, many)
        turned = ((value - mean) * plain).T
        total[pl.ds(0, local)] += dot_wide(halves(turned), wide(halves(counter)), local)

    loop(rows // many, block)


def last_cross_kernel(own, other, left, right, spread, before, after, total):
    total[...] = before[...]
    rows, size, local = own.shape
    many = grouping(rows)
    depth = many * size

    def block(b):
        at = pl.ds(b * depth, depth)
        value, partner = cells_of(own, b, many), cells_of(other, b, many)
        counter = tally(total, local, value, partner, *(spread[at, i : i + 1] for i in range(3)))
        total[pl.ds(0, local)] += dot_wide(
            (left[:, at], right[:, at]), wide(halves(counter)), local
        )

    loop(rows // many, block)


def deviation_kernel(pieces, own, other, after, upper, lower, centre):
    rows, size, _ = own.shape
    many = grouping(rows)

    def block(b):
        value, partner = cells_of(own, b, many), cells_of(other, b, many)
        part_deviations(pieces, value, partner, size, upper, lower, centre, b, many)

    loop(rows // many, block)


def first_gram_kernel(groups, pieces, own, others, weight, upper, lower, centre, total, tilt):
    total[...] = jnp.zeros_like(total)
    tilt[...] = jnp.zeros_like(tilt)
    gram_kernel(groups, pieces, own, others, weight, upper, lower, centre, total, tilt)


def last_gram_kernel(
    groups, pieces, own, others, weight, before, tilted, gram, upper, lower, centre, total, tilt
):
    total[...] = before[...]
    tilt[...] = tilted[...]
    gram_kernel(groups, pieces, own, others, weight, upper, lower, centre, total, tilt)
    pull = gram.shape[0] - 8
    blocks = total.shape[0] // 128
    innovation = tilt[...]
    at = 0
    gram[pl.ds(pull, 8)] = jnp.zeros((8, 128), jnp.float32)
    for i in range(blocks):
        gram[pl.ds(pull + i, 1)] = innovation[:, i * 128 : (i + 1) * 128]
        for j in range(i, blocks):
            gram[pl.ds(at, 128)] = total[i * 128 : (i + 1) * 128, j * 128 : (j + 1) * 128]
            at += 128


def assemble(first, second, whole):
    blocks = whole.shape[0] // 128
    pull = first.shape[0] - 8
    at = 0
    for i in range(blocks):
        for j in range(i, blocks):
            block = first[pl.ds(at, 128)] + second[pl.ds(at, 128)]
            whole[i * 128 : (i + 1) * 128, j * 128 : (j + 1) * 128] = block
            if j > i:
                whole[j * 128 : (j + 1) * 128, i * 128 : (i + 1) * 128] = block.T
            at += 128
    return wide([first[pl.ds(pull + i, 1)] + second[pl.ds(pull + i, 1)] for i in range(blocks)])


def assemble_pair(first, second, own, other, whole):
    local = own.shape[1]
    cross = first[pl.ds(0, local)] + second[pl.ds(0, local)]
    rest = first[pl.ds(local, 8)] + second[pl.ds(local, 8)]
    square = rest[4:5]
    diagonal = lax.broadcasted_iota(jnp.int32, (local, local), 0) == lax.broadcasted_iota(
        jnp.int32, (local, local), 1
    )
    uprights = []
    for i, part in enumerate((own, other)):
        tie = rest[2 + i : 3 + i]
        upright = jnp.sum(jnp.where(diagonal, tie, 0.0), axis=1, keepdims=True)
        uprights.append(upright)
        at = slice(i * local, (i + 1) * local)
        whole[at, at] = part[...] + upright + (tie - square)
    cross = cross - uprights[0] + (square - rest[3:4])
    whole[:local, local:] = cross
    whole[local:, :local] = cross.T
    return wide([rest[0:1], rest[1:2]])


def analysis_kernel(layout, pair, *rest):
    if pair:
        first, second, own, other, *rest = rest
    else:
        first, second, *rest = rest
    uppers, lowers, centres = rest[0:2], rest[2:4], rest[4:6]
    out, whole, chosen, natural = rest[6:]
    rows, _ = centres[0].shape
    local = natural.shape[2]
    members = whole.shape[0]
    if pair:
        innovation = assemble_pair(first, second, own, other, whole)
    else:
        innovation = assemble(first, second, whole)
    down = lax.broadcasted_iota(jnp.int32, (members, members), 0)
    across = lax.broadcasted_iota(jnp.int32, (members, members), 1)
    identity = jnp.where(down == across, 1.0, 0.0)
    matrix = whole[...] + (members - 1.0) * identity
    parts = halves(matrix)
    square = dot3(parts, parts)
    squares = jnp.sum(jnp.sum(matrix * matrix, axis=1, keepdims=True), axis=0, keepdims=True)
    scaling = jnp.sqrt(squares)
    current = matrix * (1.0 / scaling)
    square = square * (1.0 / scaling) * (1.0 / scaling)
    inverse = None
    for repeat in range(0, ITERS, 2):
        if repeat:
            parts = halves(current)
            square = dot3(parts, parts)
        inner = 0.0625 * square - 0.5625 * current
        outer = 2.25 * identity - 2.4375 * current + 1.6875 * square
        both = outer + dot3(halves(square), halves(inner))
        both_parts = halves(both)
        if repeat + 2 < ITERS:
            twice = dot3(both_parts, both_parts)
            current = dot3(halves(current), halves(twice))
        inverse = both if inverse is None else dot3(halves(inverse), both_parts)
    once = jnp.sum(inverse * innovation, axis=1, keepdims=True)
    once_row = jnp.sum(jnp.where(down == across, once, 0.0), axis=0, keepdims=True)
    shifted = jnp.sum(inverse * once_row, axis=1, keepdims=True) * (1.0 / scaling)
    factor = jnp.sqrt((members - 1.0) / scaling)
    mixing = (factor * inverse + shifted)[:, :local]
    high, low = halves(mixing)
    chosen[:, :local] = high
    chosen[:, local:] = low
    many = grouping(rows)

    def block(b):
        for pieces, upper, lower in zip(layout, uppers, lowers):
            size = upper.shape[0] // rows
            at = pl.ds(b * many * size, many * size)
            value = dot(upper[at], chosen[...])
            value = value[:, :local] + value[:, local:] + dot(lower[at], chosen[:, :local])
            for i in range(many):
                for start, column, length in pieces:
                    natural[i, pl.ds(column, length)] = value[
                        i * size + start : i * size + start + length
                    ]
        for i in range(many):
            r = b * many + i
            middle_row = centres[0][pl.ds(r, 1)] + centres[1][pl.ds(r, 1)]
            out[pl.ds(r, local, stride=rows)] = natural[i].T + middle_row

    loop(rows // many, block)


def shift(value, axes, *moves):
    sizes = [lax.axis_size(a) for a in axes]
    pairs = []
    total = 1
    for s in sizes:
        total *= s
    for flat in range(total):
        rest, place = flat, []
        for s in reversed(sizes):
            place.append(rest % s)
            rest //= s
        place = place[::-1]
        to = 0
        for s, p, m in zip(sizes, place, moves):
            to = to * s + (p + m) % s
        pairs.append((flat, to))
    return lax.ppermute(value, axes if len(axes) > 1 else axes[0], pairs)


def trade(value, axis, first):
    size = lax.axis_size(axis)
    if size % 2:
        raise ValueError("odd ring")
    start = 1 if first else 0
    pairs = [(i % size, (i + 1) % size) for i in range(start, size, 2)]
    return lax.ppermute(value, axis, pairs + [(j, i) for i, j in pairs])


def role_sums(value):
    size = lax.axis_size("role")
    if size & (size - 1) or size == 1:
        return [(lax.psum(value, "role"), jnp.zeros_like(value))]
    stages = []
    step = 1
    while step < size:
        other = lax.ppermute(value, "role", [(i, i ^ step) for i in range(size)])
        stages.append((value, other))
        value = value + other
        step *= 2
    return stages


def shards(
    ensemble,
    diffusion,
    drift_rows,
    drift_cols,
    observed_cells,
    observed_count,
    observed_values,
    observed_weights,
):
    groups = lax.axis_size("member")
    local, rows, cols = ensemble.shape
    members = local * groups
    width = STEPS
    lanes = max(local, cols)
    cut, low, high = parted(cols)
    strip = struct(width * cut + 4 * width, lanes)
    rest = struct(width * (cols - cut) + 2 * width * width + 2 * width, lanes)
    edge = struct(rows * width + rows, lanes)
    field, kept, early, late, left, right = call(
        functools.partial(pack_kernel, "domain"),
        (struct(rows, cols, local), struct(3, rows, cols), strip, strip, edge, edge),
        ensemble.reshape(local * rows, cols),
        diffusion,
        drift_rows,
        drift_cols,
        raw=4,
    )
    early = trade(early, "domain", True)
    late = trade(late, "domain", False)
    left, right = shift(right, ("role",), 1), shift(left, ("role",), -1)
    weight = call(
        functools.partial(weight_kernel, "role"),
        struct(cols, 2 * rows),
        observed_count.reshape(1, 1),
        observed_cells,
        observed_values,
        observed_weights,
        raw=4,
    )
    early_rest, late_rest = call(
        functools.partial(turn_kernel, "domain"), (rest, rest), field, left, right, weight
    )
    early_rest = trade(early_rest, "domain", True)
    late_rest = trade(late_rest, "domain", False)
    padded = pltpu.VMEM((rows + 2 * width, cols + 2 * LEAD, local), jnp.float32)
    scratch = (
        padded,
        padded,
        pltpu.VMEM((4, rows + 2 * width, cols + 2 * LEAD, local), jnp.float32),
        pltpu.VMEM((5, 2 * width, cols), jnp.float32),
    )
    middle = call(
        functools.partial(middle_kernel, "domain"),
        struct(rows, high - low, local),
        field,
        kept,
        early,
        late,
        scratch=scratch,
    )
    sides = call(
        functools.partial(sides_kernel, "domain"),
        struct(rows, cols - high + low, local),
        field,
        kept,
        early,
        late,
        left,
        right,
        early_rest,
        late_rest,
        scratch=scratch,
    )

    def gathered(value):
        others = [shift(value, ("member",), s) for s in range(1, groups)]
        return jnp.concatenate(others, axis=0) if len(others) > 1 else others[0]

    middle_others = gathered(middle)
    sides_others = gathered(sides)
    layout = (
        ((0, low, high - low),),
        ((0, high, cols - high), (cols - high, 0, low)),
    )

    def deviations(columns):
        one = struct(rows * columns, members, kind=jnp.bfloat16)
        return one, one, struct(rows, cols)

    pair = groups == 2 and local % 128 == 0
    if pair:
        sided = rows * (cols - high + low)
        half = struct(local, sided, kind=jnp.bfloat16)
        alone, left_half, right_half, spread = call(
            functools.partial(own_gram_kernel, layout),
            (struct(local, local), half, half, struct(sided, local)),
            middle,
            sides,
            weight,
        )
        stages = role_sums(alone)
        started = sum(stages[0])
        cross = struct(local + 8, local)
        upper_a, lower_a, centre_a, total = call(
            functools.partial(first_cross_kernel, layout[0]),
            (*deviations(high - low), cross),
            middle,
            middle_others,
            weight,
            started,
        )
        alone, arriving = stages[-1]
        total, alone = lax.optimization_barrier((total, alone))
        alone = alone + arriving
        gram = call(
            last_cross_kernel,
            cross,
            sides,
            sides_others,
            left_half,
            right_half,
            spread,
            total,
            alone,
        )
        gram, alone = lax.optimization_barrier((gram, alone))
        facing = shift(alone, ("member",), 1)
        grams = (*role_sums(gram)[-1], alone, facing)
        upper_b, lower_b, centre_b = call(
            functools.partial(deviation_kernel, layout[1]),
            deviations(cols - high + low),
            sides,
            sides_others,
            gram,
        )
    else:
        blocks = members // 128
        size = blocks * (blocks + 1) // 2 * 128 + 8
        square = struct(members, members)
        vector = struct(1, members)
        upper_a, lower_a, centre_a, total, tilt = call(
            functools.partial(first_gram_kernel, groups, layout[0]),
            (*deviations(high - low), square, vector),
            middle,
            middle_others,
            weight,
        )
        gram, upper_b, lower_b, centre_b = call(
            functools.partial(last_gram_kernel, groups, layout[1]),
            (struct(size, 128), *deviations(cols - high + low)),
            sides,
            sides_others,
            weight,
            total,
            tilt,
            scratch=(
                pltpu.VMEM((members, members), jnp.float32),
                pltpu.VMEM((1, members), jnp.float32),
            ),
        )
        grams = role_sums(gram)[-1]
    return call(
        functools.partial(analysis_kernel, layout, pair),
        struct(local * rows, cols),
        *grams,
        upper_a,
        upper_b,
        lower_a,
        lower_b,
        centre_a,
        centre_b,
        scratch=(
            pltpu.VMEM((members, members), jnp.float32),
            pltpu.VMEM((members, 2 * local), jnp.bfloat16),
            pltpu.VMEM((4, cols, local), jnp.float32),
        ),
        result=True,
    ).reshape(local, rows, cols)


def solution(mesh):
    placed = (
        P("member", "domain", "role"),
        P("domain", "role"),
        P("domain", "role"),
        P("domain", "role"),
        P("domain", None),
        P("domain"),
        P("domain", None),
        P("domain", None),
    )
    return jax.shard_map(
        shards, mesh=mesh, in_specs=placed, out_specs=P("member", "domain", "role"), check_vma=False
    )
```

profile of v0, /device:TPU:0, one launch (start us, length us, event | category | flops | bytes accessed | tf_op | source)
XLA Modules:
  0.0 42.9 jit_solution(5798613082909627701)
XLA Ops:
  0.0 1.3 %shard_map.82 = (f32[8,128,128]{2,1,0:T(8,128)S(1)}, f32[3,8,128]{2,1,0:T(8,128)S(1)}, f32[336,128]{1,0:T(8,128)S(1)}, f32[336,128]{1,0:T(8,128)S(1)}, f32[40,128]{1,0:T(8,128)S(1)}, /*index=5*/f32[40,128]{1,0:T(8,128)S(1)}) custom-call(f32[1024,128]{1,0:T(8,128)} %bitcast.4, f32[8,128]{1,0:T(8,128)} %diffusion.1, f32[8,128]{1,0:T(8,128)} %drift_rows.1, ...), custom_call_target="tpu_custom_call" | custom-call | tf_op jit(solution)/shard_map/pallas_call | solution.py:43
  1.3 5.1 %collective-permute-start = (f32[336,128]{1,0:T(8,128)S(1)}, f32[336,128]{1,0:T(8,128)S(1)}, u32[]{:S(2)}, u32[]{:S(2)}) collective-permute-start(f32[336,128]{1,0:T(8,128)S(1)} %get-tuple-element.30), channel_id=1, source_target_pairs={{4,8},{12,0},{8,4},{0,12},{5,9},{13,1},{9,5},{1,13},{6,10},{14,2},... | collective-permute-start | bytes 516104 | tf_op jit(solution)/shard_map/ppermute | solution.py:652
  6.5 0.0 collective-permute-start.1
  6.5 0.0 collective-permute-start.2
  6.5 1.7 %collective-permute-start.3 = (f32[40,128]{1,0:T(8,128)S(1)}, f32[40,128]{1,0:T(8,128)S(1)}, u32[]{:S(2)}, u32[]{:S(2)}) collective-permute-start(f32[40,128]{1,0:T(8,128)S(1)} %get-tuple-element.33), channel_id=1, source_target_pairs={{0,3},{1,0},{2,1},{3,2},{4,7},{5,4},{6,5},{7,6},{8,11},{9,8},{10,9... | collective-permute-start | bytes 61448 | tf_op jit(solution)/shard_map/ppermute | solution.py:643
  8.9 1.1 %shard_map.83.after.weight = f32[128,16]{1,0:T(8,128)S(1)} custom-call(s32[1,1]{1,0:T(1,128)} %bitcast.3.count, s32[1,1024]{1,0:T(1,128)} %cells.1, f32[1,1024]{1,0:T(1,128)} %values.1, f32[1,1024]{1,0:T(1,128)} %weights.1), custom_call_target="tpu_custom_call" | custom-call | tf_op jit(solution)/shard_map/pallas_call | solution.py:43
  10.0 0.0 collective-permute-done.2.left
  10.0 0.0 collective-permute-done.3.right
  10.1 1.0 %collective-permute-start.4 = (f32[232,128]{1,0:T(8,128)S(1)}, f32[232,128]{1,0:T(8,128)S(1)}, u32[]{:S(2)}, u32[]{:S(2)}) collective-permute-start(f32[232,128]{1,0:T(8,128)S(1)} %get-tuple-element.34), channel_id=1, source_target_pairs={{4,8},{12,0},{8,4},{0,12},{5,9},{13,1},{9,5},{1,13},{6,10},{14,2},... | collective-permute-start | bytes 356360 | tf_op jit(solution)/shard_map/ppermute | solution.py:652
  11.1 1.2 %collective-permute-start.5 = (f32[232,128]{1,0:T(8,128)S(1)}, f32[232,128]{1,0:T(8,128)S(1)}, u32[]{:S(2)}, u32[]{:S(2)}) collective-permute-start(f32[232,128]{1,0:T(8,128)S(1)} %get-tuple-element.35), channel_id=1, source_target_pairs={{0,4},{8,12},{4,0},{12,8},{1,5},{9,13},{5,1},{13,9},{2,6},{10,14},... | collective-permute-start | bytes 356360 | tf_op jit(solution)/shard_map/ppermute | solution.py:652
  12.3 0.0 collective-permute-done.early
  12.3 2.7 %collective-permute-done.1.late = f32[336,128]{1,0:T(8,128)S(1)} collective-permute-done((f32[336,128]{1,0:T(8,128)S(1)}, f32[336,128]{1,0:T(8,128)S(1)}, u32[]{:S(2)}, u32[]{:S(2)}) %collective-permute-start.1) | collective-permute-done | bytes 172064 | tf_op jit(solution)/shard_map/ppermute | solution.py:652
  14.9 1.0 %shard_map.86.middle.own = f32[8,64,128]{2,1,0:T(8,128)S(1)} custom-call(f32[8,128,128]{2,1,0:T(8,128)S(1)} %get-tuple-element.28.field, f32[3,8,128]{2,1,0:T(8,128)S(1)} %get-tuple-element.29.kept, f32[336,128]{1,0:T(8,128)S(1)} %collective-permute-done.early, f32[336,128]{1,0:T(8,128)S(1)} %collective-permute-done.1.late), custom_call_target="tpu_custom_call" | custom-call | tf_op jit(solution)/shard_map/pallas_call | solution.py:43
  16.0 1.6 %collective-permute-start.7 = (f32[8,64,128]{2,1,0:T(8,128)S(1)}, f32[8,64,128]{2,1,0:T(8,128)S(1)}, u32[]{:S(2)}, u32[]{:S(2)}) collective-permute-start(f32[8,64,128]{2,1,0:T(8,128)S(1)} %shard_map.86.middle.own), channel_id=1, source_target_pairs={{0,16},{16,0},{1,17},{17,1},{2,18},{18,2},{3,19},{19,3},{4,20},{20... | collective-permute-start | bytes 786440 | tf_op jit(solution)/shard_map/ppermute | solution.py:643
  17.6 0.0 collective-permute-done.4.early_rest
  17.6 1.9 %collective-permute-done.5.late_rest = f32[232,128]{1,0:T(8,128)S(1)} collective-permute-done((f32[232,128]{1,0:T(8,128)S(1)}, f32[232,128]{1,0:T(8,128)S(1)}, u32[]{:S(2)}, u32[]{:S(2)}) %collective-permute-start.5) | collective-permute-done | bytes 118816 | tf_op jit(solution)/shard_map/ppermute | solution.py:652
  19.5 1.3 %shard_map.85.sides.own = f32[8,64,128]{2,1,0:T(8,128)S(1)} custom-call(f32[8,128,128]{2,1,0:T(8,128)S(1)} %get-tuple-element.28.field, f32[3,8,128]{2,1,0:T(8,128)S(1)} %get-tuple-element.29.kept, f32[336,128]{1,0:T(8,128)S(1)} %collective-permute-done.early, f32[336,128]{1,0:T(8,128)S(1)} %collective-permute-done.1.late, ...), custom_call_target="tpu_custom_call" | custom-call | tf_op jit(solution)/shard_map/pallas_call | solution.py:43
  20.8 1.6 %collective-permute-start.6 = (f32[8,64,128]{2,1,0:T(8,128)S(1)}, f32[8,64,128]{2,1,0:T(8,128)S(1)}, u32[]{:S(2)}, u32[]{:S(2)}) collective-permute-start(f32[8,64,128]{2,1,0:T(8,128)S(1)} %shard_map.85.sides.own), channel_id=1, source_target_pairs={{0,16},{16,0},{1,17},{17,1},{2,18},{18,2},{3,19},{19,3},{4,20},{20... | collective-permute-start | bytes 786440 | tf_op jit(solution)/shard_map/ppermute | solution.py:643
  22.4 1.0 %shard_map.87 = (f32[128,128]{1,0:T(8,128)S(1)}, bf16[128,512]{1,0:T(8,128)(2,1)S(1)}, bf16[128,512]{1,0:T(8,128)(2,1)S(1)}, f32[512,128]{1,0:T(8,128)S(1)}) custom-call(f32[8,64,128]{2,1,0:T(8,128)S(1)} %shard_map.86.middle.own, f32[8,64,128]{2,1,0:T(8,128)S(1)} %shard_map.85.sides.own, f32[128,16]{1,0:T(8,128)S(1)} %shard_map.83.after.weight), custom_call_target="tpu_custom_call" | custom-call | tf_op jit(solution)/shard_map/pallas_call | solution.py:43
  23.4 0.2 collective-permute-start.8
  23.6 1.2 %collective-permute-done.8 = f32[128,128]{1,0:T(8,128)S(1)} collective-permute-done((f32[128,128]{1,0:T(8,128)S(1)}, f32[128,128]{1,0:T(8,128)S(1)}, u32[]{:S(2)}, u32[]{:S(2)}) %collective-permute-start.8) | collective-permute-done | bytes 65568 | tf_op jit(solution)/shard_map/ppermute | solution.py:662
  24.7 1.8 %collective-permute-start.9 = (f32[128,128]{1,0:T(8,128)S(1)}, f32[128,128]{1,0:T(8,128)S(1)}, u32[]{:S(2)}, u32[]{:S(2)}) collective-permute-start(f32[128,128]{1,0:T(8,128)S(1)} %add.10.after), channel_id=1, source_target_pairs={{0,2},{1,3},{2,0},{3,1},{4,6},{5,7},{6,4},{7,5},{8,10},{9,11},{10,... | collective-permute-start | bytes 196616 | tf_op jit(solution)/shard_map/ppermute | solution.py:662
  26.6 0.0 collective-permute-done.7.other
  26.6 1.2 %shard_map.88 = (bf16[512,256]{1,0:T(8,128)(2,1)S(1)}, bf16[512,256]{1,0:T(8,128)(2,1)S(1)}, f32[8,128]{1,0:T(8,128)S(1)}, f32[136,128]{1,0:T(8,128)S(1)}) custom-call(f32[8,64,128]{2,1,0:T(8,128)S(1)} %shard_map.86.middle.own, f32[8,64,128]{2,1,0:T(8,128)S(1)} %collective-permute-done.7.other, f32[128,16]{1,0:T(8,128)S(1)} %shard_map.83.after.weight, ...), custom_call_target="tpu_custom_call" | custom-call | tf_op jit(solution)/shard_map/pallas_call | solution.py:43
  27.8 1.3 %collective-permute-done.9 = f32[128,128]{1,0:T(8,128)S(1)} collective-permute-done((f32[128,128]{1,0:T(8,128)S(1)}, f32[128,128]{1,0:T(8,128)S(1)}, u32[]{:S(2)}, u32[]{:S(2)}) %collective-permute-start.9) | collective-permute-done | bytes 65568 | tf_op jit(solution)/shard_map/ppermute | solution.py:662
  29.1 0.5 %collective-permute-done.6.other = f32[8,64,128]{2,1,0:T(8,128)S(1)} collective-permute-done((f32[8,64,128]{2,1,0:T(8,128)S(1)}, f32[8,64,128]{2,1,0:T(8,128)S(1)}, u32[]{:S(2)}, u32[]{:S(2)}) %collective-permute-start.6) | collective-permute-done | bytes 262176 | tf_op jit(solution)/shard_map/ppermute | solution.py:643
  29.6 0.9 %shard_map.89.after = f32[136,128]{1,0:T(8,128)S(1)} custom-call(f32[8,64,128]{2,1,0:T(8,128)S(1)} %shard_map.85.sides.own, f32[8,64,128]{2,1,0:T(8,128)S(1)} %collective-permute-done.6.other, bf16[128,512]{1,0:T(8,128)(2,1)S(1)} %get-tuple-element.36.left, bf16[128,512]{1,0:T(8,128)(2,1)S(1)} %get-tuple-element.37.right, ...), custom_call_target="tpu_custom_call" | custom-call | tf_op jit(solution)/shard_map/pallas_call | solution.py:43
  30.5 0.1 collective-permute-start.10
  30.6 1.2 %collective-permute-done.10 = f32[136,128]{1,0:T(8,128)S(1)} collective-permute-done((f32[136,128]{1,0:T(8,128)S(1)}, f32[136,128]{1,0:T(8,128)S(1)}, u32[]{:S(2)}, u32[]{:S(2)}) %collective-permute-start.10) | collective-permute-done | bytes 69664 | tf_op jit(solution)/shard_map/ppermute | solution.py:662
  31.8 1.6 %collective-permute-start.11 = (f32[136,128]{1,0:T(8,128)S(1)}, f32[136,128]{1,0:T(8,128)S(1)}, u32[]{:S(2)}, u32[]{:S(2)}) collective-permute-start(f32[136,128]{1,0:T(8,128)S(1)} %add.12.rest_0_), channel_id=1, source_target_pairs={{0,2},{1,3},{2,0},{3,1},{4,6},{5,7},{6,4},{7,5},{8,10},{9,11},{10,... | collective-permute-start | bytes 208904 | tf_op jit(solution)/shard_map/ppermute | solution.py:662
  33.4 1.5 %collective-permute-start.12 = (f32[128,128]{1,0:T(8,128)S(1)}, f32[128,128]{1,0:T(8,128)S(1)}, u32[]{:S(2)}, u32[]{:S(2)}) collective-permute-start(f32[128,128]{1,0:T(8,128)S(1)} %add.11.after.rest_2_), channel_id=1, source_target_pairs={{0,16},{16,0},{1,17},{17,1},{2,18},{18,2},{3,19},{19,3},{4,20},{20... | collective-permute-start | bytes 196616 | tf_op jit(solution)/shard_map/ppermute | solution.py:643
  34.9 0.2 shard_map.90
  35.1 2.5 %collective-permute-done.12.rest_3_ = f32[128,128]{1,0:T(8,128)S(1)} collective-permute-done((f32[128,128]{1,0:T(8,128)S(1)}, f32[128,128]{1,0:T(8,128)S(1)}, u32[]{:S(2)}, u32[]{:S(2)}) %collective-permute-start.12) | collective-permute-done | bytes 65568 | tf_op jit(solution)/shard_map/ppermute | solution.py:643
  37.6 0.0 collective-permute-done.11.rest_1_
  37.6 5.3 %shard_map.91 = f32[1024,128]{1,0:T(8,128)} custom-call(f32[136,128]{1,0:T(8,128)S(1)} %add.12.rest_0_, f32[136,128]{1,0:T(8,128)S(1)} %collective-permute-done.11.rest_1_, f32[128,128]{1,0:T(8,128)S(1)} %add.11.after.rest_2_, f32[128,128]{1,0:T(8,128)S(1)} %collective-permute-done.12.rest_3_, bf16[512,256]{1,0:T(8,128)(2,1)S(1)} %get-tuple-element.45.rest_4_, ...), custom_call_target="tpu_custom_call" | custom-call | tf_op jit(solution)/shard_map/pallas_call | solution.py:43
  (4 shorter events, 0.1 us)
Async XLA Ops:
  1.3 10.9 %collective-permute-start = (f32[336,128]{1,0:T(8,128)S(1)}, f32[336,128]{1,0:T(8,128)S(1)}, u32[]{:S(2)}, u32[]{:S(2)}) collective-permute-start(f32[336,128]{1,0:T(8,128)S(1)} %get-tuple-element.30), channel_id=1, source_target_pairs={{4,8},{12,0},{8,4},{0,12},{5,9},{13,1},{9,5},{1,13},{6,10},{14,2},... | collective-permute-start | bytes 516104 | tf_op jit(solution)/shard_map/ppermute | solution.py:652
  6.5 8.5 %collective-permute-start.1 = (f32[336,128]{1,0:T(8,128)S(1)}, f32[336,128]{1,0:T(8,128)S(1)}, u32[]{:S(2)}, u32[]{:S(2)}) collective-permute-start(f32[336,128]{1,0:T(8,128)S(1)} %get-tuple-element.31), channel_id=1, source_target_pairs={{0,4},{8,12},{4,0},{12,8},{1,5},{9,13},{5,1},{13,9},{2,6},{10,14},... | collective-permute-start | bytes 516104 | tf_op jit(solution)/shard_map/ppermute | solution.py:652
  6.5 3.5 %collective-permute-start.2 = (f32[40,128]{1,0:T(8,128)S(1)}, f32[40,128]{1,0:T(8,128)S(1)}, u32[]{:S(2)}, u32[]{:S(2)}) collective-permute-start(f32[40,128]{1,0:T(8,128)S(1)} %get-tuple-element.32), channel_id=1, source_target_pairs={{0,1},{1,2},{2,3},{3,0},{4,5},{5,6},{6,7},{7,4},{8,9},{9,10},{10,1... | collective-permute-start | bytes 61448 | tf_op jit(solution)/shard_map/ppermute | solution.py:643
  6.5 3.6 %collective-permute-start.3 = (f32[40,128]{1,0:T(8,128)S(1)}, f32[40,128]{1,0:T(8,128)S(1)}, u32[]{:S(2)}, u32[]{:S(2)}) collective-permute-start(f32[40,128]{1,0:T(8,128)S(1)} %get-tuple-element.33), channel_id=1, source_target_pairs={{0,3},{1,0},{2,1},{3,2},{4,7},{5,4},{6,5},{7,6},{8,11},{9,8},{10,9... | collective-permute-start | bytes 61448 | tf_op jit(solution)/shard_map/ppermute | solution.py:643
  10.1 7.5 %collective-permute-start.4 = (f32[232,128]{1,0:T(8,128)S(1)}, f32[232,128]{1,0:T(8,128)S(1)}, u32[]{:S(2)}, u32[]{:S(2)}) collective-permute-start(f32[232,128]{1,0:T(8,128)S(1)} %get-tuple-element.34), channel_id=1, source_target_pairs={{4,8},{12,0},{8,4},{0,12},{5,9},{13,1},{9,5},{1,13},{6,10},{14,2},... | collective-permute-start | bytes 356360 | tf_op jit(solution)/shard_map/ppermute | solution.py:652
  11.1 8.4 %collective-permute-start.5 = (f32[232,128]{1,0:T(8,128)S(1)}, f32[232,128]{1,0:T(8,128)S(1)}, u32[]{:S(2)}, u32[]{:S(2)}) collective-permute-start(f32[232,128]{1,0:T(8,128)S(1)} %get-tuple-element.35), channel_id=1, source_target_pairs={{0,4},{8,12},{4,0},{12,8},{1,5},{9,13},{5,1},{13,9},{2,6},{10,14},... | collective-permute-start | bytes 356360 | tf_op jit(solution)/shard_map/ppermute | solution.py:652
  16.0 10.6 %collective-permute-start.7 = (f32[8,64,128]{2,1,0:T(8,128)S(1)}, f32[8,64,128]{2,1,0:T(8,128)S(1)}, u32[]{:S(2)}, u32[]{:S(2)}) collective-permute-start(f32[8,64,128]{2,1,0:T(8,128)S(1)} %shard_map.86.middle.own), channel_id=1, source_target_pairs={{0,16},{16,0},{1,17},{17,1},{2,18},{18,2},{3,19},{19,3},{4,20},{20... | collective-permute-start | bytes 786440 | tf_op jit(solution)/shard_map/ppermute | solution.py:643
  20.8 8.8 %collective-permute-start.6 = (f32[8,64,128]{2,1,0:T(8,128)S(1)}, f32[8,64,128]{2,1,0:T(8,128)S(1)}, u32[]{:S(2)}, u32[]{:S(2)}) collective-permute-start(f32[8,64,128]{2,1,0:T(8,128)S(1)} %shard_map.85.sides.own), channel_id=1, source_target_pairs={{0,16},{16,0},{1,17},{17,1},{2,18},{18,2},{3,19},{19,3},{4,20},{20... | collective-permute-start | bytes 786440 | tf_op jit(solution)/shard_map/ppermute | solution.py:643
  23.4 1.3 %collective-permute-start.8 = (f32[128,128]{1,0:T(8,128)S(1)}, f32[128,128]{1,0:T(8,128)S(1)}, u32[]{:S(2)}, u32[]{:S(2)}) collective-permute-start(f32[128,128]{1,0:T(8,128)S(1)} %get-tuple-element.39), channel_id=1, source_target_pairs={{0,1},{1,0},{2,3},{3,2},{4,5},{5,4},{6,7},{7,6},{8,9},{9,8},{10,11... | collective-permute-start | bytes 196616 | tf_op jit(solution)/shard_map/ppermute | solution.py:662
  24.7 4.3 %collective-permute-start.9 = (f32[128,128]{1,0:T(8,128)S(1)}, f32[128,128]{1,0:T(8,128)S(1)}, u32[]{:S(2)}, u32[]{:S(2)}) collective-permute-start(f32[128,128]{1,0:T(8,128)S(1)} %add.10.after), channel_id=1, source_target_pairs={{0,2},{1,3},{2,0},{3,1},{4,6},{5,7},{6,4},{7,5},{8,10},{9,11},{10,... | collective-permute-start | bytes 196616 | tf_op jit(solution)/shard_map/ppermute | solution.py:662
  30.5 1.3 %collective-permute-start.10 = (f32[136,128]{1,0:T(8,128)S(1)}, f32[136,128]{1,0:T(8,128)S(1)}, u32[]{:S(2)}, u32[]{:S(2)}) collective-permute-start(f32[136,128]{1,0:T(8,128)S(1)} %shard_map.89.after), channel_id=1, source_target_pairs={{0,1},{1,0},{2,3},{3,2},{4,5},{5,4},{6,7},{7,6},{8,9},{9,8},{10,11... | collective-permute-start | bytes 208904 | tf_op jit(solution)/shard_map/ppermute | solution.py:662
  31.8 5.8 %collective-permute-start.11 = (f32[136,128]{1,0:T(8,128)S(1)}, f32[136,128]{1,0:T(8,128)S(1)}, u32[]{:S(2)}, u32[]{:S(2)}) collective-permute-start(f32[136,128]{1,0:T(8,128)S(1)} %add.12.rest_0_), channel_id=1, source_target_pairs={{0,2},{1,3},{2,0},{3,1},{4,6},{5,7},{6,4},{7,5},{8,10},{9,11},{10,... | collective-permute-start | bytes 208904 | tf_op jit(solution)/shard_map/ppermute | solution.py:662
  33.4 4.3 %collective-permute-start.12 = (f32[128,128]{1,0:T(8,128)S(1)}, f32[128,128]{1,0:T(8,128)S(1)}, u32[]{:S(2)}, u32[]{:S(2)}) collective-permute-start(f32[128,128]{1,0:T(8,128)S(1)} %add.11.after.rest_2_), channel_id=1, source_target_pairs={{0,16},{16,0},{1,17},{17,1},{2,18},{18,2},{3,19},{19,3},{4,20},{20... | collective-permute-start | bytes 196616 | tf_op jit(solution)/shard_map/ppermute | solution.py:643
where the time goes:
time: 43.1 us; the launch traced here: 42.9 us
  starting transfers between devices  17.3 us (40%)
  Pallas kernels  13.4 us (31%)
  waiting for transfers between devices  11.4 us (26%)
  between operations  0.76 us (2%)
    pallas_call x10, Pallas kernels, call(): pl.pallas_call(body, out_shape=outs, in_specs=[SMEM] * scalars + [VMEM] *...  13.4 us
    ppermute x4, starting transfers between devices, trade(): return lax.ppermute(value, axis, pairs + [(j, i) for i, j in pairs])  7.32 us
    ppermute x5, starting transfers between devices, shift(): return lax.ppermute(value, axes if len(axes) > 1 else axes[0], pairs)  6.43 us
    ppermute x4, waiting for transfers between devices, trade(): return lax.ppermute(value, axis, pairs + [(j, i) for i, j in pairs])  4.59 us
    ppermute x4, waiting for transfers between devices, role_sums(): other = lax.ppermute(value, 'role', [(i, i ^ step) for i in range(size)])  3.7 us
    ppermute x4, starting transfers between devices, role_sums(): other = lax.ppermute(value, 'role', [(i, i ^ step) for i in range(size)])  3.59 us
    ppermute x5, waiting for transfers between devices, shift(): return lax.ppermute(value, axes if len(axes) > 1 else axes[0], pairs)  3.08 us
  transfers between devices with their start and end apart: 13, of which 7 were waited for; matrix products, arithmetic and copies ran while one was open for 0% of the time, Pallas kernels for 14%

commit v1 on v0

--- a/solution.py
+++ b/solution.py
@@ -71,20 +71,37 @@
         lax.fori_loop(0, count, lambda i, c: (body(i), c)[1], 0)
 
 
+EDGE = 8
+
+
 def parted(cols):
-    cut = (cols // 2 + 16) // 8 * 8
-    return cut, 8, cut - 8
+    return cols * 3 // 8 // 8 * 8, cols * 3 // 4 // 8 * 8
 
 
 def parity(axis):
     return lax.rem(lax.axis_index(axis), 2)
 
 
-def pack_kernel(axis, ens, diffusion, drift_rows, drift_cols, field, kept, early, late, left, right):
+def pack_kernel(
+    axis,
+    ens,
+    diffusion,
+    drift_rows,
+    drift_cols,
+    field,
+    kept,
+    early,
+    late,
+    early_next,
+    late_next,
+    left,
+    right,
+):
     odd = parity(axis)
     rows, cols, members = field.shape
     width = STEPS
-    cut = parted(cols)[0]
+    cut, end = parted(cols)
+    more = end - cut
     lanes = pl.ds(0, members)
     for r in range(rows):
         turned = ens[pl.ds(r, members, stride=rows)].T
@@ -96,6 +113,9 @@
         part = pl.ds(i * cut, cut)
         early[part, lanes] = field[i + odd * (rows - width), pl.ds(0, cut)]
         late[part, lanes] = field[i + (1 - odd) * (rows - width), pl.ds(0, cut)]
+        part = pl.ds(i * more, more)
+        early_next[part, lanes] = field[i + odd * (rows - width), pl.ds(cut, more)]
+        late_next[part, lanes] = field[i + (1 - odd) * (rows - width), pl.ds(cut, more)]
     near_edge = jnp.zeros((rows, cols), jnp.float32)
     far_edge = near_edge
     lane = lax.broadcasted_iota(jnp.int32, (rows, cols), 1)
@@ -121,7 +141,7 @@
     odd = parity(axis)
     width = STEPS
     area = width * width
-    cut = parted(cols)[0]
+    cut = parted(cols)[1]
     size = cols - cut
     lanes = pl.ds(0, members)
     for i in range(width):
@@ -200,35 +220,51 @@
     return [kept[k].T for k in range(3)], inside, [stage[k].T for k in range(3)], lines
 
 
-def middle_kernel(axis, field, kept, early, late, out, one, two, spread, stage):
+def middle_kernel(axis, low, high, pieces, after, field, kept, *refs):
+    strips, (out, one, two, spread, stage) = refs[:-5], refs[-5:]
     rows, cols, members = field.shape
     width = STEPS
-    cut, low, high = parted(cols)
     lanes = pl.ds(0, members)
     odd = parity(axis)
-    own, inside, beyond, lines = coefficient_rows(odd, kept, early, late, stage, cut)
+    own, inside, beyond, lines = coefficient_rows(
+        odd, kept, strips[0], strips[1], stage, parted(cols)[0]
+    )
+    start = pieces[0][3]
+    end = pieces[-1][3] + pieces[-1][4]
     for parts, places in ((beyond, lines), (own, inside)):
-        spread_rows(spread, places, [(LEAD, [p[:cut] for p in parts])], members)
-    here = pl.ds(LEAD, cut)
-    for i in range(width):
-        part = pl.ds(i * cut, cut)
-        one[i + odd * (rows + width), here] = early[part, lanes]
-        one[i + (1 - odd) * (rows + width), here] = late[part, lanes]
+        spread_rows(spread, places, [(LEAD + start, [p[start:end] for p in parts])], members)
+    for pair, strip_cols, first, column, size in pieces:
+        here = pl.ds(LEAD + column, size)
+        for i in range(width):
+            part = pl.ds(i * strip_cols + first, size)
+            one[i + odd * (rows + width), here] = strips[2 * pair][part, lanes]
+            one[i + (1 - odd) * (rows + width), here] = strips[2 * pair + 1][part, lanes]
     for r in range(rows):
-        one[width + r, here] = field[r, pl.ds(0, cut)]
+        one[width + r, pl.ds(LEAD + start, end - start)] = field[r, pl.ds(start, end - start)]
 
     def store(r, at, value):
         out[r] = value
 
-    march(rows, one, two, spread, [(LEAD, cut)], [(LEAD + low, high - low)], store)
+    march(
+        rows,
+        one,
+        two,
+        spread,
+        [(LEAD + start, end - start)],
+        [(LEAD + low, high - low)],
+        store,
+    )
 
 
 def sides_kernel(
     axis,
+    after,
     field,
     kept,
     early,
     late,
+    early_next,
+    late_next,
     left,
     right,
     early_rest,
@@ -240,14 +276,15 @@
     stage,
 ):
     rows, cols, members = field.shape
+    odd = parity(axis)
     width = STEPS
     area = width * width
-    cut, low, high = parted(cols)
-    first, second = low + 8, high - 8
-    size = cols - cut
+    cut, end = parted(cols)
+    more = end - cut
+    first, second, high = 2 * EDGE, end - 2 * EDGE, end - EDGE
+    size = cols - end
     base = width * size
     lanes = pl.ds(0, members)
-    odd = parity(axis)
     own, inside, beyond, lines = coefficient_rows(odd, kept, early, late, stage, cut)
     for side in range(2):
         at = pl.ds(base + 2 * area + side * width, width), pl.ds(0, cols)
@@ -269,16 +306,16 @@
     before = pl.ds(LEAD - width, width)
     after = pl.ds(LEAD + cols, width)
     for i in range(width):
-        for j, strip, rest in (
-            (i + odd * (rows + width), early, early_rest),
-            (i + (1 - odd) * (rows + width), late, late_rest),
+        for j, strip, following, rest in (
+            (i + odd * (rows + width), early, early_next, early_rest),
+            (i + (1 - odd) * (rows + width), late, late_next, late_rest),
         ):
             one[j, before] = rest[pl.ds(base + i * width, width), lanes]
             one[j, pl.ds(LEAD, first)] = strip[pl.ds(i * cut, first), lanes]
-            one[j, pl.ds(LEAD + second, cut - second)] = strip[
-                pl.ds(i * cut + second, cut - second), lanes
+            one[j, pl.ds(LEAD + second, end - second)] = following[
+                pl.ds(i * more + second - cut, end - second), lanes
             ]
-            one[j, pl.ds(LEAD + cut, size)] = rest[pl.ds(i * size, size), lanes]
+            one[j, pl.ds(LEAD + end, size)] = rest[pl.ds(i * size, size), lanes]
             one[j, after] = rest[pl.ds(base + area + i * width, width), lanes]
     for r in range(rows):
         part = pl.ds(r * width, width)
@@ -291,7 +328,7 @@
 
     def store(r, at, value):
         if at == LEAD:
-            out[r, pl.ds(cols - high, low)] = value
+            out[r, pl.ds(cols - high, EDGE)] = value
         else:
             out[r, pl.ds(0, cols - high)] = value
 
@@ -301,7 +338,7 @@
         two,
         spread,
         [(LEAD + second, cols - second + 8), (LEAD - 8, first + 8)],
-        [(LEAD + high, cols - high), (LEAD, low)],
+        [(LEAD + high, cols - high), (LEAD, EDGE)],
         store,
     )
 
@@ -357,7 +394,7 @@
 
 
 def grouping(rows):
-    return next(n for n in (4, 2, 1) if rows % n == 0)
+    return next(n for n in (8, 4, 2, 1) if rows % n == 0)
 
 
 def cells_of(ref, b, many, start=0):
@@ -402,10 +439,10 @@
     loop(rows // many, block)
 
 
-def own_gram_kernel(layout, middle, sides, weight, total, left, right, spread):
+def own_gram_kernel(layout, first, second, sides, weight, total, left, right, spread):
     local = total.shape[0]
     total[...] = jnp.zeros_like(total)
-    for pieces, own in zip(layout, (middle, sides)):
+    for pieces, own in zip(layout, (first, second, sides)):
         rows, size, _ = own.shape
         many = grouping(rows)
         depth = many * size
@@ -454,8 +491,9 @@
     upper[at], lower[at] = halves(value - mean)
 
 
-def first_cross_kernel(pieces, own, other, weight, after, upper, lower, centre, total):
-    total[...] = jnp.zeros_like(total)
+def part_cross_kernel(pieces, own, other, weight, after, *refs):
+    before, (upper, lower, centre, total) = refs[:-4], refs[-4:]
+    total[...] = before[0][...] if before else jnp.zeros_like(total)
     rows, size, local = own.shape
     many = grouping(rows)
 
@@ -499,9 +537,10 @@
     loop(rows // many, block)
 
 
-def first_gram_kernel(groups, pieces, own, others, weight, upper, lower, centre, total, tilt):
-    total[...] = jnp.zeros_like(total)
-    tilt[...] = jnp.zeros_like(tilt)
+def part_gram_kernel(groups, pieces, own, others, weight, *refs):
+    before, (upper, lower, centre, total, tilt) = refs[:-5], refs[-5:]
+    total[...] = before[0][...] if before else jnp.zeros_like(total)
+    tilt[...] = before[1][...] if before else jnp.zeros_like(tilt)
     gram_kernel(groups, pieces, own, others, weight, upper, lower, centre, total, tilt)
 
 
@@ -563,8 +602,9 @@
         first, second, own, other, *rest = rest
     else:
         first, second, *rest = rest
-    uppers, lowers, centres = rest[0:2], rest[2:4], rest[4:6]
-    out, whole, chosen, natural = rest[6:]
+    count = len(layout)
+    uppers, lowers, centres = (rest[i * count : (i + 1) * count] for i in range(3))
+    out, whole, chosen, natural = rest[3 * count :]
     rows, _ = centres[0].shape
     local = natural.shape[2]
     members = whole.shape[0]
@@ -618,7 +658,7 @@
                     ]
         for i in range(many):
             r = b * many + i
-            middle_row = centres[0][pl.ds(r, 1)] + centres[1][pl.ds(r, 1)]
+            middle_row = sum(c[pl.ds(r, 1)] for c in centres)
             out[pl.ds(r, local, stride=rows)] = natural[i].T + middle_row
 
     loop(rows // many, block)
@@ -681,13 +721,23 @@
     members = local * groups
     width = STEPS
     lanes = max(local, cols)
-    cut, low, high = parted(cols)
+    cut, end = parted(cols)
     strip = struct(width * cut + 4 * width, lanes)
-    rest = struct(width * (cols - cut) + 2 * width * width + 2 * width, lanes)
+    following = struct(width * (end - cut), lanes)
+    rest = struct(width * (cols - end) + 2 * width * width + 2 * width, lanes)
     edge = struct(rows * width + rows, lanes)
-    field, kept, early, late, left, right = call(
+    field, kept, early, late, early_next, late_next, left, right = call(
         functools.partial(pack_kernel, "domain"),
-        (struct(rows, cols, local), struct(3, rows, cols), strip, strip, edge, edge),
+        (
+            struct(rows, cols, local),
+            struct(3, rows, cols),
+            strip,
+            strip,
+            following,
+            following,
+            edge,
+            edge,
+        ),
         ensemble.reshape(local * rows, cols),
         diffusion,
         drift_rows,
@@ -696,6 +746,8 @@
     )
     early = trade(early, "domain", True)
     late = trade(late, "domain", False)
+    early_next = trade(early_next, "domain", True)
+    late_next = trade(late_next, "domain", False)
     left, right = shift(right, ("role",), 1), shift(left, ("role",), -1)
     weight = call(
         functools.partial(weight_kernel, "role"),
@@ -718,22 +770,36 @@
         pltpu.VMEM((4, rows + 2 * width, cols + 2 * LEAD, local), jnp.float32),
         pltpu.VMEM((5, 2 * width, cols), jnp.float32),
     )
-    middle = call(
-        functools.partial(middle_kernel, "domain"),
-        struct(rows, high - low, local),
+    ends = (EDGE, cut - EDGE, end - EDGE)
+
+    def forecast(after, low, high, pieces, *strips):
+        return call(
+            functools.partial(middle_kernel, "domain", low, high, pieces),
+            struct(rows, high - low, local),
+            after,
+            field,
+            kept,
+            *strips,
+            scratch=scratch,
+        )
+
+    first = forecast(weight, *ends[:2], ((0, cut, 0, 0, cut),), early, late)
+    back = 2 * EDGE
+    pieces = (
+        (0, cut, cut - back, cut - back, back),
+        (1, end - cut, 0, cut, end - cut),
+    )
+    second = forecast(first, *ends[1:], pieces, early, late, early_next, late_next)
+    sides = call(
+        functools.partial(sides_kernel, "domain"),
+        struct(rows, cols - end + 2 * EDGE, local),
+        second,
         field,
         kept,
         early,
         late,
-        scratch=scratch,
-    )
-    sides = call(
-        functools.partial(sides_kernel, "domain"),
-        struct(rows, cols - high + low, local),
-        field,
-        kept,
-        early,
-        late,
+        early_next,
+        late_next,
         left,
         right,
         early_rest,
@@ -745,103 +811,101 @@
         others = [shift(value, ("member",), s) for s in range(1, groups)]
         return jnp.concatenate(others, axis=0) if len(others) > 1 else others[0]
 
-    middle_others = gathered(middle)
-    sides_others = gathered(sides)
+    owns = (first, second, sides)
+    theirs = []
+    for value in owns:
+        theirs.append(gathered(value))
+    tail = cols - end + EDGE
     layout = (
-        ((0, low, high - low),),
-        ((0, high, cols - high), (cols - high, 0, low)),
-    )
-
-    def deviations(columns):
-        one = struct(rows * columns, members, kind=jnp.bfloat16)
+        ((0, ends[0], ends[1] - ends[0]),),
+        ((0, ends[1], ends[2] - ends[1]),),
+        ((0, ends[2], tail), (tail, 0, EDGE)),
+    )
+
+    def deviations(value):
+        one = struct(rows * value.shape[1], members, kind=jnp.bfloat16)
         return one, one, struct(rows, cols)
 
+    made = []
     pair = groups == 2 and local % 128 == 0
     if pair:
-        sided = rows * (cols - high + low)
+        sided = rows * sides.shape[1]
         half = struct(local, sided, kind=jnp.bfloat16)
         alone, left_half, right_half, spread = call(
             functools.partial(own_gram_kernel, layout),
             (struct(local, local), half, half, struct(sided, local)),
-            middle,
-            sides,
+            *owns,
             weight,
         )
         stages = role_sums(alone)
         started = sum(stages[0])
         cross = struct(local + 8, local)
-        upper_a, lower_a, centre_a, total = call(
-            functools.partial(first_cross_kernel, layout[0]),
-            (*deviations(high - low), cross),
-            middle,
-            middle_others,
-            weight,
-            started,
-        )
+        total = ()
+        for i in range(2):
+            *three, total = call(
+                functools.partial(part_cross_kernel, layout[i]),
+                (*deviations(owns[i]), cross),
+                owns[i],
+                theirs[i],
+                weight,
+                started,
+                *total,
+            )
+            made.append(three)
+            total = (total,)
         alone, arriving = stages[-1]
-        total, alone = lax.optimization_barrier((total, alone))
+        total, alone = lax.optimization_barrier((total[0], alone))
         alone = alone + arriving
         gram = call(
-            last_cross_kernel,
-            cross,
-            sides,
-            sides_others,
-            left_half,
-            right_half,
-            spread,
-            total,
-            alone,
+            last_cross_kernel, cross, sides, theirs[-1], left_half, right_half, spread, total, alone
         )
         gram, alone = lax.optimization_barrier((gram, alone))
         facing = shift(alone, ("member",), 1)
         grams = (*role_sums(gram)[-1], alone, facing)
-        upper_b, lower_b, centre_b = call(
-            functools.partial(deviation_kernel, layout[1]),
-            deviations(cols - high + low),
+        three = call(
+            functools.partial(deviation_kernel, layout[-1]),
+            deviations(sides),
             sides,
-            sides_others,
+            theirs[-1],
             gram,
         )
+        made.append(three)
     else:
         blocks = members // 128
         size = blocks * (blocks + 1) // 2 * 128 + 8
-        square = struct(members, members)
-        vector = struct(1, members)
-        upper_a, lower_a, centre_a, total, tilt = call(
-            functools.partial(first_gram_kernel, groups, layout[0]),
-            (*deviations(high - low), square, vector),
-            middle,
-            middle_others,
+        sums = struct(members, members), struct(1, members)
+        totals = ()
+        for i in range(2):
+            *three, total, tilt = call(
+                functools.partial(part_gram_kernel, groups, layout[i]),
+                (*deviations(owns[i]), *sums),
+                owns[i],
+                theirs[i],
+                weight,
+                *totals,
+            )
+            made.append(three)
+            totals = total, tilt
+        gram, *three = call(
+            functools.partial(last_gram_kernel, groups, layout[-1]),
+            (struct(size, 128), *deviations(sides)),
+            sides,
+            theirs[-1],
             weight,
+            *totals,
+            scratch=tuple(pltpu.VMEM(v.shape, v.dtype) for v in sums),
         )
-        gram, upper_b, lower_b, centre_b = call(
-            functools.partial(last_gram_kernel, groups, layout[1]),
-            (struct(size, 128), *deviations(cols - high + low)),
-            sides,
-            sides_others,
-            weight,
-            total,
-            tilt,
-            scratch=(
-                pltpu.VMEM((members, members), jnp.float32),
-                pltpu.VMEM((1, members), jnp.float32),
-            ),
-        )
+        made.append(three)
         grams = role_sums(gram)[-1]
     return call(
         functools.partial(analysis_kernel, layout, pair),
         struct(local * rows, cols),
         *grams,
-        upper_a,
-        upper_b,
-        lower_a,
-        lower_b,
-        centre_a,
-        centre_b,
+        *(three[k] for k in range(3) for three in made),
         scratch=(
             pltpu.VMEM((members, members), jnp.float32),
             pltpu.VMEM((members, 2 * local), jnp.bfloat16),
-            pltpu.VMEM((4, cols, local), jnp.float32),
+            pltpu.VMEM((grouping(rows), cols, local), jnp.float32),
         ),
         result=True,
     ).reshape(local, rows, cols)

time: 43.1 us -> 47 us (1.090)
  starting transfers between devices: 17.3 us -> 20.1 us
  waiting for transfers between devices: 11.4 us -> 12.1 us
    ppermute x5 -> x6, waiting for transfers between devices: 3.08 us -> 7.42 us  [shift(): return lax.ppermute(value, axes if len(axes) > 1 else axes[0], pairs)]
    ppermute x4 -> x6, waiting for transfers between devices: 4.59 us -> 2.24 us  [trade(): return lax.ppermute(value, axis, pairs + [(j, i) for i, j in pairs])]
    ppermute x4 -> x6, starting transfers between devices: 7.32 us -> 9.33 us  [trade(): return lax.ppermute(value, axis, pairs + [(j, i) for i, j in pairs])]
    ppermute x4, waiting for transfers between devices: 3.7 us -> 2.49 us  [role_sums(): other = lax.ppermute(value, 'role', [(i, i ^ step) for i in range(size)])]
    ppermute x5 -> x6, starting transfers between devices: 6.43 us -> 6.95 us  [shift(): return lax.ppermute(value, axes if len(axes) > 1 else axes[0], pairs)]
    pallas_call x10 -> x12, Pallas kernels: 13.4 us -> 13.8 us  [call(): pl.pallas_call(body, out_shape=outs, in_specs=[SMEM] * scalars + [VMEM] *...]
  transfers between devices with their start and end apart: 13 -> 16, of which waited for: 7 -> 6; matrix products, arithmetic and copies ran while one was open for 0% -> 0% of each run, Pallas kernels for 14% -> 14%
where the time goes in v1:
time: 47 us; the launch traced here: 46.9 us
  starting transfers between devices  20.1 us (43%)
  Pallas kernels  13.8 us (29%)
  waiting for transfers between devices  12.1 us (26%)
  between operations  0.8 us (2%)
    pallas_call x12, Pallas kernels, call(): pl.pallas_call(body, out_shape=outs, in_specs=[SMEM] * scalars + [VMEM] *...  13.8 us
    ppermute x6, starting transfers between devices, trade(): return lax.ppermute(value, axis, pairs + [(j, i) for i, j in pairs])  9.33 us
    ppermute x6, waiting for transfers between devices, shift(): return lax.ppermute(value, axes if len(axes) > 1 else axes[0], pairs)  7.42 us
    ppermute x6, starting transfers between devices, shift(): return lax.ppermute(value, axes if len(axes) > 1 else axes[0], pairs)  6.95 us
    ppermute x4, starting transfers between devices, role_sums(): other = lax.ppermute(value, 'role', [(i, i ^ step) for i in range(size)])  3.85 us
    ppermute x4, waiting for transfers between devices, role_sums(): other = lax.ppermute(value, 'role', [(i, i ^ step) for i in range(size)])  2.49 us
    ppermute x6, waiting for transfers between devices, trade(): return lax.ppermute(value, axis, pairs + [(j, i) for i, j in pairs])  2.24 us
  transfers between devices with their start and end apart: 16, of which 6 were waited for; matrix products, arithmetic and copies ran while one was open for 0% of the time, Pallas kernels for 14%

profile of v1, /device:TPU:0, one launch (start us, length us, event | category | flops | bytes accessed | tf_op | source)
XLA Modules:
  0.0 46.9 jit_solution(11529039520692512715)
XLA Ops:
  0.0 1.3 %shard_map.83 = (f32[8,128,128]{2,1,0:T(8,128)S(1)}, f32[3,8,128]{2,1,0:T(8,128)S(1)}, f32[208,128]{1,0:T(8,128)S(1)}, f32[208,128]{1,0:T(8,128)S(1)}, f32[192,1...) custom-call(f32[1024,128]{1,0:T(8,128)} %bitcast.4, ...), custom_call_target="tpu_custom_call" | custom-call | tf_op jit(solution)/shard_map/pallas_call | solution.py:43
  1.4 5.1 %collective-permute-start = (f32[208,128]{1,0:T(8,128)S(1)}, f32[208,128]{1,0:T(8,128)S(1)}, u32[]{:S(2)}, u32[]{:S(2)}) collective-permute-start(f32[208,128]{1,0:T(8,128)S(1)} %get-tuple-element.36), channel_id=1, source_target_pairs={{4,8},{12,0},{8,4},{0,12},{5,9},{13,1},{9,5},{1,13},{6,10},{14,2},... | collective-permute-start | bytes 319496 | tf_op jit(solution)/shard_map/ppermute | solution.py:692
  6.5 0.0 collective-permute-start.4
  6.5 0.0 collective-permute-start.1
  6.5 1.7 %collective-permute-start.5 = (f32[40,128]{1,0:T(8,128)S(1)}, f32[40,128]{1,0:T(8,128)S(1)}, u32[]{:S(2)}, u32[]{:S(2)}) collective-permute-start(f32[40,128]{1,0:T(8,128)S(1)} %get-tuple-element.41), channel_id=1, source_target_pairs={{0,3},{1,0},{2,1},{3,2},{4,7},{5,4},{6,5},{7,6},{8,11},{9,8},{10,9... | collective-permute-start | bytes 61448 | tf_op jit(solution)/shard_map/ppermute | solution.py:683
  8.3 0.6 %collective-permute-start.2 = (f32[192,128]{1,0:T(8,128)S(1)}, f32[192,128]{1,0:T(8,128)S(1)}, u32[]{:S(2)}, u32[]{:S(2)}) collective-permute-start(f32[192,128]{1,0:T(8,128)S(1)} %get-tuple-element.38), channel_id=1, source_target_pairs={{4,8},{12,0},{8,4},{0,12},{5,9},{13,1},{9,5},{1,13},{6,10},{14,2},... | collective-permute-start | bytes 294920 | tf_op jit(solution)/shard_map/ppermute | solution.py:692
  8.9 0.8 %collective-permute-done.4.left = f32[40,128]{1,0:T(8,128)S(1)} collective-permute-done((f32[40,128]{1,0:T(8,128)S(1)}, f32[40,128]{1,0:T(8,128)S(1)}, u32[]{:S(2)}, u32[]{:S(2)}) %collective-permute-start.4) | collective-permute-done | bytes 20512 | tf_op jit(solution)/shard_map/ppermute | solution.py:683
  9.7 0.3 collective-permute-start.3
  10.7 1.1 %shard_map.82.after.weight = f32[128,16]{1,0:T(8,128)S(1)} custom-call(s32[1,1]{1,0:T(1,128)} %bitcast.3.count, s32[1,1024]{1,0:T(1,128)} %cells.1, f32[1,1024]{1,0:T(1,128)} %values.1, f32[1,1024]{1,0:T(1,128)} %weights.1), custom_call_target="tpu_custom_call" | custom-call | tf_op jit(solution)/shard_map/pallas_call | solution.py:43
  11.8 0.0 collective-permute-done.5.right
  11.9 3.0 %collective-permute-start.6 = (f32[168,128]{1,0:T(8,128)S(1)}, f32[168,128]{1,0:T(8,128)S(1)}, u32[]{:S(2)}, u32[]{:S(2)}) collective-permute-start(f32[168,128]{1,0:T(8,128)S(1)} %get-tuple-element.42), channel_id=1, source_target_pairs={{4,8},{12,0},{8,4},{0,12},{5,9},{13,1},{9,5},{1,13},{6,10},{14,2},... | collective-permute-start | bytes 258056 | tf_op jit(solution)/shard_map/ppermute | solution.py:692
  14.8 0.0 collective-permute-done.refs_0_.early
  14.8 0.3 collective-permute-start.7
  15.1 0.0 collective-permute-done.1.refs_1_.late
  15.1 0.7 %shard_map.84.after.first.own = f32[8,32,128]{2,1,0:T(8,128)S(1)} custom-call(f32[128,16]{1,0:T(8,128)S(1)} %shard_map.82.after.weight, f32[8,128,128]{2,1,0:T(8,128)S(1)} %get-tuple-element.34.field, f32[3,8,128]{2,1,0:T(8,128)S(1)} %get-tuple-element.35.kept, f32[208,128]{1,0:T(8,128)S(1)} %collective-permute-done.refs_0_.early, ...), custom_call_target="tpu_custom_call" | custom-call | tf_op jit(solution)/shard_map/pallas_call | solution.py:43
  15.8 0.0 collective-permute-done.2.refs_2_.early_next
  15.8 2.2 %collective-permute-done.3.refs_3_.late_next = f32[192,128]{1,0:T(8,128)S(1)} collective-permute-done((f32[192,128]{1,0:T(8,128)S(1)}, f32[192,128]{1,0:T(8,128)S(1)}, u32[]{:S(2)}, u32[]{:S(2)}) %collective-permute-start.3) | collective-permute-done | bytes 98336 | tf_op jit(solution)/shard_map/ppermute | solution.py:692
  18.0 0.9 %shard_map.85.after.second.own = f32[8,48,128]{2,1,0:T(8,128)S(1)} custom-call(f32[8,32,128]{2,1,0:T(8,128)S(1)} %shard_map.84.after.first.own, f32[8,128,128]{2,1,0:T(8,128)S(1)} %get-tuple-element.34.field, f32[3,8,128]{2,1,0:T(8,128)S(1)} %get-tuple-element.35.kept, f32[208,128]{1,0:T(8,128)S(1)} %collective-permute-done.refs_0_.early, ...), custom_call_target="tpu_custom_call" | custom-call | tf_op jit(solution)/shard_map/pallas_call | solution.py:43
  18.9 1.6 %collective-permute-start.9 = (f32[8,48,128]{2,1,0:T(8,128)S(1)}, f32[8,48,128]{2,1,0:T(8,128)S(1)}, u32[]{:S(2)}, u32[]{:S(2)}) collective-permute-start(f32[8,48,128]{2,1,0:T(8,128)S(1)} %shard_map.85.after.second.own), channel_id=1, source_target_pairs={{0,16},{16,0},{1,17},{17,1},{2,18},{18,2},{3,19},{19,3},{4,20},{20... | collective-permute-start | bytes 589832 | tf_op jit(solution)/shard_map/ppermute | solution.py:683
  20.5 0.0 collective-permute-done.6.early_rest
  20.5 0.0 collective-permute-done.7.late_rest
  20.5 1.1 %shard_map.87.sides.own = f32[8,48,128]{2,1,0:T(8,128)S(1)} custom-call(f32[8,48,128]{2,1,0:T(8,128)S(1)} %shard_map.85.after.second.own, f32[8,128,128]{2,1,0:T(8,128)S(1)} %get-tuple-element.34.field, f32[3,8,128]{2,1,0:T(8,128)S(1)} %get-tuple-element.35.kept, f32[208,128]{1,0:T(8,128)S(1)} %collective-permute-done.refs_0_.early, ...), custom_call_target="tpu_custom_call" | custom-call | tf_op jit(solution)/shard_map/pallas_call | solution.py:43
  21.6 1.3 %collective-permute-start.8 = (f32[8,48,128]{2,1,0:T(8,128)S(1)}, f32[8,48,128]{2,1,0:T(8,128)S(1)}, u32[]{:S(2)}, u32[]{:S(2)}) collective-permute-start(f32[8,48,128]{2,1,0:T(8,128)S(1)} %shard_map.87.sides.own), channel_id=1, source_target_pairs={{0,16},{16,0},{1,17},{17,1},{2,18},{18,2},{3,19},{19,3},{4,20},{20... | collective-permute-start | bytes 589832 | tf_op jit(solution)/shard_map/ppermute | solution.py:683
  23.0 0.8 %collective-permute-start.11 = (f32[8,32,128]{2,1,0:T(8,128)S(1)}, f32[8,32,128]{2,1,0:T(8,128)S(1)}, u32[]{:S(2)}, u32[]{:S(2)}) collective-permute-start(f32[8,32,128]{2,1,0:T(8,128)S(1)} %shard_map.84.after.first.own), channel_id=1, source_target_pairs={{0,16},{16,0},{1,17},{17,1},{2,18},{18,2},{3,19},{19,3},{4,20},{20... | collective-permute-start | bytes 393224 | tf_op jit(solution)/shard_map/ppermute | solution.py:683
  23.7 1.0 %shard_map.88 = (f32[128,128]{1,0:T(8,128)S(1)}, bf16[128,384]{1,0:T(8,128)(2,1)S(1)}, bf16[128,384]{1,0:T(8,128)(2,1)S(1)}, f32[384,128]{1,0:T(8,128)S(1)}) custom-call(f32[8,32,128]{2,1,0:T(8,128)S(1)} %shard_map.84.after.first.own, f32[8,48,128]{2,1,0:T(8,128)S(1)} %shard_map.85.after.second.own, f32[8,48,128]{2,1,0:T(8,128)S(1)} %shard_map.87.sides.own, ...), custom_call_target="tpu_custom_call" | custom-call | tf_op jit(solution)/shard_map/pallas_call | solution.py:43
  24.8 0.1 collective-permute-start.10
  24.9 1.2 %collective-permute-done.10 = f32[128,128]{1,0:T(8,128)S(1)} collective-permute-done((f32[128,128]{1,0:T(8,128)S(1)}, f32[128,128]{1,0:T(8,128)S(1)}, u32[]{:S(2)}, u32[]{:S(2)}) %collective-permute-start.10) | collective-permute-done | bytes 65568 | tf_op jit(solution)/shard_map/ppermute | solution.py:702
  26.1 1.6 %collective-permute-start.12 = (f32[128,128]{1,0:T(8,128)S(1)}, f32[128,128]{1,0:T(8,128)S(1)}, u32[]{:S(2)}, u32[]{:S(2)}) collective-permute-start(f32[128,128]{1,0:T(8,128)S(1)} %add.10.after), channel_id=1, source_target_pairs={{0,2},{1,3},{2,0},{3,1},{4,6},{5,7},{6,4},{7,5},{8,10},{9,11},{10,... | collective-permute-start | bytes 196616 | tf_op jit(solution)/shard_map/ppermute | solution.py:702
  27.7 4.0 %collective-permute-done.11.other = f32[8,32,128]{2,1,0:T(8,128)S(1)} collective-permute-done((f32[8,32,128]{2,1,0:T(8,128)S(1)}, f32[8,32,128]{2,1,0:T(8,128)S(1)}, u32[]{:S(2)}, u32[]{:S(2)}) %collective-permute-start.11) | collective-permute-done | bytes 131104 | tf_op jit(solution)/shard_map/ppermute | solution.py:683
  31.7 0.6 %shard_map.89 = (bf16[256,256]{1,0:T(8,128)(2,1)S(1)}, bf16[256,256]{1,0:T(8,128)(2,1)S(1)}, f32[8,128]{1,0:T(8,128)S(1)}, f32[136,128]{1,0:T(8,128)S(1)}) custom-call(f32[8,32,128]{2,1,0:T(8,128)S(1)} %shard_map.84.after.first.own, f32[8,32,128]{2,1,0:T(8,128)S(1)} %collective-permute-done.11.other, f32[128,16]{1,0:T(8,128)S(1)} %shard_map.82.after.weight, ...), custom_call_target="tpu_custom_call" | custom-call | tf_op jit(solution)/shard_map/pallas_call | solution.py:43
  32.3 0.0 collective-permute-done.9.other
  32.3 0.9 %shard_map.90 = (bf16[384,256]{1,0:T(8,128)(2,1)S(1)}, bf16[384,256]{1,0:T(8,128)(2,1)S(1)}, f32[8,128]{1,0:T(8,128)S(1)}, f32[136,128]{1,0:T(8,128)S(1)}) custom-call(f32[8,48,128]{2,1,0:T(8,128)S(1)} %shard_map.85.after.second.own, f32[8,48,128]{2,1,0:T(8,128)S(1)} %collective-permute-done.9.other, f32[128,16]{1,0:T(8,128)S(1)} %shard_map.82.after.weight, ...), custom_call_target="tpu_custom_call" | custom-call | tf_op jit(solution)/shard_map/pallas_call | solution.py:43
  33.2 0.0 collective-permute-done.12
  33.2 0.0 collective-permute-done.8.other
  33.2 0.6 %shard_map.91.after = f32[136,128]{1,0:T(8,128)S(1)} custom-call(f32[8,48,128]{2,1,0:T(8,128)S(1)} %shard_map.87.sides.own, f32[8,48,128]{2,1,0:T(8,128)S(1)} %collective-permute-done.8.other, bf16[128,384]{1,0:T(8,128)(2,1)S(1)} %get-tuple-element.44.left, bf16[128,384]{1,0:T(8,128)(2,1)S(1)} %get-tuple-element.45.right, ...), custom_call_target="tpu_custom_call" | custom-call | tf_op jit(solution)/shard_map/pallas_call | solution.py:43
  33.8 0.1 collective-permute-start.13
  33.9 1.2 %collective-permute-done.13 = f32[136,128]{1,0:T(8,128)S(1)} collective-permute-done((f32[136,128]{1,0:T(8,128)S(1)}, f32[136,128]{1,0:T(8,128)S(1)}, u32[]{:S(2)}, u32[]{:S(2)}) %collective-permute-start.13) | collective-permute-done | bytes 69664 | tf_op jit(solution)/shard_map/ppermute | solution.py:702
  35.2 2.2 %collective-permute-start.14 = (f32[136,128]{1,0:T(8,128)S(1)}, f32[136,128]{1,0:T(8,128)S(1)}, u32[]{:S(2)}, u32[]{:S(2)}) collective-permute-start(f32[136,128]{1,0:T(8,128)S(1)} %add.12.rest_0_), channel_id=1, source_target_pairs={{0,2},{1,3},{2,0},{3,1},{4,6},{5,7},{6,4},{7,5},{8,10},{9,11},{10,... | collective-permute-start | bytes 208904 | tf_op jit(solution)/shard_map/ppermute | solution.py:702
  37.3 1.5 %collective-permute-start.15 = (f32[128,128]{1,0:T(8,128)S(1)}, f32[128,128]{1,0:T(8,128)S(1)}, u32[]{:S(2)}, u32[]{:S(2)}) collective-permute-start(f32[128,128]{1,0:T(8,128)S(1)} %add.11.after.rest_2_), channel_id=1, source_target_pairs={{0,16},{16,0},{1,17},{17,1},{2,18},{18,2},{3,19},{19,3},{4,20},{20... | collective-permute-start | bytes 196616 | tf_op jit(solution)/shard_map/ppermute | solution.py:683
  38.8 0.2 shard_map.92
  39.0 2.6 %collective-permute-done.15.rest_3_ = f32[128,128]{1,0:T(8,128)S(1)} collective-permute-done((f32[128,128]{1,0:T(8,128)S(1)}, f32[128,128]{1,0:T(8,128)S(1)}, u32[]{:S(2)}, u32[]{:S(2)}) %collective-permute-start.15) | collective-permute-done | bytes 65568 | tf_op jit(solution)/shard_map/ppermute | solution.py:683
  41.6 0.0 collective-permute-done.14.rest_1_
  41.6 5.3 %shard_map.93 = f32[1024,128]{1,0:T(8,128)} custom-call(f32[136,128]{1,0:T(8,128)S(1)} %add.12.rest_0_, f32[136,128]{1,0:T(8,128)S(1)} %collective-permute-done.14.rest_1_, f32[128,128]{1,0:T(8,128)S(1)} %add.11.after.rest_2_, f32[128,128]{1,0:T(8,128)S(1)} %collective-permute-done.15.rest_3_, bf16[256,256]{1,0:T(8,128)(2,1)S(1)} %get-tuple-element.54.rest_4_, ...), custom_call_target="tpu_custom_call" | custom-call | tf_op jit(solution)/shard_map/pallas_call | solution.py:43
  (4 shorter events, 0.1 us)
Async XLA Ops:
  1.4 13.5 %collective-permute-start = (f32[208,128]{1,0:T(8,128)S(1)}, f32[208,128]{1,0:T(8,128)S(1)}, u32[]{:S(2)}, u32[]{:S(2)}) collective-permute-start(f32[208,128]{1,0:T(8,128)S(1)} %get-tuple-element.36), channel_id=1, source_target_pairs={{4,8},{12,0},{8,4},{0,12},{5,9},{13,1},{9,5},{1,13},{6,10},{14,2},... | collective-permute-start | bytes 319496 | tf_op jit(solution)/shard_map/ppermute | solution.py:692
  6.5 3.2 %collective-permute-start.4 = (f32[40,128]{1,0:T(8,128)S(1)}, f32[40,128]{1,0:T(8,128)S(1)}, u32[]{:S(2)}, u32[]{:S(2)}) collective-permute-start(f32[40,128]{1,0:T(8,128)S(1)} %get-tuple-element.40), channel_id=1, source_target_pairs={{0,1},{1,2},{2,3},{3,0},{4,5},{5,6},{6,7},{7,4},{8,9},{9,10},{10,1... | collective-permute-start | bytes 61448 | tf_op jit(solution)/shard_map/ppermute | solution.py:683
  6.5 8.6 %collective-permute-start.1 = (f32[208,128]{1,0:T(8,128)S(1)}, f32[208,128]{1,0:T(8,128)S(1)}, u32[]{:S(2)}, u32[]{:S(2)}) collective-permute-start(f32[208,128]{1,0:T(8,128)S(1)} %get-tuple-element.37), channel_id=1, source_target_pairs={{0,4},{8,12},{4,0},{12,8},{1,5},{9,13},{5,1},{13,9},{2,6},{10,14},... | collective-permute-start | bytes 319496 | tf_op jit(solution)/shard_map/ppermute | solution.py:692
  6.5 5.3 %collective-permute-start.5 = (f32[40,128]{1,0:T(8,128)S(1)}, f32[40,128]{1,0:T(8,128)S(1)}, u32[]{:S(2)}, u32[]{:S(2)}) collective-permute-start(f32[40,128]{1,0:T(8,128)S(1)} %get-tuple-element.41), channel_id=1, source_target_pairs={{0,3},{1,0},{2,1},{3,2},{4,7},{5,4},{6,5},{7,6},{8,11},{9,8},{10,9... | collective-permute-start | bytes 61448 | tf_op jit(solution)/shard_map/ppermute | solution.py:683
  8.3 7.6 %collective-permute-start.2 = (f32[192,128]{1,0:T(8,128)S(1)}, f32[192,128]{1,0:T(8,128)S(1)}, u32[]{:S(2)}, u32[]{:S(2)}) collective-permute-start(f32[192,128]{1,0:T(8,128)S(1)} %get-tuple-element.38), channel_id=1, source_target_pairs={{4,8},{12,0},{8,4},{0,12},{5,9},{13,1},{9,5},{1,13},{6,10},{14,2},... | collective-permute-start | bytes 294920 | tf_op jit(solution)/shard_map/ppermute | solution.py:692
  9.7 8.3 %collective-permute-start.3 = (f32[192,128]{1,0:T(8,128)S(1)}, f32[192,128]{1,0:T(8,128)S(1)}, u32[]{:S(2)}, u32[]{:S(2)}) collective-permute-start(f32[192,128]{1,0:T(8,128)S(1)} %get-tuple-element.39), channel_id=1, source_target_pairs={{0,4},{8,12},{4,0},{12,8},{1,5},{9,13},{5,1},{13,9},{2,6},{10,14},... | collective-permute-start | bytes 294920 | tf_op jit(solution)/shard_map/ppermute | solution.py:692
  11.9 8.7 %collective-permute-start.6 = (f32[168,128]{1,0:T(8,128)S(1)}, f32[168,128]{1,0:T(8,128)S(1)}, u32[]{:S(2)}, u32[]{:S(2)}) collective-permute-start(f32[168,128]{1,0:T(8,128)S(1)} %get-tuple-element.42), channel_id=1, source_target_pairs={{4,8},{12,0},{8,4},{0,12},{5,9},{13,1},{9,5},{1,13},{6,10},{14,2},... | collective-permute-start | bytes 258056 | tf_op jit(solution)/shard_map/ppermute | solution.py:692
  14.8 5.7 %collective-permute-start.7 = (f32[168,128]{1,0:T(8,128)S(1)}, f32[168,128]{1,0:T(8,128)S(1)}, u32[]{:S(2)}, u32[]{:S(2)}) collective-permute-start(f32[168,128]{1,0:T(8,128)S(1)} %get-tuple-element.43), channel_id=1, source_target_pairs={{0,4},{8,12},{4,0},{12,8},{1,5},{9,13},{5,1},{13,9},{2,6},{10,14},... | collective-permute-start | bytes 258056 | tf_op jit(solution)/shard_map/ppermute | solution.py:692
  18.9 13.4 %collective-permute-start.9 = (f32[8,48,128]{2,1,0:T(8,128)S(1)}, f32[8,48,128]{2,1,0:T(8,128)S(1)}, u32[]{:S(2)}, u32[]{:S(2)}) collective-permute-start(f32[8,48,128]{2,1,0:T(8,128)S(1)} %shard_map.85.after.second.own), channel_id=1, source_target_pairs={{0,16},{16,0},{1,17},{17,1},{2,18},{18,2},{3,19},{19,3},{4,20},{20... | collective-permute-start | bytes 589832 | tf_op jit(solution)/shard_map/ppermute | solution.py:683
  21.6 11.6 %collective-permute-start.8 = (f32[8,48,128]{2,1,0:T(8,128)S(1)}, f32[8,48,128]{2,1,0:T(8,128)S(1)}, u32[]{:S(2)}, u32[]{:S(2)}) collective-permute-start(f32[8,48,128]{2,1,0:T(8,128)S(1)} %shard_map.87.sides.own), channel_id=1, source_target_pairs={{0,16},{16,0},{1,17},{17,1},{2,18},{18,2},{3,19},{19,3},{4,20},{20... | collective-permute-start | bytes 589832 | tf_op jit(solution)/shard_map/ppermute | solution.py:683
  23.0 8.7 %collective-permute-start.11 = (f32[8,32,128]{2,1,0:T(8,128)S(1)}, f32[8,32,128]{2,1,0:T(8,128)S(1)}, u32[]{:S(2)}, u32[]{:S(2)}) collective-permute-start(f32[8,32,128]{2,1,0:T(8,128)S(1)} %shard_map.84.after.first.own), channel_id=1, source_target_pairs={{0,16},{16,0},{1,17},{17,1},{2,18},{18,2},{3,19},{19,3},{4,20},{20... | collective-permute-start | bytes 393224 | tf_op jit(solution)/shard_map/ppermute | solution.py:683
  24.8 1.3 %collective-permute-start.10 = (f32[128,128]{1,0:T(8,128)S(1)}, f32[128,128]{1,0:T(8,128)S(1)}, u32[]{:S(2)}, u32[]{:S(2)}) collective-permute-start(f32[128,128]{1,0:T(8,128)S(1)} %get-tuple-element.47), channel_id=1, source_target_pairs={{0,1},{1,0},{2,3},{3,2},{4,5},{5,4},{6,7},{7,6},{8,9},{9,8},{10,11... | collective-permute-start | bytes 196616 | tf_op jit(solution)/shard_map/ppermute | solution.py:702
  26.1 7.1 %collective-permute-start.12 = (f32[128,128]{1,0:T(8,128)S(1)}, f32[128,128]{1,0:T(8,128)S(1)}, u32[]{:S(2)}, u32[]{:S(2)}) collective-permute-start(f32[128,128]{1,0:T(8,128)S(1)} %add.10.after), channel_id=1, source_target_pairs={{0,2},{1,3},{2,0},{3,1},{4,6},{5,7},{6,4},{7,5},{8,10},{9,11},{10,... | collective-permute-start | bytes 196616 | tf_op jit(solution)/shard_map/ppermute | solution.py:702
  33.8 1.3 %collective-permute-start.13 = (f32[136,128]{1,0:T(8,128)S(1)}, f32[136,128]{1,0:T(8,128)S(1)}, u32[]{:S(2)}, u32[]{:S(2)}) collective-permute-start(f32[136,128]{1,0:T(8,128)S(1)} %shard_map.91.after), channel_id=1, source_target_pairs={{0,1},{1,0},{2,3},{3,2},{4,5},{5,4},{6,7},{7,6},{8,9},{9,8},{10,11... | collective-permute-start | bytes 208904 | tf_op jit(solution)/shard_map/ppermute | solution.py:702
  35.2 6.4 %collective-permute-start.14 = (f32[136,128]{1,0:T(8,128)S(1)}, f32[136,128]{1,0:T(8,128)S(1)}, u32[]{:S(2)}, u32[]{:S(2)}) collective-permute-start(f32[136,128]{1,0:T(8,128)S(1)} %add.12.rest_0_), channel_id=1, source_target_pairs={{0,2},{1,3},{2,0},{3,1},{4,6},{5,7},{6,4},{7,5},{8,10},{9,11},{10,... | collective-permute-start | bytes 208904 | tf_op jit(solution)/shard_map/ppermute | solution.py:702
  37.3 4.3 %collective-permute-start.15 = (f32[128,128]{1,0:T(8,128)S(1)}, f32[128,128]{1,0:T(8,128)S(1)}, u32[]{:S(2)}, u32[]{:S(2)}) collective-permute-start(f32[128,128]{1,0:T(8,128)S(1)} %add.11.after.rest_2_), channel_id=1, source_target_pairs={{0,16},{16,0},{1,17},{17,1},{2,18},{18,2},{3,19},{19,3},{4,20},{20... | collective-permute-start | bytes 196616 | tf_op jit(solution)/shard_map/ppermute | solution.py:683

commit v2 on v1

--- a/solution.py
+++ b/solution.py
@@ -355,7 +355,7 @@
         row_of = lax.shift_right_logical(cell, full.bit_length() - 1)
     col_of = cell - row_of * full - lax.axis_index(axis) * cols
     slot = lax.broadcasted_iota(jnp.int32, (1, slots), 1)
-    plain = jnp.where(slot < count[...], weights[...], 0.0)
+    plain = jnp.where(slot < count[0], weights[...], 0.0)
     valued = plain * values[...]
     here = lax.broadcasted_iota(jnp.int32, (cols, slots), 0) == col_of
     here = jnp.where(here, 1.0, 0.0).astype(jnp.bfloat16)
@@ -509,7 +509,7 @@
     loop(rows // many, block)
 
 
-def last_cross_kernel(own, other, left, right, spread, before, after, total):
+def last_cross_kernel(own, other, left, right, spread, before, total):
     total[...] = before[...]
     rows, size, local = own.shape
     many = grouping(rows)
@@ -748,15 +748,17 @@
     late = trade(late, "domain", False)
     early_next = trade(early_next, "domain", True)
     late_next = trade(late_next, "domain", False)
-    left, right = shift(right, ("role",), 1), shift(left, ("role",), -1)
+    received = shift(right, ("role",), 1)
+    right = shift(left, ("role",), -1)
+    left = received
     weight = call(
         functools.partial(weight_kernel, "role"),
         struct(cols, 2 * rows),
-        observed_count.reshape(1, 1),
+        observed_count,
         observed_cells,
         observed_values,
         observed_weights,
-        raw=4,
+        scalars=1,
     )
     early_rest, late_rest = call(
         functools.partial(turn_kernel, "domain"), (rest, rest), field, left, right, weight
@@ -857,9 +859,8 @@
         total, alone = lax.optimization_barrier((total[0], alone))
         alone = alone + arriving
         gram = call(
-            last_cross_kernel, cross, sides, theirs[-1], left_half, right_half, spread, total, alone
+            last_cross_kernel, cross, sides, theirs[-1], left_half, right_half, spread, total
         )
-        gram, alone = lax.optimization_barrier((gram, alone))
         facing = shift(alone, ("member",), 1)
         grams = (*role_sums(gram)[-1], alone, facing)
         three = call(

time: 47 us -> 48.9 us (1.040)
  waiting for transfers between devices: 12.1 us -> 14.6 us
  Pallas kernels: 13.8 us -> 13 us
    ppermute x6, waiting for transfers between devices: 7.42 us -> 8.98 us  [shift(): return lax.ppermute(value, axes if len(axes) > 1 else axes[0], pairs)]
    pallas_call x12, Pallas kernels: 13.8 us -> 13 us  [call(): pl.pallas_call(body, out_shape=outs, in_specs=[SMEM] * scalars + [VMEM] *...]
    ppermute x6, waiting for transfers between devices: 2.24 us -> 2.97 us  [trade(): return lax.ppermute(value, axis, pairs + [(j, i) for i, j in pairs])]
  transfers between devices with their start and end apart: 16 -> 16, of which waited for: 6 -> 7; matrix products, arithmetic and copies ran while one was open for 0% -> 0% of each run, Pallas kernels for 14% -> 12%
where the time goes in v2:
time: 48.9 us; the launch traced here: 48.7 us
  starting transfers between devices  20.3 us (42%)
  waiting for transfers between devices  14.6 us (30%)
  Pallas kernels  13 us (27%)
  between operations  0.83 us (2%)
    pallas_call x12, Pallas kernels, call(): pl.pallas_call(body, out_shape=outs, in_specs=[SMEM] * scalars + [VMEM] *...  13 us
    ppermute x6, starting transfers between devices, trade(): return lax.ppermute(value, axis, pairs + [(j, i) for i, j in pairs])  9.33 us
    ppermute x6, waiting for transfers between devices, shift(): return lax.ppermute(value, axes if len(axes) > 1 else axes[0], pairs)  8.98 us
    ppermute x6, starting transfers between devices, shift(): return lax.ppermute(value, axes if len(axes) > 1 else axes[0], pairs)  7 us
    ppermute x4, starting transfers between devices, role_sums(): other = lax.ppermute(value, 'role', [(i, i ^ step) for i in range(size)])  3.92 us
    ppermute x6, waiting for transfers between devices, trade(): return lax.ppermute(value, axis, pairs + [(j, i) for i, j in pairs])  2.97 us
    ppermute x4, waiting for transfers between devices, role_sums(): other = lax.ppermute(value, 'role', [(i, i ^ step) for i in range(size)])  2.67 us
  transfers between devices with their start and end apart: 16, of which 7 were waited for; matrix products, arithmetic and copies ran while one was open for 0% of the time, Pallas kernels for 12%

profile of v2, /device:TPU:0, one launch (start us, length us, event | category | flops | bytes accessed | tf_op | source)
XLA Modules:
  0.0 48.7 jit_solution(7932288974013195022)
XLA Ops:
  0.0 1.3 %shard_map.83 = (f32[8,128,128]{2,1,0:T(8,128)S(1)}, f32[3,8,128]{2,1,0:T(8,128)S(1)}, f32[208,128]{1,0:T(8,128)S(1)}, f32[208,128]{1,0:T(8,128)S(1)}, f32[192,1...) custom-call(f32[1024,128]{1,0:T(8,128)} %bitcast.2, ...), custom_call_target="tpu_custom_call" | custom-call | tf_op jit(solution)/shard_map/pallas_call | solution.py:43
  1.4 0.0 copy-start.2
  1.4 5.1 %collective-permute-start = (f32[208,128]{1,0:T(8,128)S(1)}, f32[208,128]{1,0:T(8,128)S(1)}, u32[]{:S(2)}, u32[]{:S(2)}) collective-permute-start(f32[208,128]{1,0:T(8,128)S(1)} %get-tuple-element.34), channel_id=1, source_target_pairs={{4,8},{12,0},{8,4},{0,12},{5,9},{13,1},{9,5},{1,13},{6,10},{14,2},... | collective-permute-start | bytes 319496 | tf_op jit(solution)/shard_map/ppermute | solution.py:692
  6.5 0.0 collective-permute-start.4
  6.5 0.0 copy-start.1
  6.5 0.0 collective-permute-start.1
  6.5 1.7 %collective-permute-start.5 = (f32[40,128]{1,0:T(8,128)S(1)}, f32[40,128]{1,0:T(8,128)S(1)}, u32[]{:S(2)}, u32[]{:S(2)}) collective-permute-start(f32[40,128]{1,0:T(8,128)S(1)} %get-tuple-element.39), channel_id=1, source_target_pairs={{0,3},{1,0},{2,1},{3,2},{4,7},{5,4},{6,5},{7,6},{8,11},{9,8},{10,9... | collective-permute-start | bytes 61448 | tf_op jit(solution)/shard_map/ppermute | solution.py:683
  8.3 0.6 %collective-permute-start.2 = (f32[192,128]{1,0:T(8,128)S(1)}, f32[192,128]{1,0:T(8,128)S(1)}, u32[]{:S(2)}, u32[]{:S(2)}) collective-permute-start(f32[192,128]{1,0:T(8,128)S(1)} %get-tuple-element.36), channel_id=1, source_target_pairs={{4,8},{12,0},{8,4},{0,12},{5,9},{13,1},{9,5},{1,13},{6,10},{14,2},... | collective-permute-start | bytes 294920 | tf_op jit(solution)/shard_map/ppermute | solution.py:692
  8.9 0.8 %collective-permute-done.4.left = f32[40,128]{1,0:T(8,128)S(1)} collective-permute-done((f32[40,128]{1,0:T(8,128)S(1)}, f32[40,128]{1,0:T(8,128)S(1)}, u32[]{:S(2)}, u32[]{:S(2)}) %collective-permute-start.4) | collective-permute-done | bytes 20512 | tf_op jit(solution)/shard_map/ppermute | solution.py:683
  9.7 0.3 collective-permute-start.3
  10.7 0.0 copy-done.2
  10.7 0.0 copy-done.1
  10.7 0.0 copy-done
  10.7 0.4 shard_map.82.after.weight
  11.1 0.0 collective-permute-done.5.right
  11.1 3.0 %collective-permute-start.6 = (f32[168,128]{1,0:T(8,128)S(1)}, f32[168,128]{1,0:T(8,128)S(1)}, u32[]{:S(2)}, u32[]{:S(2)}) collective-permute-start(f32[168,128]{1,0:T(8,128)S(1)} %get-tuple-element.40), channel_id=1, source_target_pairs={{4,8},{12,0},{8,4},{0,12},{5,9},{13,1},{9,5},{1,13},{6,10},{14,2},... | collective-permute-start | bytes 258056 | tf_op jit(solution)/shard_map/ppermute | solution.py:692
  14.1 0.0 collective-permute-done.refs_0_.early
  14.1 0.3 collective-permute-start.7
  14.4 0.0 collective-permute-done.1.refs_1_.late
  14.4 0.7 %shard_map.84.after.first.own = f32[8,32,128]{2,1,0:T(8,128)S(1)} custom-call(f32[128,16]{1,0:T(8,128)S(1)} %shard_map.82.after.weight, f32[8,128,128]{2,1,0:T(8,128)S(1)} %get-tuple-element.32.field, f32[3,8,128]{2,1,0:T(8,128)S(1)} %get-tuple-element.33.kept, f32[208,128]{1,0:T(8,128)S(1)} %collective-permute-done.refs_0_.early, ...), custom_call_target="tpu_custom_call" | custom-call | tf_op jit(solution)/shard_map/pallas_call | solution.py:43
  15.1 0.6 %collective-permute-done.2.refs_2_.early_next = f32[192,128]{1,0:T(8,128)S(1)} collective-permute-done((f32[192,128]{1,0:T(8,128)S(1)}, f32[192,128]{1,0:T(8,128)S(1)}, u32[]{:S(2)}, u32[]{:S(2)}) %collective-permute-start.2) | collective-permute-done | bytes 98336 | tf_op jit(solution)/shard_map/ppermute | solution.py:692
  15.7 2.3 %collective-permute-done.3.refs_3_.late_next = f32[192,128]{1,0:T(8,128)S(1)} collective-permute-done((f32[192,128]{1,0:T(8,128)S(1)}, f32[192,128]{1,0:T(8,128)S(1)}, u32[]{:S(2)}, u32[]{:S(2)}) %collective-permute-start.3) | collective-permute-done | bytes 98336 | tf_op jit(solution)/shard_map/ppermute | solution.py:692
  18.1 0.9 %shard_map.85.after.second.own = f32[8,48,128]{2,1,0:T(8,128)S(1)} custom-call(f32[8,32,128]{2,1,0:T(8,128)S(1)} %shard_map.84.after.first.own, f32[8,128,128]{2,1,0:T(8,128)S(1)} %get-tuple-element.32.field, f32[3,8,128]{2,1,0:T(8,128)S(1)} %get-tuple-element.33.kept, f32[208,128]{1,0:T(8,128)S(1)} %collective-permute-done.refs_0_.early, ...), custom_call_target="tpu_custom_call" | custom-call | tf_op jit(solution)/shard_map/pallas_call | solution.py:43
  18.9 1.6 %collective-permute-start.9 = (f32[8,48,128]{2,1,0:T(8,128)S(1)}, f32[8,48,128]{2,1,0:T(8,128)S(1)}, u32[]{:S(2)}, u32[]{:S(2)}) collective-permute-start(f32[8,48,128]{2,1,0:T(8,128)S(1)} %shard_map.85.after.second.own), channel_id=1, source_target_pairs={{0,16},{16,0},{1,17},{17,1},{2,18},{18,2},{3,19},{19,3},{4,20},{20... | collective-permute-start | bytes 589832 | tf_op jit(solution)/shard_map/ppermute | solution.py:683
  20.5 0.0 collective-permute-done.6.early_rest
  20.5 0.0 collective-permute-done.7.late_rest
  20.5 1.1 %shard_map.87.sides.own = f32[8,48,128]{2,1,0:T(8,128)S(1)} custom-call(f32[8,48,128]{2,1,0:T(8,128)S(1)} %shard_map.85.after.second.own, f32[8,128,128]{2,1,0:T(8,128)S(1)} %get-tuple-element.32.field, f32[3,8,128]{2,1,0:T(8,128)S(1)} %get-tuple-element.33.kept, f32[208,128]{1,0:T(8,128)S(1)} %collective-permute-done.refs_0_.early, ...), custom_call_target="tpu_custom_call" | custom-call | tf_op jit(solution)/shard_map/pallas_call | solution.py:43
  21.7 1.3 %collective-permute-start.8 = (f32[8,48,128]{2,1,0:T(8,128)S(1)}, f32[8,48,128]{2,1,0:T(8,128)S(1)}, u32[]{:S(2)}, u32[]{:S(2)}) collective-permute-start(f32[8,48,128]{2,1,0:T(8,128)S(1)} %shard_map.87.sides.own), channel_id=1, source_target_pairs={{0,16},{16,0},{1,17},{17,1},{2,18},{18,2},{3,19},{19,3},{4,20},{20... | collective-permute-start | bytes 589832 | tf_op jit(solution)/shard_map/ppermute | solution.py:683
  23.0 0.8 %collective-permute-start.11 = (f32[8,32,128]{2,1,0:T(8,128)S(1)}, f32[8,32,128]{2,1,0:T(8,128)S(1)}, u32[]{:S(2)}, u32[]{:S(2)}) collective-permute-start(f32[8,32,128]{2,1,0:T(8,128)S(1)} %shard_map.84.after.first.own), channel_id=1, source_target_pairs={{0,16},{16,0},{1,17},{17,1},{2,18},{18,2},{3,19},{19,3},{4,20},{20... | collective-permute-start | bytes 393224 | tf_op jit(solution)/shard_map/ppermute | solution.py:683
  23.7 1.0 %shard_map.88 = (f32[128,128]{1,0:T(8,128)S(1)}, bf16[128,384]{1,0:T(8,128)(2,1)S(1)}, bf16[128,384]{1,0:T(8,128)(2,1)S(1)}, f32[384,128]{1,0:T(8,128)S(1)}) custom-call(f32[8,32,128]{2,1,0:T(8,128)S(1)} %shard_map.84.after.first.own, f32[8,48,128]{2,1,0:T(8,128)S(1)} %shard_map.85.after.second.own, f32[8,48,128]{2,1,0:T(8,128)S(1)} %shard_map.87.sides.own, ...), custom_call_target="tpu_custom_call" | custom-call | tf_op jit(solution)/shard_map/pallas_call | solution.py:43
  24.8 0.1 collective-permute-start.10
  24.9 1.2 %collective-permute-done.10 = f32[128,128]{1,0:T(8,128)S(1)} collective-permute-done((f32[128,128]{1,0:T(8,128)S(1)}, f32[128,128]{1,0:T(8,128)S(1)}, u32[]{:S(2)}, u32[]{:S(2)}) %collective-permute-start.10) | collective-permute-done | bytes 65568 | tf_op jit(solution)/shard_map/ppermute | solution.py:702
  26.1 5.6 %collective-permute-done.11.other = f32[8,32,128]{2,1,0:T(8,128)S(1)} collective-permute-done((f32[8,32,128]{2,1,0:T(8,128)S(1)}, f32[8,32,128]{2,1,0:T(8,128)S(1)}, u32[]{:S(2)}, u32[]{:S(2)}) %collective-permute-start.11) | collective-permute-done | bytes 131104 | tf_op jit(solution)/shard_map/ppermute | solution.py:683
  31.7 0.6 %shard_map.89 = (bf16[256,256]{1,0:T(8,128)(2,1)S(1)}, bf16[256,256]{1,0:T(8,128)(2,1)S(1)}, f32[8,128]{1,0:T(8,128)S(1)}, f32[136,128]{1,0:T(8,128)S(1)}) custom-call(f32[8,32,128]{2,1,0:T(8,128)S(1)} %shard_map.84.after.first.own, f32[8,32,128]{2,1,0:T(8,128)S(1)} %collective-permute-done.11.other, f32[128,16]{1,0:T(8,128)S(1)} %shard_map.82.after.weight, ...), custom_call_target="tpu_custom_call" | custom-call | tf_op jit(solution)/shard_map/pallas_call | solution.py:43
  32.3 0.0 collective-permute-done.9.other
  32.3 0.9 %shard_map.90 = (bf16[384,256]{1,0:T(8,128)(2,1)S(1)}, bf16[384,256]{1,0:T(8,128)(2,1)S(1)}, f32[8,128]{1,0:T(8,128)S(1)}, f32[136,128]{1,0:T(8,128)S(1)}) custom-call(f32[8,48,128]{2,1,0:T(8,128)S(1)} %shard_map.85.after.second.own, f32[8,48,128]{2,1,0:T(8,128)S(1)} %collective-permute-done.9.other, f32[128,16]{1,0:T(8,128)S(1)} %shard_map.82.after.weight, ...), custom_call_target="tpu_custom_call" | custom-call | tf_op jit(solution)/shard_map/pallas_call | solution.py:43
  33.2 0.0 collective-permute-done.8.other
  33.2 0.6 %shard_map.91.after = f32[136,128]{1,0:T(8,128)S(1)} custom-call(f32[8,48,128]{2,1,0:T(8,128)S(1)} %shard_map.87.sides.own, f32[8,48,128]{2,1,0:T(8,128)S(1)} %collective-permute-done.8.other, bf16[128,384]{1,0:T(8,128)(2,1)S(1)} %get-tuple-element.42.left, bf16[128,384]{1,0:T(8,128)(2,1)S(1)} %get-tuple-element.43.right, ...), custom_call_target="tpu_custom_call" | custom-call | tf_op jit(solution)/shard_map/pallas_call | solution.py:43
  33.8 0.1 collective-permute-start.12
  33.9 2.5 %collective-permute-start.14 = (f32[128,128]{1,0:T(8,128)S(1)}, f32[128,128]{1,0:T(8,128)S(1)}, u32[]{:S(2)}, u32[]{:S(2)}) collective-permute-start(f32[128,128]{1,0:T(8,128)S(1)} %add.10.after), channel_id=1, source_target_pairs={{0,2},{1,3},{2,0},{3,1},{4,6},{5,7},{6,4},{7,5},{8,10},{9,11},{10,... | collective-permute-start | bytes 196616 | tf_op jit(solution)/shard_map/ppermute | solution.py:702
  36.4 0.0 collective-permute-done.12
  36.4 1.2 %collective-permute-start.13 = (f32[136,128]{1,0:T(8,128)S(1)}, f32[136,128]{1,0:T(8,128)S(1)}, u32[]{:S(2)}, u32[]{:S(2)}) collective-permute-start(f32[136,128]{1,0:T(8,128)S(1)} %add.11.rest_0_), channel_id=1, source_target_pairs={{0,2},{1,3},{2,0},{3,1},{4,6},{5,7},{6,4},{7,5},{8,10},{9,11},{10,... | collective-permute-start | bytes 208904 | tf_op jit(solution)/shard_map/ppermute | solution.py:702
  37.7 1.4 %collective-permute-done.14 = f32[128,128]{1,0:T(8,128)S(1)} collective-permute-done((f32[128,128]{1,0:T(8,128)S(1)}, f32[128,128]{1,0:T(8,128)S(1)}, u32[]{:S(2)}, u32[]{:S(2)}) %collective-permute-start.14) | collective-permute-done | bytes 65568 | tf_op jit(solution)/shard_map/ppermute | solution.py:702
  39.1 1.6 %collective-permute-start.15 = (f32[128,128]{1,0:T(8,128)S(1)}, f32[128,128]{1,0:T(8,128)S(1)}, u32[]{:S(2)}, u32[]{:S(2)}) collective-permute-start(f32[128,128]{1,0:T(8,128)S(1)} %add.12.rest_2_), channel_id=1, source_target_pairs={{0,16},{16,0},{1,17},{17,1},{2,18},{18,2},{3,19},{19,3},{4,20},{20... | collective-permute-start | bytes 196616 | tf_op jit(solution)/shard_map/ppermute | solution.py:683
  40.7 0.2 shard_map.92
  40.9 2.6 %collective-permute-done.15.rest_3_ = f32[128,128]{1,0:T(8,128)S(1)} collective-permute-done((f32[128,128]{1,0:T(8,128)S(1)}, f32[128,128]{1,0:T(8,128)S(1)}, u32[]{:S(2)}, u32[]{:S(2)}) %collective-permute-start.15) | collective-permute-done | bytes 65568 | tf_op jit(solution)/shard_map/ppermute | solution.py:683
  43.5 0.0 collective-permute-done.13.rest_1_
  43.5 5.3 %shard_map.93 = f32[1024,128]{1,0:T(8,128)} custom-call(f32[136,128]{1,0:T(8,128)S(1)} %add.11.rest_0_, f32[136,128]{1,0:T(8,128)S(1)} %collective-permute-done.13.rest_1_, f32[128,128]{1,0:T(8,128)S(1)} %add.12.rest_2_, f32[128,128]{1,0:T(8,128)S(1)} %collective-permute-done.15.rest_3_, bf16[256,256]{1,0:T(8,128)(2,1)S(1)} %get-tuple-element.50.rest_4_, ...), custom_call_target="tpu_custom_call" | custom-call | tf_op jit(solution)/shard_map/pallas_call | solution.py:43
  (5 shorter events, 0.1 us)
Async XLA Ops:
  1.4 9.3 %copy-start.2 = (f32[1,1024]{1,0:T(1,128)S(1)}, f32[1,1024]{1,0:T(1,128)}, u32[]{:S(2)}) copy-start(f32[1,1024]{1,0:T(1,128)} %weights.1) | copy-start | bytes 12292
  1.4 12.8 %collective-permute-start = (f32[208,128]{1,0:T(8,128)S(1)}, f32[208,128]{1,0:T(8,128)S(1)}, u32[]{:S(2)}, u32[]{:S(2)}) collective-permute-start(f32[208,128]{1,0:T(8,128)S(1)} %get-tuple-element.34), channel_id=1, source_target_pairs={{4,8},{12,0},{8,4},{0,12},{5,9},{13,1},{9,5},{1,13},{6,10},{14,2},... | collective-permute-start | bytes 319496 | tf_op jit(solution)/shard_map/ppermute | solution.py:692
  6.5 3.2 %collective-permute-start.4 = (f32[40,128]{1,0:T(8,128)S(1)}, f32[40,128]{1,0:T(8,128)S(1)}, u32[]{:S(2)}, u32[]{:S(2)}) collective-permute-start(f32[40,128]{1,0:T(8,128)S(1)} %get-tuple-element.38), channel_id=1, source_target_pairs={{0,1},{1,2},{2,3},{3,0},{4,5},{5,6},{6,7},{7,4},{8,9},{9,10},{10,1... | collective-permute-start | bytes 61448 | tf_op jit(solution)/shard_map/ppermute | solution.py:683
  6.5 4.2 %copy-start.1 = (f32[1,1024]{1,0:T(1,128)S(1)}, f32[1,1024]{1,0:T(1,128)}, u32[]{:S(2)}) copy-start(f32[1,1024]{1,0:T(1,128)} %values.1) | copy-start | bytes 12292
  6.5 4.2 %copy-start = (s32[1,1024]{1,0:T(1,128)S(1)}, s32[1,1024]{1,0:T(1,128)}, u32[]{:S(2)}) copy-start(s32[1,1024]{1,0:T(1,128)} %cells.1) | copy-start | bytes 12292
  6.5 7.9 %collective-permute-start.1 = (f32[208,128]{1,0:T(8,128)S(1)}, f32[208,128]{1,0:T(8,128)S(1)}, u32[]{:S(2)}, u32[]{:S(2)}) collective-permute-start(f32[208,128]{1,0:T(8,128)S(1)} %get-tuple-element.35), channel_id=1, source_target_pairs={{0,4},{8,12},{4,0},{12,8},{1,5},{9,13},{5,1},{13,9},{2,6},{10,14},... | collective-permute-start | bytes 319496 | tf_op jit(solution)/shard_map/ppermute | solution.py:692
  6.5 4.6 %collective-permute-start.5 = (f32[40,128]{1,0:T(8,128)S(1)}, f32[40,128]{1,0:T(8,128)S(1)}, u32[]{:S(2)}, u32[]{:S(2)}) collective-permute-start(f32[40,128]{1,0:T(8,128)S(1)} %get-tuple-element.39), channel_id=1, source_target_pairs={{0,3},{1,0},{2,1},{3,2},{4,7},{5,4},{6,5},{7,6},{8,11},{9,8},{10,9... | collective-permute-start | bytes 61448 | tf_op jit(solution)/shard_map/ppermute | solution.py:683
  8.3 7.5 %collective-permute-start.2 = (f32[192,128]{1,0:T(8,128)S(1)}, f32[192,128]{1,0:T(8,128)S(1)}, u32[]{:S(2)}, u32[]{:S(2)}) collective-permute-start(f32[192,128]{1,0:T(8,128)S(1)} %get-tuple-element.36), channel_id=1, source_target_pairs={{4,8},{12,0},{8,4},{0,12},{5,9},{13,1},{9,5},{1,13},{6,10},{14,2},... | collective-permute-start | bytes 294920 | tf_op jit(solution)/shard_map/ppermute | solution.py:692
  9.7 8.3 %collective-permute-start.3 = (f32[192,128]{1,0:T(8,128)S(1)}, f32[192,128]{1,0:T(8,128)S(1)}, u32[]{:S(2)}, u32[]{:S(2)}) collective-permute-start(f32[192,128]{1,0:T(8,128)S(1)} %get-tuple-element.37), channel_id=1, source_target_pairs={{0,4},{8,12},{4,0},{12,8},{1,5},{9,13},{5,1},{13,9},{2,6},{10,14},... | collective-permute-start | bytes 294920 | tf_op jit(solution)/shard_map/ppermute | solution.py:692
  11.1 9.4 %collective-permute-start.6 = (f32[168,128]{1,0:T(8,128)S(1)}, f32[168,128]{1,0:T(8,128)S(1)}, u32[]{:S(2)}, u32[]{:S(2)}) collective-permute-start(f32[168,128]{1,0:T(8,128)S(1)} %get-tuple-element.40), channel_id=1, source_target_pairs={{4,8},{12,0},{8,4},{0,12},{5,9},{13,1},{9,5},{1,13},{6,10},{14,2},... | collective-permute-start | bytes 258056 | tf_op jit(solution)/shard_map/ppermute | solution.py:692
  14.1 6.4 %collective-permute-start.7 = (f32[168,128]{1,0:T(8,128)S(1)}, f32[168,128]{1,0:T(8,128)S(1)}, u32[]{:S(2)}, u32[]{:S(2)}) collective-permute-start(f32[168,128]{1,0:T(8,128)S(1)} %get-tuple-element.41), channel_id=1, source_target_pairs={{0,4},{8,12},{4,0},{12,8},{1,5},{9,13},{5,1},{13,9},{2,6},{10,14},... | collective-permute-start | bytes 258056 | tf_op jit(solution)/shard_map/ppermute | solution.py:692
  18.9 13.4 %collective-permute-start.9 = (f32[8,48,128]{2,1,0:T(8,128)S(1)}, f32[8,48,128]{2,1,0:T(8,128)S(1)}, u32[]{:S(2)}, u32[]{:S(2)}) collective-permute-start(f32[8,48,128]{2,1,0:T(8,128)S(1)} %shard_map.85.after.second.own), channel_id=1, source_target_pairs={{0,16},{16,0},{1,17},{17,1},{2,18},{18,2},{3,19},{19,3},{4,20},{20... | collective-permute-start | bytes 589832 | tf_op jit(solution)/shard_map/ppermute | solution.py:683
  21.7 11.5 %collective-permute-start.8 = (f32[8,48,128]{2,1,0:T(8,128)S(1)}, f32[8,48,128]{2,1,0:T(8,128)S(1)}, u32[]{:S(2)}, u32[]{:S(2)}) collective-permute-start(f32[8,48,128]{2,1,0:T(8,128)S(1)} %shard_map.87.sides.own), channel_id=1, source_target_pairs={{0,16},{16,0},{1,17},{17,1},{2,18},{18,2},{3,19},{19,3},{4,20},{20... | collective-permute-start | bytes 589832 | tf_op jit(solution)/shard_map/ppermute | solution.py:683
  23.0 8.7 %collective-permute-start.11 = (f32[8,32,128]{2,1,0:T(8,128)S(1)}, f32[8,32,128]{2,1,0:T(8,128)S(1)}, u32[]{:S(2)}, u32[]{:S(2)}) collective-permute-start(f32[8,32,128]{2,1,0:T(8,128)S(1)} %shard_map.84.after.first.own), channel_id=1, source_target_pairs={{0,16},{16,0},{1,17},{17,1},{2,18},{18,2},{3,19},{19,3},{4,20},{20... | collective-permute-start | bytes 393224 | tf_op jit(solution)/shard_map/ppermute | solution.py:683
  24.8 1.3 %collective-permute-start.10 = (f32[128,128]{1,0:T(8,128)S(1)}, f32[128,128]{1,0:T(8,128)S(1)}, u32[]{:S(2)}, u32[]{:S(2)}) collective-permute-start(f32[128,128]{1,0:T(8,128)S(1)} %get-tuple-element.45), channel_id=1, source_target_pairs={{0,1},{1,0},{2,3},{3,2},{4,5},{5,4},{6,7},{7,6},{8,9},{9,8},{10,11... | collective-permute-start | bytes 196616 | tf_op jit(solution)/shard_map/ppermute | solution.py:702
  33.8 2.6 %collective-permute-start.12 = (f32[136,128]{1,0:T(8,128)S(1)}, f32[136,128]{1,0:T(8,128)S(1)}, u32[]{:S(2)}, u32[]{:S(2)}) collective-permute-start(f32[136,128]{1,0:T(8,128)S(1)} %shard_map.91.after), channel_id=1, source_target_pairs={{0,1},{1,0},{2,3},{3,2},{4,5},{5,4},{6,7},{7,6},{8,9},{9,8},{10,11... | collective-permute-start | bytes 208904 | tf_op jit(solution)/shard_map/ppermute | solution.py:702
  33.9 5.2 %collective-permute-start.14 = (f32[128,128]{1,0:T(8,128)S(1)}, f32[128,128]{1,0:T(8,128)S(1)}, u32[]{:S(2)}, u32[]{:S(2)}) collective-permute-start(f32[128,128]{1,0:T(8,128)S(1)} %add.10.after), channel_id=1, source_target_pairs={{0,2},{1,3},{2,0},{3,1},{4,6},{5,7},{6,4},{7,5},{8,10},{9,11},{10,... | collective-permute-start | bytes 196616 | tf_op jit(solution)/shard_map/ppermute | solution.py:702
  36.4 7.0 %collective-permute-start.13 = (f32[136,128]{1,0:T(8,128)S(1)}, f32[136,128]{1,0:T(8,128)S(1)}, u32[]{:S(2)}, u32[]{:S(2)}) collective-permute-start(f32[136,128]{1,0:T(8,128)S(1)} %add.11.rest_0_), channel_id=1, source_target_pairs={{0,2},{1,3},{2,0},{3,1},{4,6},{5,7},{6,4},{7,5},{8,10},{9,11},{10,... | collective-permute-start | bytes 208904 | tf_op jit(solution)/shard_map/ppermute | solution.py:702
  39.1 4.3 %collective-permute-start.15 = (f32[128,128]{1,0:T(8,128)S(1)}, f32[128,128]{1,0:T(8,128)S(1)}, u32[]{:S(2)}, u32[]{:S(2)}) collective-permute-start(f32[128,128]{1,0:T(8,128)S(1)} %add.12.rest_2_), channel_id=1, source_target_pairs={{0,16},{16,0},{1,17},{17,1},{2,18},{18,2},{3,19},{19,3},{4,20},{20... | collective-permute-start | bytes 196616 | tf_op jit(solution)/shard_map/ppermute | solution.py:683

commit v3 on v2

--- a/solution.py
+++ b/solution.py
@@ -136,7 +136,7 @@
     right[pl.ds(rows * width, rows), pl.ds(0, cols)] = far_edge
 
 
-def turn_kernel(axis, field, left, right, after, early, late):
+def turn_kernel(axis, field, left, right, early, late):
     rows, cols, members = field.shape
     odd = parity(axis)
     width = STEPS
@@ -220,7 +220,7 @@
     return [kept[k].T for k in range(3)], inside, [stage[k].T for k in range(3)], lines
 
 
-def middle_kernel(axis, low, high, pieces, after, field, kept, *refs):
+def middle_kernel(axis, low, high, pieces, field, kept, *refs):
     strips, (out, one, two, spread, stage) = refs[:-5], refs[-5:]
     rows, cols, members = field.shape
     width = STEPS
@@ -343,7 +343,7 @@
     )
 
 
-def weight_kernel(axis, count, cells, values, weights, out):
+def weight_kernel(axis, count, cells, values, weights, after, out):
     cols, twice = out.shape
     rows = twice // 2
     slots = cells.shape[1]
@@ -751,17 +751,8 @@
     received = shift(right, ("role",), 1)
     right = shift(left, ("role",), -1)
     left = received
-    weight = call(
-        functools.partial(weight_kernel, "role"),
-        struct(cols, 2 * rows),
-        observed_count,
-        observed_cells,
-        observed_values,
-        observed_weights,
-        scalars=1,
-    )
     early_rest, late_rest = call(
-        functools.partial(turn_kernel, "domain"), (rest, rest), field, left, right, weight
+        functools.partial(turn_kernel, "domain"), (rest, rest), field, left, right
     )
     early_rest = trade(early_rest, "domain", True)
     late_rest = trade(late_rest, "domain", False)
@@ -774,28 +765,38 @@
     )
     ends = (EDGE, cut - EDGE, end - EDGE)
 
-    def forecast(after, low, high, pieces, *strips):
+    def forecast(low, high, pieces, *strips):
         return call(
             functools.partial(middle_kernel, "domain", low, high, pieces),
             struct(rows, high - low, local),
-            after,
             field,
             kept,
             *strips,
             scratch=scratch,
         )
 
-    first = forecast(weight, *ends[:2], ((0, cut, 0, 0, cut),), early, late)
+    first = forecast(*ends[:2], ((0, cut, 0, 0, cut),), early, late)
     back = 2 * EDGE
     pieces = (
         (0, cut, cut - back, cut - back, back),
         (1, end - cut, 0, cut, end - cut),
     )
-    second = forecast(first, *ends[1:], pieces, early, late, early_next, late_next)
+    second = forecast(*ends[1:], pieces, early, late, early_next, late_next, first)
+    limit = jnp.minimum(observed_count, observed_cells.shape[1])
+    weight = call(
+        functools.partial(weight_kernel, "role"),
+        struct(cols, 2 * rows),
+        limit,
+        observed_cells,
+        observed_values,
+        observed_weights,
+        second,
+        scalars=1,
+    )
     sides = call(
         functools.partial(sides_kernel, "domain"),
         struct(rows, cols - end + 2 * EDGE, local),
-        second,
+        weight,
         field,
         kept,
         early,

time: 48.9 us -> 48.9 us (level)
  no operation moved by 1% of the time
where the time goes in v3:
time: 48.9 us; the launch traced here: 48.7 us
  starting transfers between devices  20.3 us (42%)
  waiting for transfers between devices  14.6 us (30%)
  Pallas kernels  13 us (27%)
  between operations  0.82 us (2%)
    pallas_call x12, Pallas kernels, call(): pl.pallas_call(body, out_shape=outs, in_specs=[SMEM] * scalars + [VMEM] *...  13 us
    ppermute x6, starting transfers between devices, trade(): return lax.ppermute(value, axis, pairs + [(j, i) for i, j in pairs])  9.33 us
    ppermute x6, waiting for transfers between devices, shift(): return lax.ppermute(value, axes if len(axes) > 1 else axes[0], pairs)  8.56 us
    ppermute x6, starting transfers between devices, shift(): return lax.ppermute(value, axes if len(axes) > 1 else axes[0], pairs)  7.01 us
    ppermute x4, starting transfers between devices, role_sums(): other = lax.ppermute(value, 'role', [(i, i ^ step) for i in range(size)])  3.92 us
    ppermute x6, waiting for transfers between devices, trade(): return lax.ppermute(value, axis, pairs + [(j, i) for i, j in pairs])  3.37 us
    ppermute x4, waiting for transfers between devices, role_sums(): other = lax.ppermute(value, 'role', [(i, i ^ step) for i in range(size)])  2.67 us
  transfers between devices with their start and end apart: 16, of which 7 were waited for; matrix products, arithmetic and copies ran while one was open for 0% of the time, Pallas kernels for 12%

profile of v3, /device:TPU:0, one launch (start us, length us, event | category | flops | bytes accessed | tf_op | source)
XLA Modules:
  0.0 48.7 jit_solution(16054926764765572654)
XLA Ops:
  0.0 1.3 %shard_map.82 = (f32[8,128,128]{2,1,0:T(8,128)S(1)}, f32[3,8,128]{2,1,0:T(8,128)S(1)}, f32[208,128]{1,0:T(8,128)S(1)}, f32[208,128]{1,0:T(8,128)S(1)}, f32[192,1...) custom-call(f32[1024,128]{1,0:T(8,128)} %bitcast.2, ...), custom_call_target="tpu_custom_call" | custom-call | tf_op jit(solution)/shard_map/pallas_call | solution.py:43
  1.4 5.1 %collective-permute-start = (f32[208,128]{1,0:T(8,128)S(1)}, f32[208,128]{1,0:T(8,128)S(1)}, u32[]{:S(2)}, u32[]{:S(2)}) collective-permute-start(f32[208,128]{1,0:T(8,128)S(1)} %get-tuple-element.34), channel_id=1, source_target_pairs={{4,8},{12,0},{8,4},{0,12},{5,9},{13,1},{9,5},{1,13},{6,10},{14,2},... | collective-permute-start | bytes 319496 | tf_op jit(solution)/shard_map/ppermute | solution.py:692
  6.5 0.0 collective-permute-start.4
  6.5 0.0 collective-permute-start.1
  6.5 1.7 %collective-permute-start.5 = (f32[40,128]{1,0:T(8,128)S(1)}, f32[40,128]{1,0:T(8,128)S(1)}, u32[]{:S(2)}, u32[]{:S(2)}) collective-permute-start(f32[40,128]{1,0:T(8,128)S(1)} %get-tuple-element.39), channel_id=1, source_target_pairs={{0,3},{1,0},{2,1},{3,2},{4,7},{5,4},{6,5},{7,6},{8,11},{9,8},{10,9... | collective-permute-start | bytes 61448 | tf_op jit(solution)/shard_map/ppermute | solution.py:683
  8.3 0.6 %collective-permute-start.2 = (f32[192,128]{1,0:T(8,128)S(1)}, f32[192,128]{1,0:T(8,128)S(1)}, u32[]{:S(2)}, u32[]{:S(2)}) collective-permute-start(f32[192,128]{1,0:T(8,128)S(1)} %get-tuple-element.36), channel_id=1, source_target_pairs={{4,8},{12,0},{8,4},{0,12},{5,9},{13,1},{9,5},{1,13},{6,10},{14,2},... | collective-permute-start | bytes 294920 | tf_op jit(solution)/shard_map/ppermute | solution.py:692
  8.9 0.8 %collective-permute-done.4.left = f32[40,128]{1,0:T(8,128)S(1)} collective-permute-done((f32[40,128]{1,0:T(8,128)S(1)}, f32[40,128]{1,0:T(8,128)S(1)}, u32[]{:S(2)}, u32[]{:S(2)}) %collective-permute-start.4) | collective-permute-done | bytes 20512 | tf_op jit(solution)/shard_map/ppermute | solution.py:683
  9.7 0.3 collective-permute-start.3
  10.0 0.0 collective-permute-done.5.right
  10.0 3.0 %collective-permute-start.6 = (f32[168,128]{1,0:T(8,128)S(1)}, f32[168,128]{1,0:T(8,128)S(1)}, u32[]{:S(2)}, u32[]{:S(2)}) collective-permute-start(f32[168,128]{1,0:T(8,128)S(1)} %get-tuple-element.40), channel_id=1, source_target_pairs={{4,8},{12,0},{8,4},{0,12},{5,9},{13,1},{9,5},{1,13},{6,10},{14,2},... | collective-permute-start | bytes 258056 | tf_op jit(solution)/shard_map/ppermute | solution.py:692
  13.0 0.0 collective-permute-done.refs_0_.early
  13.0 0.3 collective-permute-start.7
  14.0 0.0 collective-permute-done.1.refs_1_.late
  14.0 0.7 %shard_map.83.refs_4_.first.own = f32[8,32,128]{2,1,0:T(8,128)S(1)} custom-call(f32[8,128,128]{2,1,0:T(8,128)S(1)} %get-tuple-element.32.field, f32[3,8,128]{2,1,0:T(8,128)S(1)} %get-tuple-element.33.kept, f32[208,128]{1,0:T(8,128)S(1)} %collective-permute-done.refs_0_.early, f32[208,128]{1,0:T(8,128)S(1)} %collective-permute-done.1.refs_1_.late), custom_call_target="tpu_custom_call" | custom-call | tf_op jit(solution)/shard_map/pallas_call | solution.py:43
  14.6 0.0 copy-start
  14.6 0.0 copy-start.1
  14.7 0.0 copy-start.2
  14.7 1.0 %collective-permute-done.2.refs_2_.early_next = f32[192,128]{1,0:T(8,128)S(1)} collective-permute-done((f32[192,128]{1,0:T(8,128)S(1)}, f32[192,128]{1,0:T(8,128)S(1)}, u32[]{:S(2)}, u32[]{:S(2)}) %collective-permute-start.2) | collective-permute-done | bytes 98336 | tf_op jit(solution)/shard_map/ppermute | solution.py:692
  15.7 2.3 %collective-permute-done.3.refs_3_.late_next = f32[192,128]{1,0:T(8,128)S(1)} collective-permute-done((f32[192,128]{1,0:T(8,128)S(1)}, f32[192,128]{1,0:T(8,128)S(1)}, u32[]{:S(2)}, u32[]{:S(2)}) %collective-permute-start.3) | collective-permute-done | bytes 98336 | tf_op jit(solution)/shard_map/ppermute | solution.py:692
  18.0 0.9 %shard_map.84.after.second.own = f32[8,48,128]{2,1,0:T(8,128)S(1)} custom-call(f32[8,128,128]{2,1,0:T(8,128)S(1)} %get-tuple-element.32.field, f32[3,8,128]{2,1,0:T(8,128)S(1)} %get-tuple-element.33.kept, f32[208,128]{1,0:T(8,128)S(1)} %collective-permute-done.refs_0_.early, f32[208,128]{1,0:T(8,128)S(1)} %collective-permute-done.1.refs_1_.late, ...), custom_call_target="tpu_custom_call" | custom-call | tf_op jit(solution)/shard_map/pallas_call | solution.py:43
  18.9 1.6 %collective-permute-start.9 = (f32[8,48,128]{2,1,0:T(8,128)S(1)}, f32[8,48,128]{2,1,0:T(8,128)S(1)}, u32[]{:S(2)}, u32[]{:S(2)}) collective-permute-start(f32[8,48,128]{2,1,0:T(8,128)S(1)} %shard_map.84.after.second.own), channel_id=1, source_target_pairs={{0,16},{16,0},{1,17},{17,1},{2,18},{18,2},{3,19},{19,3},{4,20},{20... | collective-permute-start | bytes 589832 | tf_op jit(solution)/shard_map/ppermute | solution.py:683
  20.5 0.0 copy-done
  20.5 0.0 copy-done.1
  20.5 0.4 shard_map.85.after.weight
  20.9 0.0 collective-permute-done.6.early_rest
  20.9 0.0 collective-permute-done.7.late_rest
  20.9 1.1 %shard_map.87.sides.own = f32[8,48,128]{2,1,0:T(8,128)S(1)} custom-call(f32[128,16]{1,0:T(8,128)S(1)} %shard_map.85.after.weight, f32[8,128,128]{2,1,0:T(8,128)S(1)} %get-tuple-element.32.field, f32[3,8,128]{2,1,0:T(8,128)S(1)} %get-tuple-element.33.kept, f32[208,128]{1,0:T(8,128)S(1)} %collective-permute-done.refs_0_.early, ...), custom_call_target="tpu_custom_call" | custom-call | tf_op jit(solution)/shard_map/pallas_call | solution.py:43
  22.1 0.9 %collective-permute-start.8 = (f32[8,48,128]{2,1,0:T(8,128)S(1)}, f32[8,48,128]{2,1,0:T(8,128)S(1)}, u32[]{:S(2)}, u32[]{:S(2)}) collective-permute-start(f32[8,48,128]{2,1,0:T(8,128)S(1)} %shard_map.87.sides.own), channel_id=1, source_target_pairs={{0,16},{16,0},{1,17},{17,1},{2,18},{18,2},{3,19},{19,3},{4,20},{20... | collective-permute-start | bytes 589832 | tf_op jit(solution)/shard_map/ppermute | solution.py:683
  23.0 1.2 %collective-permute-start.11 = (f32[8,32,128]{2,1,0:T(8,128)S(1)}, f32[8,32,128]{2,1,0:T(8,128)S(1)}, u32[]{:S(2)}, u32[]{:S(2)}) collective-permute-start(f32[8,32,128]{2,1,0:T(8,128)S(1)} %shard_map.83.refs_4_.first.own), channel_id=1, source_target_pairs={{0,16},{16,0},{1,17},{17,1},{2,18},{18,2},{3,19},{19,3},{4,20},{20... | collective-permute-start | bytes 393224 | tf_op jit(solution)/shard_map/ppermute | solution.py:683
  24.2 1.0 %shard_map.88 = (f32[128,128]{1,0:T(8,128)S(1)}, bf16[128,384]{1,0:T(8,128)(2,1)S(1)}, bf16[128,384]{1,0:T(8,128)(2,1)S(1)}, f32[384,128]{1,0:T(8,128)S(1)}) custom-call(f32[8,32,128]{2,1,0:T(8,128)S(1)} %shard_map.83.refs_4_.first.own, f32[8,48,128]{2,1,0:T(8,128)S(1)} %shard_map.84.after.second.own, f32[8,48,128]{2,1,0:T(8,128)S(1)} %shard_map.87.sides.own, ...), custom_call_target="tpu_custom_call" | custom-call | tf_op jit(solution)/shard_map/pallas_call | solution.py:43
  25.2 0.1 collective-permute-start.10
  25.3 1.2 %collective-permute-done.10 = f32[128,128]{1,0:T(8,128)S(1)} collective-permute-done((f32[128,128]{1,0:T(8,128)S(1)}, f32[128,128]{1,0:T(8,128)S(1)}, u32[]{:S(2)}, u32[]{:S(2)}) %collective-permute-start.10) | collective-permute-done | bytes 65568 | tf_op jit(solution)/shard_map/ppermute | solution.py:702
  26.5 5.1 %collective-permute-done.11.other = f32[8,32,128]{2,1,0:T(8,128)S(1)} collective-permute-done((f32[8,32,128]{2,1,0:T(8,128)S(1)}, f32[8,32,128]{2,1,0:T(8,128)S(1)}, u32[]{:S(2)}, u32[]{:S(2)}) %collective-permute-start.11) | collective-permute-done | bytes 131104 | tf_op jit(solution)/shard_map/ppermute | solution.py:683
  31.7 0.6 %shard_map.89 = (bf16[256,256]{1,0:T(8,128)(2,1)S(1)}, bf16[256,256]{1,0:T(8,128)(2,1)S(1)}, f32[8,128]{1,0:T(8,128)S(1)}, f32[136,128]{1,0:T(8,128)S(1)}) custom-call(f32[8,32,128]{2,1,0:T(8,128)S(1)} %shard_map.83.refs_4_.first.own, f32[8,32,128]{2,1,0:T(8,128)S(1)} %collective-permute-done.11.other, f32[128,16]{1,0:T(8,128)S(1)} %shard_map.85.after.weight, ...), custom_call_target="tpu_custom_call" | custom-call | tf_op jit(solution)/shard_map/pallas_call | solution.py:43
  32.3 0.0 collective-permute-done.9.other
  32.3 0.9 %shard_map.90 = (bf16[384,256]{1,0:T(8,128)(2,1)S(1)}, bf16[384,256]{1,0:T(8,128)(2,1)S(1)}, f32[8,128]{1,0:T(8,128)S(1)}, f32[136,128]{1,0:T(8,128)S(1)}) custom-call(f32[8,48,128]{2,1,0:T(8,128)S(1)} %shard_map.84.after.second.own, f32[8,48,128]{2,1,0:T(8,128)S(1)} %collective-permute-done.9.other, f32[128,16]{1,0:T(8,128)S(1)} %shard_map.85.after.weight, ...), custom_call_target="tpu_custom_call" | custom-call | tf_op jit(solution)/shard_map/pallas_call | solution.py:43
  33.2 0.0 collective-permute-done.8.other
  33.2 0.6 %shard_map.91.after = f32[136,128]{1,0:T(8,128)S(1)} custom-call(f32[8,48,128]{2,1,0:T(8,128)S(1)} %shard_map.87.sides.own, f32[8,48,128]{2,1,0:T(8,128)S(1)} %collective-permute-done.8.other, bf16[128,384]{1,0:T(8,128)(2,1)S(1)} %get-tuple-element.42.left, bf16[128,384]{1,0:T(8,128)(2,1)S(1)} %get-tuple-element.43.right, ...), custom_call_target="tpu_custom_call" | custom-call | tf_op jit(solution)/shard_map/pallas_call | solution.py:43
  33.8 0.1 collective-permute-start.12
  33.9 2.5 %collective-permute-start.14 = (f32[128,128]{1,0:T(8,128)S(1)}, f32[128,128]{1,0:T(8,128)S(1)}, u32[]{:S(2)}, u32[]{:S(2)}) collective-permute-start(f32[128,128]{1,0:T(8,128)S(1)} %add.10.after), channel_id=1, source_target_pairs={{0,2},{1,3},{2,0},{3,1},{4,6},{5,7},{6,4},{7,5},{8,10},{9,11},{10,... | collective-permute-start | bytes 196616 | tf_op jit(solution)/shard_map/ppermute | solution.py:702
  36.4 0.0 collective-permute-done.12
  36.4 1.2 %collective-permute-start.13 = (f32[136,128]{1,0:T(8,128)S(1)}, f32[136,128]{1,0:T(8,128)S(1)}, u32[]{:S(2)}, u32[]{:S(2)}) collective-permute-start(f32[136,128]{1,0:T(8,128)S(1)} %add.11.rest_0_), channel_id=1, source_target_pairs={{0,2},{1,3},{2,0},{3,1},{4,6},{5,7},{6,4},{7,5},{8,10},{9,11},{10,... | collective-permute-start | bytes 208904 | tf_op jit(solution)/shard_map/ppermute | solution.py:702
  37.7 1.4 %collective-permute-done.14 = f32[128,128]{1,0:T(8,128)S(1)} collective-permute-done((f32[128,128]{1,0:T(8,128)S(1)}, f32[128,128]{1,0:T(8,128)S(1)}, u32[]{:S(2)}, u32[]{:S(2)}) %collective-permute-start.14) | collective-permute-done | bytes 65568 | tf_op jit(solution)/shard_map/ppermute | solution.py:702
  39.1 1.6 %collective-permute-start.15 = (f32[128,128]{1,0:T(8,128)S(1)}, f32[128,128]{1,0:T(8,128)S(1)}, u32[]{:S(2)}, u32[]{:S(2)}) collective-permute-start(f32[128,128]{1,0:T(8,128)S(1)} %add.12.rest_2_), channel_id=1, source_target_pairs={{0,16},{16,0},{1,17},{17,1},{2,18},{18,2},{3,19},{19,3},{4,20},{20... | collective-permute-start | bytes 196616 | tf_op jit(solution)/shard_map/ppermute | solution.py:683
  40.7 0.2 shard_map.92
  40.9 2.6 %collective-permute-done.15.rest_3_ = f32[128,128]{1,0:T(8,128)S(1)} collective-permute-done((f32[128,128]{1,0:T(8,128)S(1)}, f32[128,128]{1,0:T(8,128)S(1)}, u32[]{:S(2)}, u32[]{:S(2)}) %collective-permute-start.15) | collective-permute-done | bytes 65568 | tf_op jit(solution)/shard_map/ppermute | solution.py:683
  43.4 0.0 collective-permute-done.13.rest_1_
  43.4 5.3 %shard_map.93 = f32[1024,128]{1,0:T(8,128)} custom-call(f32[136,128]{1,0:T(8,128)S(1)} %add.11.rest_0_, f32[136,128]{1,0:T(8,128)S(1)} %collective-permute-done.13.rest_1_, f32[128,128]{1,0:T(8,128)S(1)} %add.12.rest_2_, f32[128,128]{1,0:T(8,128)S(1)} %collective-permute-done.15.rest_3_, bf16[256,256]{1,0:T(8,128)(2,1)S(1)} %get-tuple-element.50.rest_4_, ...), custom_call_target="tpu_custom_call" | custom-call | tf_op jit(solution)/shard_map/pallas_call | solution.py:43
  (5 shorter events, 0.0 us)
Async XLA Ops:
  1.4 11.7 %collective-permute-start = (f32[208,128]{1,0:T(8,128)S(1)}, f32[208,128]{1,0:T(8,128)S(1)}, u32[]{:S(2)}, u32[]{:S(2)}) collective-permute-start(f32[208,128]{1,0:T(8,128)S(1)} %get-tuple-element.34), channel_id=1, source_target_pairs={{4,8},{12,0},{8,4},{0,12},{5,9},{13,1},{9,5},{1,13},{6,10},{14,2},... | collective-permute-start | bytes 319496 | tf_op jit(solution)/shard_map/ppermute | solution.py:692
  6.5 3.2 %collective-permute-start.4 = (f32[40,128]{1,0:T(8,128)S(1)}, f32[40,128]{1,0:T(8,128)S(1)}, u32[]{:S(2)}, u32[]{:S(2)}) collective-permute-start(f32[40,128]{1,0:T(8,128)S(1)} %get-tuple-element.38), channel_id=1, source_target_pairs={{0,1},{1,2},{2,3},{3,0},{4,5},{5,6},{6,7},{7,4},{8,9},{9,10},{10,1... | collective-permute-start | bytes 61448 | tf_op jit(solution)/shard_map/ppermute | solution.py:683
  6.5 7.5 %collective-permute-start.1 = (f32[208,128]{1,0:T(8,128)S(1)}, f32[208,128]{1,0:T(8,128)S(1)}, u32[]{:S(2)}, u32[]{:S(2)}) collective-permute-start(f32[208,128]{1,0:T(8,128)S(1)} %get-tuple-element.35), channel_id=1, source_target_pairs={{0,4},{8,12},{4,0},{12,8},{1,5},{9,13},{5,1},{13,9},{2,6},{10,14},... | collective-permute-start | bytes 319496 | tf_op jit(solution)/shard_map/ppermute | solution.py:692
  6.5 3.5 %collective-permute-start.5 = (f32[40,128]{1,0:T(8,128)S(1)}, f32[40,128]{1,0:T(8,128)S(1)}, u32[]{:S(2)}, u32[]{:S(2)}) collective-permute-start(f32[40,128]{1,0:T(8,128)S(1)} %get-tuple-element.39), channel_id=1, source_target_pairs={{0,3},{1,0},{2,1},{3,2},{4,7},{5,4},{6,5},{7,6},{8,11},{9,8},{10,9... | collective-permute-start | bytes 61448 | tf_op jit(solution)/shard_map/ppermute | solution.py:683
  8.3 7.5 %collective-permute-start.2 = (f32[192,128]{1,0:T(8,128)S(1)}, f32[192,128]{1,0:T(8,128)S(1)}, u32[]{:S(2)}, u32[]{:S(2)}) collective-permute-start(f32[192,128]{1,0:T(8,128)S(1)} %get-tuple-element.36), channel_id=1, source_target_pairs={{4,8},{12,0},{8,4},{0,12},{5,9},{13,1},{9,5},{1,13},{6,10},{14,2},... | collective-permute-start | bytes 294920 | tf_op jit(solution)/shard_map/ppermute | solution.py:692
  9.7 8.3 %collective-permute-start.3 = (f32[192,128]{1,0:T(8,128)S(1)}, f32[192,128]{1,0:T(8,128)S(1)}, u32[]{:S(2)}, u32[]{:S(2)}) collective-permute-start(f32[192,128]{1,0:T(8,128)S(1)} %get-tuple-element.37), channel_id=1, source_target_pairs={{0,4},{8,12},{4,0},{12,8},{1,5},{9,13},{5,1},{13,9},{2,6},{10,14},... | collective-permute-start | bytes 294920 | tf_op jit(solution)/shard_map/ppermute | solution.py:692
  10.0 10.9 %collective-permute-start.6 = (f32[168,128]{1,0:T(8,128)S(1)}, f32[168,128]{1,0:T(8,128)S(1)}, u32[]{:S(2)}, u32[]{:S(2)}) collective-permute-start(f32[168,128]{1,0:T(8,128)S(1)} %get-tuple-element.40), channel_id=1, source_target_pairs={{4,8},{12,0},{8,4},{0,12},{5,9},{13,1},{9,5},{1,13},{6,10},{14,2},... | collective-permute-start | bytes 258056 | tf_op jit(solution)/shard_map/ppermute | solution.py:692
  13.0 7.9 %collective-permute-start.7 = (f32[168,128]{1,0:T(8,128)S(1)}, f32[168,128]{1,0:T(8,128)S(1)}, u32[]{:S(2)}, u32[]{:S(2)}) collective-permute-start(f32[168,128]{1,0:T(8,128)S(1)} %get-tuple-element.41), channel_id=1, source_target_pairs={{0,4},{8,12},{4,0},{12,8},{1,5},{9,13},{5,1},{13,9},{2,6},{10,14},... | collective-permute-start | bytes 258056 | tf_op jit(solution)/shard_map/ppermute | solution.py:692
  14.6 5.9 %copy-start = (s32[1,1024]{1,0:T(1,128)S(1)}, s32[1,1024]{1,0:T(1,128)}, u32[]{:S(2)}) copy-start(s32[1,1024]{1,0:T(1,128)} %cells.1) | copy-start | bytes 12292
  14.6 5.9 %copy-start.1 = (f32[1,1024]{1,0:T(1,128)S(1)}, f32[1,1024]{1,0:T(1,128)}, u32[]{:S(2)}) copy-start(f32[1,1024]{1,0:T(1,128)} %values.1) | copy-start | bytes 12292
  14.7 5.9 %copy-start.2 = (f32[1,1024]{1,0:T(1,128)S(1)}, f32[1,1024]{1,0:T(1,128)}, u32[]{:S(2)}) copy-start(f32[1,1024]{1,0:T(1,128)} %weights.1) | copy-start | bytes 12292
  18.9 13.4 %collective-permute-start.9 = (f32[8,48,128]{2,1,0:T(8,128)S(1)}, f32[8,48,128]{2,1,0:T(8,128)S(1)}, u32[]{:S(2)}, u32[]{:S(2)}) collective-permute-start(f32[8,48,128]{2,1,0:T(8,128)S(1)} %shard_map.84.after.second.own), channel_id=1, source_target_pairs={{0,16},{16,0},{1,17},{17,1},{2,18},{18,2},{3,19},{19,3},{4,20},{20... | collective-permute-start | bytes 589832 | tf_op jit(solution)/shard_map/ppermute | solution.py:683
  22.1 11.1 %collective-permute-start.8 = (f32[8,48,128]{2,1,0:T(8,128)S(1)}, f32[8,48,128]{2,1,0:T(8,128)S(1)}, u32[]{:S(2)}, u32[]{:S(2)}) collective-permute-start(f32[8,48,128]{2,1,0:T(8,128)S(1)} %shard_map.87.sides.own), channel_id=1, source_target_pairs={{0,16},{16,0},{1,17},{17,1},{2,18},{18,2},{3,19},{19,3},{4,20},{20... | collective-permute-start | bytes 589832 | tf_op jit(solution)/shard_map/ppermute | solution.py:683
  23.0 8.7 %collective-permute-start.11 = (f32[8,32,128]{2,1,0:T(8,128)S(1)}, f32[8,32,128]{2,1,0:T(8,128)S(1)}, u32[]{:S(2)}, u32[]{:S(2)}) collective-permute-start(f32[8,32,128]{2,1,0:T(8,128)S(1)} %shard_map.83.refs_4_.first.own), channel_id=1, source_target_pairs={{0,16},{16,0},{1,17},{17,1},{2,18},{18,2},{3,19},{19,3},{4,20},{20... | collective-permute-start | bytes 393224 | tf_op jit(solution)/shard_map/ppermute | solution.py:683
  25.2 1.3 %collective-permute-start.10 = (f32[128,128]{1,0:T(8,128)S(1)}, f32[128,128]{1,0:T(8,128)S(1)}, u32[]{:S(2)}, u32[]{:S(2)}) collective-permute-start(f32[128,128]{1,0:T(8,128)S(1)} %get-tuple-element.45), channel_id=1, source_target_pairs={{0,1},{1,0},{2,3},{3,2},{4,5},{5,4},{6,7},{7,6},{8,9},{9,8},{10,11... | collective-permute-start | bytes 196616 | tf_op jit(solution)/shard_map/ppermute | solution.py:702
  33.8 2.6 %collective-permute-start.12 = (f32[136,128]{1,0:T(8,128)S(1)}, f32[136,128]{1,0:T(8,128)S(1)}, u32[]{:S(2)}, u32[]{:S(2)}) collective-permute-start(f32[136,128]{1,0:T(8,128)S(1)} %shard_map.91.after), channel_id=1, source_target_pairs={{0,1},{1,0},{2,3},{3,2},{4,5},{5,4},{6,7},{7,6},{8,9},{9,8},{10,11... | collective-permute-start | bytes 208904 | tf_op jit(solution)/shard_map/ppermute | solution.py:702
  33.9 5.2 %collective-permute-start.14 = (f32[128,128]{1,0:T(8,128)S(1)}, f32[128,128]{1,0:T(8,128)S(1)}, u32[]{:S(2)}, u32[]{:S(2)}) collective-permute-start(f32[128,128]{1,0:T(8,128)S(1)} %add.10.after), channel_id=1, source_target_pairs={{0,2},{1,3},{2,0},{3,1},{4,6},{5,7},{6,4},{7,5},{8,10},{9,11},{10,... | collective-permute-start | bytes 196616 | tf_op jit(solution)/shard_map/ppermute | solution.py:702
  36.4 7.0 %collective-permute-start.13 = (f32[136,128]{1,0:T(8,128)S(1)}, f32[136,128]{1,0:T(8,128)S(1)}, u32[]{:S(2)}, u32[]{:S(2)}) collective-permute-start(f32[136,128]{1,0:T(8,128)S(1)} %add.11.rest_0_), channel_id=1, source_target_pairs={{0,2},{1,3},{2,0},{3,1},{4,6},{5,7},{6,4},{7,5},{8,10},{9,11},{10,... | collective-permute-start | bytes 208904 | tf_op jit(solution)/shard_map/ppermute | solution.py:702
  39.1 4.3 %collective-permute-start.15 = (f32[128,128]{1,0:T(8,128)S(1)}, f32[128,128]{1,0:T(8,128)S(1)}, u32[]{:S(2)}, u32[]{:S(2)}) collective-permute-start(f32[128,128]{1,0:T(8,128)S(1)} %add.12.rest_2_), channel_id=1, source_target_pairs={{0,16},{16,0},{1,17},{17,1},{2,18},{18,2},{3,19},{19,3},{4,20},{20... | collective-permute-start | bytes 196616 | tf_op jit(solution)/shard_map/ppermute | solution.py:683

commit v4 on v2

--- a/solution.py
+++ b/solution.py
@@ -59,8 +59,16 @@
     return lax.dot_general(a, b, (dims, ((), ())), preferred_element_type=jnp.float32)
 
 
-def dot3(a, b, dims=((1,), (0,))):
-    return dot(a[0], b[0], dims) + (dot(a[0], b[1], dims) + dot(a[1], b[0], dims))
+def by_halves(product, *operands):
+    half = operands[0].shape[0] // 2
+    parts = [product(*(o[at] for o in operands)) for at in (slice(0, half), slice(half, None))]
+    return jnp.concatenate(parts, axis=0)
+
+
+def dot3(a, b):
+    return by_halves(
+        lambda high, low: (dot(high, b[0]) + dot(low, b[0])) + dot(high, b[1]), *a
+    )
 
 
 def loop(count, body):

time: 48.9 us -> 48.3 us (0.988)
  Pallas kernels: 13 us -> 12.4 us
    pallas_call x12, Pallas kernels: 13 us -> 12.4 us  [call(): pl.pallas_call(body, out_shape=outs, in_specs=[SMEM] * scalars + [VMEM] *...]
where the time goes in v4:
time: 48.3 us; the launch traced here: 48.2 us
  starting transfers between devices  20.3 us (42%)
  waiting for transfers between devices  14.6 us (30%)
  Pallas kernels  12.4 us (26%)
  between operations  0.83 us (2%)
    pallas_call x12, Pallas kernels, call(): pl.pallas_call(body, out_shape=outs, in_specs=[SMEM] * scalars + [VMEM] *...  12.4 us
    ppermute x6, starting transfers between devices, trade(): return lax.ppermute(value, axis, pairs + [(j, i) for i, j in pairs])  9.33 us
    ppermute x6, waiting for transfers between devices, shift(): return lax.ppermute(value, axes if len(axes) > 1 else axes[0], pairs)  8.98 us
    ppermute x6, starting transfers between devices, shift(): return lax.ppermute(value, axes if len(axes) > 1 else axes[0], pairs)  7 us
    ppermute x4, starting transfers between devices, role_sums(): other = lax.ppermute(value, 'role', [(i, i ^ step) for i in range(size)])  3.92 us
    ppermute x6, waiting for transfers between devices, trade(): return lax.ppermute(value, axis, pairs + [(j, i) for i, j in pairs])  2.97 us
    ppermute x4, waiting for transfers between devices, role_sums(): other = lax.ppermute(value, 'role', [(i, i ^ step) for i in range(size)])  2.67 us
  transfers between devices with their start and end apart: 16, of which 7 were waited for; matrix products, arithmetic and copies ran while one was open for 0% of the time, Pallas kernels for 12%

profile of v4, /device:TPU:0, one launch (start us, length us, event | category | flops | bytes accessed | tf_op | source)
XLA Modules:
  0.0 48.2 jit_solution(10487293611841130187)
XLA Ops:
  0.0 1.3 %shard_map.83 = (f32[8,128,128]{2,1,0:T(8,128)S(1)}, f32[3,8,128]{2,1,0:T(8,128)S(1)}, f32[208,128]{1,0:T(8,128)S(1)}, f32[208,128]{1,0:T(8,128)S(1)}, f32[192,1...) custom-call(f32[1024,128]{1,0:T(8,128)} %bitcast.2, ...), custom_call_target="tpu_custom_call" | custom-call | tf_op jit(solution)/shard_map/pallas_call | solution.py:43
  1.4 0.0 copy-start.2
  1.4 5.1 %collective-permute-start = (f32[208,128]{1,0:T(8,128)S(1)}, f32[208,128]{1,0:T(8,128)S(1)}, u32[]{:S(2)}, u32[]{:S(2)}) collective-permute-start(f32[208,128]{1,0:T(8,128)S(1)} %get-tuple-element.34), channel_id=1, source_target_pairs={{4,8},{12,0},{8,4},{0,12},{5,9},{13,1},{9,5},{1,13},{6,10},{14,2},... | collective-permute-start | bytes 319496 | tf_op jit(solution)/shard_map/ppermute | solution.py:700
  6.5 0.0 collective-permute-start.4
  6.5 0.0 copy-start.1
  6.5 0.0 collective-permute-start.1
  6.5 1.7 %collective-permute-start.5 = (f32[40,128]{1,0:T(8,128)S(1)}, f32[40,128]{1,0:T(8,128)S(1)}, u32[]{:S(2)}, u32[]{:S(2)}) collective-permute-start(f32[40,128]{1,0:T(8,128)S(1)} %get-tuple-element.39), channel_id=1, source_target_pairs={{0,3},{1,0},{2,1},{3,2},{4,7},{5,4},{6,5},{7,6},{8,11},{9,8},{10,9... | collective-permute-start | bytes 61448 | tf_op jit(solution)/shard_map/ppermute | solution.py:691
  8.3 0.6 %collective-permute-start.2 = (f32[192,128]{1,0:T(8,128)S(1)}, f32[192,128]{1,0:T(8,128)S(1)}, u32[]{:S(2)}, u32[]{:S(2)}) collective-permute-start(f32[192,128]{1,0:T(8,128)S(1)} %get-tuple-element.36), channel_id=1, source_target_pairs={{4,8},{12,0},{8,4},{0,12},{5,9},{13,1},{9,5},{1,13},{6,10},{14,2},... | collective-permute-start | bytes 294920 | tf_op jit(solution)/shard_map/ppermute | solution.py:700
  8.9 0.8 %collective-permute-done.4.left = f32[40,128]{1,0:T(8,128)S(1)} collective-permute-done((f32[40,128]{1,0:T(8,128)S(1)}, f32[40,128]{1,0:T(8,128)S(1)}, u32[]{:S(2)}, u32[]{:S(2)}) %collective-permute-start.4) | collective-permute-done | bytes 20512 | tf_op jit(solution)/shard_map/ppermute | solution.py:691
  9.7 0.3 collective-permute-start.3
  10.7 0.0 copy-done.2
  10.7 0.0 copy-done.1
  10.7 0.0 copy-done
  10.7 0.4 shard_map.82.after.weight
  11.1 0.0 collective-permute-done.5.right
  11.1 3.0 %collective-permute-start.6 = (f32[168,128]{1,0:T(8,128)S(1)}, f32[168,128]{1,0:T(8,128)S(1)}, u32[]{:S(2)}, u32[]{:S(2)}) collective-permute-start(f32[168,128]{1,0:T(8,128)S(1)} %get-tuple-element.40), channel_id=1, source_target_pairs={{4,8},{12,0},{8,4},{0,12},{5,9},{13,1},{9,5},{1,13},{6,10},{14,2},... | collective-permute-start | bytes 258056 | tf_op jit(solution)/shard_map/ppermute | solution.py:700
  14.1 0.0 collective-permute-done.refs_0_.early
  14.1 0.3 collective-permute-start.7
  14.4 0.0 collective-permute-done.1.refs_1_.late
  14.4 0.7 %shard_map.84.after.first.own = f32[8,32,128]{2,1,0:T(8,128)S(1)} custom-call(f32[128,16]{1,0:T(8,128)S(1)} %shard_map.82.after.weight, f32[8,128,128]{2,1,0:T(8,128)S(1)} %get-tuple-element.32.field, f32[3,8,128]{2,1,0:T(8,128)S(1)} %get-tuple-element.33.kept, f32[208,128]{1,0:T(8,128)S(1)} %collective-permute-done.refs_0_.early, ...), custom_call_target="tpu_custom_call" | custom-call | tf_op jit(solution)/shard_map/pallas_call | solution.py:43
  15.1 0.6 %collective-permute-done.2.refs_2_.early_next = f32[192,128]{1,0:T(8,128)S(1)} collective-permute-done((f32[192,128]{1,0:T(8,128)S(1)}, f32[192,128]{1,0:T(8,128)S(1)}, u32[]{:S(2)}, u32[]{:S(2)}) %collective-permute-start.2) | collective-permute-done | bytes 98336 | tf_op jit(solution)/shard_map/ppermute | solution.py:700
  15.7 2.3 %collective-permute-done.3.refs_3_.late_next = f32[192,128]{1,0:T(8,128)S(1)} collective-permute-done((f32[192,128]{1,0:T(8,128)S(1)}, f32[192,128]{1,0:T(8,128)S(1)}, u32[]{:S(2)}, u32[]{:S(2)}) %collective-permute-start.3) | collective-permute-done | bytes 98336 | tf_op jit(solution)/shard_map/ppermute | solution.py:700
  18.1 0.9 %shard_map.85.after.second.own = f32[8,48,128]{2,1,0:T(8,128)S(1)} custom-call(f32[8,32,128]{2,1,0:T(8,128)S(1)} %shard_map.84.after.first.own, f32[8,128,128]{2,1,0:T(8,128)S(1)} %get-tuple-element.32.field, f32[3,8,128]{2,1,0:T(8,128)S(1)} %get-tuple-element.33.kept, f32[208,128]{1,0:T(8,128)S(1)} %collective-permute-done.refs_0_.early, ...), custom_call_target="tpu_custom_call" | custom-call | tf_op jit(solution)/shard_map/pallas_call | solution.py:43
  18.9 1.6 %collective-permute-start.9 = (f32[8,48,128]{2,1,0:T(8,128)S(1)}, f32[8,48,128]{2,1,0:T(8,128)S(1)}, u32[]{:S(2)}, u32[]{:S(2)}) collective-permute-start(f32[8,48,128]{2,1,0:T(8,128)S(1)} %shard_map.85.after.second.own), channel_id=1, source_target_pairs={{0,16},{16,0},{1,17},{17,1},{2,18},{18,2},{3,19},{19,3},{4,20},{20... | collective-permute-start | bytes 589832 | tf_op jit(solution)/shard_map/ppermute | solution.py:691
  20.5 0.0 collective-permute-done.6.early_rest
  20.5 0.0 collective-permute-done.7.late_rest
  20.5 1.1 %shard_map.87.sides.own = f32[8,48,128]{2,1,0:T(8,128)S(1)} custom-call(f32[8,48,128]{2,1,0:T(8,128)S(1)} %shard_map.85.after.second.own, f32[8,128,128]{2,1,0:T(8,128)S(1)} %get-tuple-element.32.field, f32[3,8,128]{2,1,0:T(8,128)S(1)} %get-tuple-element.33.kept, f32[208,128]{1,0:T(8,128)S(1)} %collective-permute-done.refs_0_.early, ...), custom_call_target="tpu_custom_call" | custom-call | tf_op jit(solution)/shard_map/pallas_call | solution.py:43
  21.7 1.3 %collective-permute-start.8 = (f32[8,48,128]{2,1,0:T(8,128)S(1)}, f32[8,48,128]{2,1,0:T(8,128)S(1)}, u32[]{:S(2)}, u32[]{:S(2)}) collective-permute-start(f32[8,48,128]{2,1,0:T(8,128)S(1)} %shard_map.87.sides.own), channel_id=1, source_target_pairs={{0,16},{16,0},{1,17},{17,1},{2,18},{18,2},{3,19},{19,3},{4,20},{20... | collective-permute-start | bytes 589832 | tf_op jit(solution)/shard_map/ppermute | solution.py:691
  23.0 0.8 %collective-permute-start.11 = (f32[8,32,128]{2,1,0:T(8,128)S(1)}, f32[8,32,128]{2,1,0:T(8,128)S(1)}, u32[]{:S(2)}, u32[]{:S(2)}) collective-permute-start(f32[8,32,128]{2,1,0:T(8,128)S(1)} %shard_map.84.after.first.own), channel_id=1, source_target_pairs={{0,16},{16,0},{1,17},{17,1},{2,18},{18,2},{3,19},{19,3},{4,20},{20... | collective-permute-start | bytes 393224 | tf_op jit(solution)/shard_map/ppermute | solution.py:691
  23.7 1.0 %shard_map.88 = (f32[128,128]{1,0:T(8,128)S(1)}, bf16[128,384]{1,0:T(8,128)(2,1)S(1)}, bf16[128,384]{1,0:T(8,128)(2,1)S(1)}, f32[384,128]{1,0:T(8,128)S(1)}) custom-call(f32[8,32,128]{2,1,0:T(8,128)S(1)} %shard_map.84.after.first.own, f32[8,48,128]{2,1,0:T(8,128)S(1)} %shard_map.85.after.second.own, f32[8,48,128]{2,1,0:T(8,128)S(1)} %shard_map.87.sides.own, ...), custom_call_target="tpu_custom_call" | custom-call | tf_op jit(solution)/shard_map/pallas_call | solution.py:43
  24.8 0.1 collective-permute-start.10
  24.9 1.2 %collective-permute-done.10 = f32[128,128]{1,0:T(8,128)S(1)} collective-permute-done((f32[128,128]{1,0:T(8,128)S(1)}, f32[128,128]{1,0:T(8,128)S(1)}, u32[]{:S(2)}, u32[]{:S(2)}) %collective-permute-start.10) | collective-permute-done | bytes 65568 | tf_op jit(solution)/shard_map/ppermute | solution.py:710
  26.1 5.6 %collective-permute-done.11.other = f32[8,32,128]{2,1,0:T(8,128)S(1)} collective-permute-done((f32[8,32,128]{2,1,0:T(8,128)S(1)}, f32[8,32,128]{2,1,0:T(8,128)S(1)}, u32[]{:S(2)}, u32[]{:S(2)}) %collective-permute-start.11) | collective-permute-done | bytes 131104 | tf_op jit(solution)/shard_map/ppermute | solution.py:691
  31.7 0.6 %shard_map.89 = (bf16[256,256]{1,0:T(8,128)(2,1)S(1)}, bf16[256,256]{1,0:T(8,128)(2,1)S(1)}, f32[8,128]{1,0:T(8,128)S(1)}, f32[136,128]{1,0:T(8,128)S(1)}) custom-call(f32[8,32,128]{2,1,0:T(8,128)S(1)} %shard_map.84.after.first.own, f32[8,32,128]{2,1,0:T(8,128)S(1)} %collective-permute-done.11.other, f32[128,16]{1,0:T(8,128)S(1)} %shard_map.82.after.weight, ...), custom_call_target="tpu_custom_call" | custom-call | tf_op jit(solution)/shard_map/pallas_call | solution.py:43
  32.3 0.0 collective-permute-done.9.other
  32.3 0.9 %shard_map.90 = (bf16[384,256]{1,0:T(8,128)(2,1)S(1)}, bf16[384,256]{1,0:T(8,128)(2,1)S(1)}, f32[8,128]{1,0:T(8,128)S(1)}, f32[136,128]{1,0:T(8,128)S(1)}) custom-call(f32[8,48,128]{2,1,0:T(8,128)S(1)} %shard_map.85.after.second.own, f32[8,48,128]{2,1,0:T(8,128)S(1)} %collective-permute-done.9.other, f32[128,16]{1,0:T(8,128)S(1)} %shard_map.82.after.weight, ...), custom_call_target="tpu_custom_call" | custom-call | tf_op jit(solution)/shard_map/pallas_call | solution.py:43
  33.2 0.0 collective-permute-done.8.other
  33.2 0.6 %shard_map.91.after = f32[136,128]{1,0:T(8,128)S(1)} custom-call(f32[8,48,128]{2,1,0:T(8,128)S(1)} %shard_map.87.sides.own, f32[8,48,128]{2,1,0:T(8,128)S(1)} %collective-permute-done.8.other, bf16[128,384]{1,0:T(8,128)(2,1)S(1)} %get-tuple-element.42.left, bf16[128,384]{1,0:T(8,128)(2,1)S(1)} %get-tuple-element.43.right, ...), custom_call_target="tpu_custom_call" | custom-call | tf_op jit(solution)/shard_map/pallas_call | solution.py:43
  33.8 0.1 collective-permute-start.12
  33.9 2.5 %collective-permute-start.14 = (f32[128,128]{1,0:T(8,128)S(1)}, f32[128,128]{1,0:T(8,128)S(1)}, u32[]{:S(2)}, u32[]{:S(2)}) collective-permute-start(f32[128,128]{1,0:T(8,128)S(1)} %add.10.after), channel_id=1, source_target_pairs={{0,2},{1,3},{2,0},{3,1},{4,6},{5,7},{6,4},{7,5},{8,10},{9,11},{10,... | collective-permute-start | bytes 196616 | tf_op jit(solution)/shard_map/ppermute | solution.py:710
  36.4 0.0 collective-permute-done.12
  36.4 1.2 %collective-permute-start.13 = (f32[136,128]{1,0:T(8,128)S(1)}, f32[136,128]{1,0:T(8,128)S(1)}, u32[]{:S(2)}, u32[]{:S(2)}) collective-permute-start(f32[136,128]{1,0:T(8,128)S(1)} %add.11.rest_0_), channel_id=1, source_target_pairs={{0,2},{1,3},{2,0},{3,1},{4,6},{5,7},{6,4},{7,5},{8,10},{9,11},{10,... | collective-permute-start | bytes 208904 | tf_op jit(solution)/shard_map/ppermute | solution.py:710
  37.7 1.4 %collective-permute-done.14 = f32[128,128]{1,0:T(8,128)S(1)} collective-permute-done((f32[128,128]{1,0:T(8,128)S(1)}, f32[128,128]{1,0:T(8,128)S(1)}, u32[]{:S(2)}, u32[]{:S(2)}) %collective-permute-start.14) | collective-permute-done | bytes 65568 | tf_op jit(solution)/shard_map/ppermute | solution.py:710
  39.1 1.6 %collective-permute-start.15 = (f32[128,128]{1,0:T(8,128)S(1)}, f32[128,128]{1,0:T(8,128)S(1)}, u32[]{:S(2)}, u32[]{:S(2)}) collective-permute-start(f32[128,128]{1,0:T(8,128)S(1)} %add.12.rest_2_), channel_id=1, source_target_pairs={{0,16},{16,0},{1,17},{17,1},{2,18},{18,2},{3,19},{19,3},{4,20},{20... | collective-permute-start | bytes 196616 | tf_op jit(solution)/shard_map/ppermute | solution.py:691
  40.7 0.2 shard_map.92
  40.9 2.6 %collective-permute-done.15.rest_3_ = f32[128,128]{1,0:T(8,128)S(1)} collective-permute-done((f32[128,128]{1,0:T(8,128)S(1)}, f32[128,128]{1,0:T(8,128)S(1)}, u32[]{:S(2)}, u32[]{:S(2)}) %collective-permute-start.15) | collective-permute-done | bytes 65568 | tf_op jit(solution)/shard_map/ppermute | solution.py:691
  43.5 0.0 collective-permute-done.13.rest_1_
  43.5 4.7 %shard_map.93 = f32[1024,128]{1,0:T(8,128)} custom-call(f32[136,128]{1,0:T(8,128)S(1)} %add.11.rest_0_, f32[136,128]{1,0:T(8,128)S(1)} %collective-permute-done.13.rest_1_, f32[128,128]{1,0:T(8,128)S(1)} %add.12.rest_2_, f32[128,128]{1,0:T(8,128)S(1)} %collective-permute-done.15.rest_3_, bf16[256,256]{1,0:T(8,128)(2,1)S(1)} %get-tuple-element.50.rest_4_, ...), custom_call_target="tpu_custom_call" | custom-call | tf_op jit(solution)/shard_map/pallas_call | solution.py:43
  (5 shorter events, 0.1 us)
Async XLA Ops:
  1.4 9.3 %copy-start.2 = (f32[1,1024]{1,0:T(1,128)S(1)}, f32[1,1024]{1,0:T(1,128)}, u32[]{:S(2)}) copy-start(f32[1,1024]{1,0:T(1,128)} %weights.1) | copy-start | bytes 12292
  1.4 12.8 %collective-permute-start = (f32[208,128]{1,0:T(8,128)S(1)}, f32[208,128]{1,0:T(8,128)S(1)}, u32[]{:S(2)}, u32[]{:S(2)}) collective-permute-start(f32[208,128]{1,0:T(8,128)S(1)} %get-tuple-element.34), channel_id=1, source_target_pairs={{4,8},{12,0},{8,4},{0,12},{5,9},{13,1},{9,5},{1,13},{6,10},{14,2},... | collective-permute-start | bytes 319496 | tf_op jit(solution)/shard_map/ppermute | solution.py:700
  6.5 3.2 %collective-permute-start.4 = (f32[40,128]{1,0:T(8,128)S(1)}, f32[40,128]{1,0:T(8,128)S(1)}, u32[]{:S(2)}, u32[]{:S(2)}) collective-permute-start(f32[40,128]{1,0:T(8,128)S(1)} %get-tuple-element.38), channel_id=1, source_target_pairs={{0,1},{1,2},{2,3},{3,0},{4,5},{5,6},{6,7},{7,4},{8,9},{9,10},{10,1... | collective-permute-start | bytes 61448 | tf_op jit(solution)/shard_map/ppermute | solution.py:691
  6.5 4.2 %copy-start.1 = (f32[1,1024]{1,0:T(1,128)S(1)}, f32[1,1024]{1,0:T(1,128)}, u32[]{:S(2)}) copy-start(f32[1,1024]{1,0:T(1,128)} %values.1) | copy-start | bytes 12292
  6.5 4.2 %copy-start = (s32[1,1024]{1,0:T(1,128)S(1)}, s32[1,1024]{1,0:T(1,128)}, u32[]{:S(2)}) copy-start(s32[1,1024]{1,0:T(1,128)} %cells.1) | copy-start | bytes 12292
  6.5 7.9 %collective-permute-start.1 = (f32[208,128]{1,0:T(8,128)S(1)}, f32[208,128]{1,0:T(8,128)S(1)}, u32[]{:S(2)}, u32[]{:S(2)}) collective-permute-start(f32[208,128]{1,0:T(8,128)S(1)} %get-tuple-element.35), channel_id=1, source_target_pairs={{0,4},{8,12},{4,0},{12,8},{1,5},{9,13},{5,1},{13,9},{2,6},{10,14},... | collective-permute-start | bytes 319496 | tf_op jit(solution)/shard_map/ppermute | solution.py:700
  6.5 4.6 %collective-permute-start.5 = (f32[40,128]{1,0:T(8,128)S(1)}, f32[40,128]{1,0:T(8,128)S(1)}, u32[]{:S(2)}, u32[]{:S(2)}) collective-permute-start(f32[40,128]{1,0:T(8,128)S(1)} %get-tuple-element.39), channel_id=1, source_target_pairs={{0,3},{1,0},{2,1},{3,2},{4,7},{5,4},{6,5},{7,6},{8,11},{9,8},{10,9... | collective-permute-start | bytes 61448 | tf_op jit(solution)/shard_map/ppermute | solution.py:691
  8.3 7.5 %collective-permute-start.2 = (f32[192,128]{1,0:T(8,128)S(1)}, f32[192,128]{1,0:T(8,128)S(1)}, u32[]{:S(2)}, u32[]{:S(2)}) collective-permute-start(f32[192,128]{1,0:T(8,128)S(1)} %get-tuple-element.36), channel_id=1, source_target_pairs={{4,8},{12,0},{8,4},{0,12},{5,9},{13,1},{9,5},{1,13},{6,10},{14,2},... | collective-permute-start | bytes 294920 | tf_op jit(solution)/shard_map/ppermute | solution.py:700
  9.7 8.3 %collective-permute-start.3 = (f32[192,128]{1,0:T(8,128)S(1)}, f32[192,128]{1,0:T(8,128)S(1)}, u32[]{:S(2)}, u32[]{:S(2)}) collective-permute-start(f32[192,128]{1,0:T(8,128)S(1)} %get-tuple-element.37), channel_id=1, source_target_pairs={{0,4},{8,12},{4,0},{12,8},{1,5},{9,13},{5,1},{13,9},{2,6},{10,14},... | collective-permute-start | bytes 294920 | tf_op jit(solution)/shard_map/ppermute | solution.py:700
  11.1 9.4 %collective-permute-start.6 = (f32[168,128]{1,0:T(8,128)S(1)}, f32[168,128]{1,0:T(8,128)S(1)}, u32[]{:S(2)}, u32[]{:S(2)}) collective-permute-start(f32[168,128]{1,0:T(8,128)S(1)} %get-tuple-element.40), channel_id=1, source_target_pairs={{4,8},{12,0},{8,4},{0,12},{5,9},{13,1},{9,5},{1,13},{6,10},{14,2},... | collective-permute-start | bytes 258056 | tf_op jit(solution)/shard_map/ppermute | solution.py:700
  14.1 6.4 %collective-permute-start.7 = (f32[168,128]{1,0:T(8,128)S(1)}, f32[168,128]{1,0:T(8,128)S(1)}, u32[]{:S(2)}, u32[]{:S(2)}) collective-permute-start(f32[168,128]{1,0:T(8,128)S(1)} %get-tuple-element.41), channel_id=1, source_target_pairs={{0,4},{8,12},{4,0},{12,8},{1,5},{9,13},{5,1},{13,9},{2,6},{10,14},... | collective-permute-start | bytes 258056 | tf_op jit(solution)/shard_map/ppermute | solution.py:700
  18.9 13.4 %collective-permute-start.9 = (f32[8,48,128]{2,1,0:T(8,128)S(1)}, f32[8,48,128]{2,1,0:T(8,128)S(1)}, u32[]{:S(2)}, u32[]{:S(2)}) collective-permute-start(f32[8,48,128]{2,1,0:T(8,128)S(1)} %shard_map.85.after.second.own), channel_id=1, source_target_pairs={{0,16},{16,0},{1,17},{17,1},{2,18},{18,2},{3,19},{19,3},{4,20},{20... | collective-permute-start | bytes 589832 | tf_op jit(solution)/shard_map/ppermute | solution.py:691
  21.7 11.5 %collective-permute-start.8 = (f32[8,48,128]{2,1,0:T(8,128)S(1)}, f32[8,48,128]{2,1,0:T(8,128)S(1)}, u32[]{:S(2)}, u32[]{:S(2)}) collective-permute-start(f32[8,48,128]{2,1,0:T(8,128)S(1)} %shard_map.87.sides.own), channel_id=1, source_target_pairs={{0,16},{16,0},{1,17},{17,1},{2,18},{18,2},{3,19},{19,3},{4,20},{20... | collective-permute-start | bytes 589832 | tf_op jit(solution)/shard_map/ppermute | solution.py:691
  23.0 8.7 %collective-permute-start.11 = (f32[8,32,128]{2,1,0:T(8,128)S(1)}, f32[8,32,128]{2,1,0:T(8,128)S(1)}, u32[]{:S(2)}, u32[]{:S(2)}) collective-permute-start(f32[8,32,128]{2,1,0:T(8,128)S(1)} %shard_map.84.after.first.own), channel_id=1, source_target_pairs={{0,16},{16,0},{1,17},{17,1},{2,18},{18,2},{3,19},{19,3},{4,20},{20... | collective-permute-start | bytes 393224 | tf_op jit(solution)/shard_map/ppermute | solution.py:691
  24.8 1.3 %collective-permute-start.10 = (f32[128,128]{1,0:T(8,128)S(1)}, f32[128,128]{1,0:T(8,128)S(1)}, u32[]{:S(2)}, u32[]{:S(2)}) collective-permute-start(f32[128,128]{1,0:T(8,128)S(1)} %get-tuple-element.45), channel_id=1, source_target_pairs={{0,1},{1,0},{2,3},{3,2},{4,5},{5,4},{6,7},{7,6},{8,9},{9,8},{10,11... | collective-permute-start | bytes 196616 | tf_op jit(solution)/shard_map/ppermute | solution.py:710
  33.8 2.6 %collective-permute-start.12 = (f32[136,128]{1,0:T(8,128)S(1)}, f32[136,128]{1,0:T(8,128)S(1)}, u32[]{:S(2)}, u32[]{:S(2)}) collective-permute-start(f32[136,128]{1,0:T(8,128)S(1)} %shard_map.91.after), channel_id=1, source_target_pairs={{0,1},{1,0},{2,3},{3,2},{4,5},{5,4},{6,7},{7,6},{8,9},{9,8},{10,11... | collective-permute-start | bytes 208904 | tf_op jit(solution)/shard_map/ppermute | solution.py:710
  33.9 5.2 %collective-permute-start.14 = (f32[128,128]{1,0:T(8,128)S(1)}, f32[128,128]{1,0:T(8,128)S(1)}, u32[]{:S(2)}, u32[]{:S(2)}) collective-permute-start(f32[128,128]{1,0:T(8,128)S(1)} %add.10.after), channel_id=1, source_target_pairs={{0,2},{1,3},{2,0},{3,1},{4,6},{5,7},{6,4},{7,5},{8,10},{9,11},{10,... | collective-permute-start | bytes 196616 | tf_op jit(solution)/shard_map/ppermute | solution.py:710
  36.4 7.0 %collective-permute-start.13 = (f32[136,128]{1,0:T(8,128)S(1)}, f32[136,128]{1,0:T(8,128)S(1)}, u32[]{:S(2)}, u32[]{:S(2)}) collective-permute-start(f32[136,128]{1,0:T(8,128)S(1)} %add.11.rest_0_), channel_id=1, source_target_pairs={{0,2},{1,3},{2,0},{3,1},{4,6},{5,7},{6,4},{7,5},{8,10},{9,11},{10,... | collective-permute-start | bytes 208904 | tf_op jit(solution)/shard_map/ppermute | solution.py:710
  39.1 4.3 %collective-permute-start.15 = (f32[128,128]{1,0:T(8,128)S(1)}, f32[128,128]{1,0:T(8,128)S(1)}, u32[]{:S(2)}, u32[]{:S(2)}) collective-permute-start(f32[128,128]{1,0:T(8,128)S(1)} %add.12.rest_2_), channel_id=1, source_target_pairs={{0,16},{16,0},{1,17},{17,1},{2,18},{18,2},{3,19},{19,3},{4,20},{20... | collective-permute-start | bytes 196616 | tf_op jit(solution)/shard_map/ppermute | solution.py:691

commit v5 on v4

--- a/solution.py
+++ b/solution.py
@@ -83,7 +83,7 @@
 
 
 def parted(cols):
-    return cols * 3 // 8 // 8 * 8, cols * 3 // 4 // 8 * 8
+    return cols * 7 // 16 // 8 * 8, cols * 13 // 16 // 8 * 8
 
 
 def parity(axis):
@@ -465,8 +465,8 @@
             if own is sides:
                 at = pl.ds(b * depth, depth)
                 left[:, at], right[:, at] = turned
-                lane = lax.broadcasted_iota(jnp.int32, (depth, local), 1)
-                spread[at] = jnp.where(lane == 0, plain, jnp.where(lane == 1, valued, mean))
+                for i, column in enumerate((plain, valued, mean)):
+                    spread[i, at] = jnp.broadcast_to(column, (depth, local))
 
         loop(rows // many, block)
 
@@ -526,7 +526,7 @@
     def block(b):
         at = pl.ds(b * depth, depth)
         value, partner = cells_of(own, b, many), cells_of(other, b, many)
-        counter = tally(total, local, value, partner, *(spread[at, i : i + 1] for i in range(3)))
+        counter = tally(total, local, value, partner, *(spread[i, at] for i in range(3)))
         total[pl.ds(0, local)] += dot_wide(
             (left[:, at], right[:, at]), wide(halves(counter)), local
         )
@@ -843,7 +843,7 @@
         half = struct(local, sided, kind=jnp.bfloat16)
         alone, left_half, right_half, spread = call(
             functools.partial(own_gram_kernel, layout),
-            (struct(local, local), half, half, struct(sided, local)),
+            (struct(local, local), half, half, struct(3, sided, local)),
             *owns,
             weight,
         )

time: 48.3 us -> 46.6 us (0.965)
  starting transfers between devices: 20.3 us -> 18.8 us
  waiting for transfers between devices: 14.6 us -> 13.7 us
  local copies, waits for them, and re-layouts: 0.01 us -> 0.68 us
    ppermute x6, starting transfers between devices: 7 us -> 5.27 us  [shift(): return lax.ppermute(value, axes if len(axes) > 1 else axes[0], pairs)]
    ppermute x6, waiting for transfers between devices: 2.97 us -> 1.6 us  [trade(): return lax.ppermute(value, axis, pairs + [(j, i) for i, j in pairs])]
    ppermute x6, starting transfers between devices: 9.33 us -> 10.2 us  [trade(): return lax.ppermute(value, axis, pairs + [(j, i) for i, j in pairs])]
    unnamed x6 -> x10, local copies, waits for them, and re-layouts: 0.01 us -> 0.68 us
    ppermute x4, starting transfers between devices: 3.92 us -> 3.41 us  [role_sums(): other = lax.ppermute(value, 'role', [(i, i ^ step) for i in range(size)])]
  transfers between devices with their start and end apart: 16 -> 16, of which waited for: 7 -> 8; matrix products, arithmetic and copies ran while one was open for 0% -> 0% of each run, Pallas kernels for 12% -> 13%
where the time goes in v5:
time: 46.6 us; the launch traced here: 46.4 us
  starting transfers between devices  18.8 us (40%)
  waiting for transfers between devices  13.7 us (29%)
  Pallas kernels  12.4 us (27%)
  between operations  0.81 us (2%)
  local copies, waits for them, and re-layouts  0.68 us (1%)
    pallas_call x12, Pallas kernels, call(): pl.pallas_call(body, out_shape=outs, in_specs=[SMEM] * scalars + [VMEM] *...  12.4 us
    ppermute x6, starting transfers between devices, trade(): return lax.ppermute(value, axis, pairs + [(j, i) for i, j in pairs])  10.2 us
    ppermute x6, waiting for transfers between devices, shift(): return lax.ppermute(value, axes if len(axes) > 1 else axes[0], pairs)  9.39 us
    ppermute x6, starting transfers between devices, shift(): return lax.ppermute(value, axes if len(axes) > 1 else axes[0], pairs)  5.27 us
    ppermute x4, starting transfers between devices, role_sums(): other = lax.ppermute(value, 'role', [(i, i ^ step) for i in range(size)])  3.41 us
    ppermute x4, waiting for transfers between devices, role_sums(): other = lax.ppermute(value, 'role', [(i, i ^ step) for i in range(size)])  2.7 us
    ppermute x6, waiting for transfers between devices, trade(): return lax.ppermute(value, axis, pairs + [(j, i) for i, j in pairs])  1.6 us
  transfers between devices with their start and end apart: 16, of which 8 were waited for; matrix products, arithmetic and copies ran while one was open for 0% of the time, Pallas kernels for 13%

profile of v5, /device:TPU:0, one launch (start us, length us, event | category | flops | bytes accessed | tf_op | source)
XLA Modules:
  0.0 46.4 jit_solution(8769165031179284463)
XLA Ops:
  0.0 1.3 %shard_map.83 = (f32[8,128,128]{2,1,0:T(8,128)S(1)}, f32[3,8,128]{2,1,0:T(8,128)S(1)}, f32[240,128]{1,0:T(8,128)S(1)}, f32[240,128]{1,0:T(8,128)S(1)}, f32[192,1...) custom-call(f32[1024,128]{1,0:T(8,128)} %bitcast.2, ...), custom_call_target="tpu_custom_call" | custom-call | tf_op jit(solution)/shard_map/pallas_call | solution.py:43
  1.3 0.0 copy-start.4
  1.4 5.1 %collective-permute-start = (f32[240,128]{1,0:T(8,128)S(1)}, f32[240,128]{1,0:T(8,128)S(1)}, u32[]{:S(2)}, u32[]{:S(2)}) collective-permute-start(f32[240,128]{1,0:T(8,128)S(1)} %get-tuple-element.34), channel_id=1, source_target_pairs={{4,8},{12,0},{8,4},{0,12},{5,9},{13,1},{9,5},{1,13},{6,10},{14,2},... | collective-permute-start | bytes 368648 | tf_op jit(solution)/shard_map/ppermute | solution.py:700
  6.5 0.0 collective-permute-start.1
  6.5 0.9 %collective-permute-start.2 = (f32[192,128]{1,0:T(8,128)S(1)}, f32[192,128]{1,0:T(8,128)S(1)}, u32[]{:S(2)}, u32[]{:S(2)}) collective-permute-start(f32[192,128]{1,0:T(8,128)S(1)} %get-tuple-element.36), channel_id=1, source_target_pairs={{4,8},{12,0},{8,4},{0,12},{5,9},{13,1},{9,5},{1,13},{6,10},{14,2},... | collective-permute-start | bytes 294920 | tf_op jit(solution)/shard_map/ppermute | solution.py:700
  7.4 1.1 %collective-permute-start.3 = (f32[192,128]{1,0:T(8,128)S(1)}, f32[192,128]{1,0:T(8,128)S(1)}, u32[]{:S(2)}, u32[]{:S(2)}) collective-permute-start(f32[192,128]{1,0:T(8,128)S(1)} %get-tuple-element.37), channel_id=1, source_target_pairs={{0,4},{8,12},{4,0},{12,8},{1,5},{9,13},{5,1},{13,9},{2,6},{10,14},... | collective-permute-start | bytes 294920 | tf_op jit(solution)/shard_map/ppermute | solution.py:700
  8.5 0.0 collective-permute-start.4
  8.5 3.2 %collective-permute-done.4.left = f32[40,128]{1,0:T(8,128)S(1)} collective-permute-done((f32[40,128]{1,0:T(8,128)S(1)}, f32[40,128]{1,0:T(8,128)S(1)}, u32[]{:S(2)}, u32[]{:S(2)}) %collective-permute-start.4) | collective-permute-done | bytes 20512 | tf_op jit(solution)/shard_map/ppermute | solution.py:691
  11.7 0.0 collective-permute-start.5
  12.4 0.0 copy-done.4
  12.4 0.4 shard_map.82.after.weight
  12.8 0.4 collective-permute-done.5.right
  13.2 3.0 %collective-permute-start.6 = (f32[136,128]{1,0:T(8,128)S(1)}, f32[136,128]{1,0:T(8,128)S(1)}, u32[]{:S(2)}, u32[]{:S(2)}) collective-permute-start(f32[136,128]{1,0:T(8,128)S(1)} %get-tuple-element.40), channel_id=1, source_target_pairs={{4,8},{12,0},{8,4},{0,12},{5,9},{13,1},{9,5},{1,13},{6,10},{14,2},... | collective-permute-start | bytes 208904 | tf_op jit(solution)/shard_map/ppermute | solution.py:700
  16.2 0.0 collective-permute-done.refs_0_.early
  16.2 0.0 collective-permute-start.7
  16.2 0.0 collective-permute-done.1.refs_1_.late
  16.2 0.8 %shard_map.84.after.first.own = f32[8,40,128]{2,1,0:T(8,128)S(1)} custom-call(f32[128,16]{1,0:T(8,128)S(1)} %shard_map.82.after.weight, f32[8,128,128]{2,1,0:T(8,128)S(1)} %get-tuple-element.32.field, f32[3,8,128]{2,1,0:T(8,128)S(1)} %get-tuple-element.33.kept, f32[240,128]{1,0:T(8,128)S(1)} %collective-permute-done.refs_0_.early, ...), custom_call_target="tpu_custom_call" | custom-call | tf_op jit(solution)/shard_map/pallas_call | solution.py:43
  17.0 0.0 collective-permute-done.2.refs_2_.early_next
  17.0 0.0 collective-permute-done.3.refs_3_.late_next
  17.0 0.9 %shard_map.85.after.second.own = f32[8,48,128]{2,1,0:T(8,128)S(1)} custom-call(f32[8,40,128]{2,1,0:T(8,128)S(1)} %shard_map.84.after.first.own, f32[8,128,128]{2,1,0:T(8,128)S(1)} %get-tuple-element.32.field, f32[3,8,128]{2,1,0:T(8,128)S(1)} %get-tuple-element.33.kept, f32[240,128]{1,0:T(8,128)S(1)} %collective-permute-done.refs_0_.early, ...), custom_call_target="tpu_custom_call" | custom-call | tf_op jit(solution)/shard_map/pallas_call | solution.py:43
  17.9 1.6 %collective-permute-start.9 = (f32[8,48,128]{2,1,0:T(8,128)S(1)}, f32[8,48,128]{2,1,0:T(8,128)S(1)}, u32[]{:S(2)}, u32[]{:S(2)}) collective-permute-start(f32[8,48,128]{2,1,0:T(8,128)S(1)} %shard_map.85.after.second.own), channel_id=1, source_target_pairs={{0,16},{16,0},{1,17},{17,1},{2,18},{18,2},{3,19},{19,3},{4,20},{20... | collective-permute-start | bytes 589832 | tf_op jit(solution)/shard_map/ppermute | solution.py:691
  19.5 0.5 %collective-permute-start.11 = (f32[8,40,128]{2,1,0:T(8,128)S(1)}, f32[8,40,128]{2,1,0:T(8,128)S(1)}, u32[]{:S(2)}, u32[]{:S(2)}) collective-permute-start(f32[8,40,128]{2,1,0:T(8,128)S(1)} %shard_map.84.after.first.own), channel_id=1, source_target_pairs={{0,16},{16,0},{1,17},{17,1},{2,18},{18,2},{3,19},{19,3},{4,20},{20... | collective-permute-start | bytes 491528 | tf_op jit(solution)/shard_map/ppermute | solution.py:691
  20.0 0.0 collective-permute-done.6.early_rest
  20.0 1.6 %collective-permute-done.7.late_rest = f32[136,128]{1,0:T(8,128)S(1)} collective-permute-done((f32[136,128]{1,0:T(8,128)S(1)}, f32[136,128]{1,0:T(8,128)S(1)}, u32[]{:S(2)}, u32[]{:S(2)}) %collective-permute-start.7) | collective-permute-done | bytes 69664 | tf_op jit(solution)/shard_map/ppermute | solution.py:700
  21.6 1.1 %shard_map.87.sides.own = f32[8,40,128]{2,1,0:T(8,128)S(1)} custom-call(f32[8,48,128]{2,1,0:T(8,128)S(1)} %shard_map.85.after.second.own, f32[8,128,128]{2,1,0:T(8,128)S(1)} %get-tuple-element.32.field, f32[3,8,128]{2,1,0:T(8,128)S(1)} %get-tuple-element.33.kept, f32[240,128]{1,0:T(8,128)S(1)} %collective-permute-done.refs_0_.early, ...), custom_call_target="tpu_custom_call" | custom-call | tf_op jit(solution)/shard_map/pallas_call | solution.py:43
  22.7 1.6 %collective-permute-start.8 = (f32[8,40,128]{2,1,0:T(8,128)S(1)}, f32[8,40,128]{2,1,0:T(8,128)S(1)}, u32[]{:S(2)}, u32[]{:S(2)}) collective-permute-start(f32[8,40,128]{2,1,0:T(8,128)S(1)} %shard_map.87.sides.own), channel_id=1, source_target_pairs={{0,16},{16,0},{1,17},{17,1},{2,18},{18,2},{3,19},{19,3},{4,20},{20... | collective-permute-start | bytes 491528 | tf_op jit(solution)/shard_map/ppermute | solution.py:691
  24.3 1.1 %shard_map.88 = (f32[128,128]{1,0:T(8,128)S(1)}, bf16[128,320]{1,0:T(8,128)(2,1)S(1)}, bf16[128,320]{1,0:T(8,128)(2,1)S(1)}, f32[3,320,128]{2,1,0:T(8,128)S(1)}) custom-call(f32[8,40,128]{2,1,0:T(8,128)S(1)} %shard_map.84.after.first.own, f32[8,48,128]{2,1,0:T(8,128)S(1)} %shard_map.85.after.second.own, f32[8,40,128]{2,1,0:T(8,128)S(1)} %shard_map.87.sides.own, ...), custom_call_target="tpu_custom_call" | custom-call | tf_op jit(solution)/shard_map/pallas_call | solution.py:43
  25.4 0.2 collective-permute-start.10
  25.6 1.1 %collective-permute-done.10 = f32[128,128]{1,0:T(8,128)S(1)} collective-permute-done((f32[128,128]{1,0:T(8,128)S(1)}, f32[128,128]{1,0:T(8,128)S(1)}, u32[]{:S(2)}, u32[]{:S(2)}) %collective-permute-start.10) | collective-permute-done | bytes 65568 | tf_op jit(solution)/shard_map/ppermute | solution.py:710
  26.7 2.0 %collective-permute-done.11.other = f32[8,40,128]{2,1,0:T(8,128)S(1)} collective-permute-done((f32[8,40,128]{2,1,0:T(8,128)S(1)}, f32[8,40,128]{2,1,0:T(8,128)S(1)}, u32[]{:S(2)}, u32[]{:S(2)}) %collective-permute-start.11) | collective-permute-done | bytes 163872 | tf_op jit(solution)/shard_map/ppermute | solution.py:691
  28.7 0.7 %shard_map.89 = (bf16[320,256]{1,0:T(8,128)(2,1)S(1)}, bf16[320,256]{1,0:T(8,128)(2,1)S(1)}, f32[8,128]{1,0:T(8,128)S(1)}, f32[136,128]{1,0:T(8,128)S(1)}) custom-call(f32[8,40,128]{2,1,0:T(8,128)S(1)} %shard_map.84.after.first.own, f32[8,40,128]{2,1,0:T(8,128)S(1)} %collective-permute-done.11.other, f32[128,16]{1,0:T(8,128)S(1)} %shard_map.82.after.weight, ...), custom_call_target="tpu_custom_call" | custom-call | tf_op jit(solution)/shard_map/pallas_call | solution.py:43
  29.4 0.0 copy-start
  29.4 0.7 %copy-done = bf16[320,256]{1,0:T(8,128)(2,1)} copy-done((bf16[320,256]{1,0:T(8,128)(2,1)}, bf16[320,256]{1,0:T(8,128)(2,1)S(1)}, u32[]{:S(2)}) %copy-start) | copy-done | bytes 163864
  30.1 0.0 collective-permute-done.9.other
  30.1 0.9 %shard_map.90 = (bf16[384,256]{1,0:T(8,128)(2,1)S(1)}, bf16[384,256]{1,0:T(8,128)(2,1)S(1)}, f32[8,128]{1,0:T(8,128)S(1)}, f32[136,128]{1,0:T(8,128)S(1)}) custom-call(f32[8,48,128]{2,1,0:T(8,128)S(1)} %shard_map.85.after.second.own, f32[8,48,128]{2,1,0:T(8,128)S(1)} %collective-permute-done.9.other, f32[128,16]{1,0:T(8,128)S(1)} %shard_map.82.after.weight, ...), custom_call_target="tpu_custom_call" | custom-call | tf_op jit(solution)/shard_map/pallas_call | solution.py:43
  30.9 1.2 %collective-permute-done.8.other = f32[8,40,128]{2,1,0:T(8,128)S(1)} collective-permute-done((f32[8,40,128]{2,1,0:T(8,128)S(1)}, f32[8,40,128]{2,1,0:T(8,128)S(1)}, u32[]{:S(2)}, u32[]{:S(2)}) %collective-permute-start.8) | collective-permute-done | bytes 163872 | tf_op jit(solution)/shard_map/ppermute | solution.py:691
  32.2 0.4 shard_map.91.after
  32.6 0.5 %collective-permute-start.12 = (f32[136,128]{1,0:T(8,128)S(1)}, f32[136,128]{1,0:T(8,128)S(1)}, u32[]{:S(2)}, u32[]{:S(2)}) collective-permute-start(f32[136,128]{1,0:T(8,128)S(1)} %shard_map.91.after), channel_id=1, source_target_pairs={{0,1},{1,0},{2,3},{3,2},{4,5},{5,4},{6,7},{7,6},{8,9},{9,8},{10,11... | collective-permute-start | bytes 208904 | tf_op jit(solution)/shard_map/ppermute | solution.py:710
  33.1 1.4 %collective-permute-start.14 = (f32[128,128]{1,0:T(8,128)S(1)}, f32[128,128]{1,0:T(8,128)S(1)}, u32[]{:S(2)}, u32[]{:S(2)}) collective-permute-start(f32[128,128]{1,0:T(8,128)S(1)} %add.10.after), channel_id=1, source_target_pairs={{0,2},{1,3},{2,0},{3,1},{4,6},{5,7},{6,4},{7,5},{8,10},{9,11},{10,... | collective-permute-start | bytes 196616 | tf_op jit(solution)/shard_map/ppermute | solution.py:710
  34.5 0.0 collective-permute-done.12
  34.5 1.2 %collective-permute-start.13 = (f32[136,128]{1,0:T(8,128)S(1)}, f32[136,128]{1,0:T(8,128)S(1)}, u32[]{:S(2)}, u32[]{:S(2)}) collective-permute-start(f32[136,128]{1,0:T(8,128)S(1)} %add.11.rest_0_), channel_id=1, source_target_pairs={{0,2},{1,3},{2,0},{3,1},{4,6},{5,7},{6,4},{7,5},{8,10},{9,11},{10,... | collective-permute-start | bytes 208904 | tf_op jit(solution)/shard_map/ppermute | solution.py:710
  35.8 1.6 %collective-permute-done.14 = f32[128,128]{1,0:T(8,128)S(1)} collective-permute-done((f32[128,128]{1,0:T(8,128)S(1)}, f32[128,128]{1,0:T(8,128)S(1)}, u32[]{:S(2)}, u32[]{:S(2)}) %collective-permute-start.14) | collective-permute-done | bytes 65568 | tf_op jit(solution)/shard_map/ppermute | solution.py:710
  37.4 0.0 copy-start.1
  37.4 1.6 %collective-permute-start.15 = (f32[128,128]{1,0:T(8,128)S(1)}, f32[128,128]{1,0:T(8,128)S(1)}, u32[]{:S(2)}, u32[]{:S(2)}) collective-permute-start(f32[128,128]{1,0:T(8,128)S(1)} %add.12.rest_2_), channel_id=1, source_target_pairs={{0,16},{16,0},{1,17},{17,1},{2,18},{18,2},{3,19},{19,3},{4,20},{20... | collective-permute-start | bytes 196616 | tf_op jit(solution)/shard_map/ppermute | solution.py:691
  39.0 0.2 shard_map.92
  39.1 2.6 %collective-permute-done.15.rest_3_ = f32[128,128]{1,0:T(8,128)S(1)} collective-permute-done((f32[128,128]{1,0:T(8,128)S(1)}, f32[128,128]{1,0:T(8,128)S(1)}, u32[]{:S(2)}, u32[]{:S(2)}) %collective-permute-start.15) | collective-permute-done | bytes 65568 | tf_op jit(solution)/shard_map/ppermute | solution.py:691
  41.7 0.0 collective-permute-done.13.rest_1_
  41.7 4.7 %shard_map.93 = f32[1024,128]{1,0:T(8,128)} custom-call(f32[136,128]{1,0:T(8,128)S(1)} %add.11.rest_0_, f32[136,128]{1,0:T(8,128)S(1)} %collective-permute-done.13.rest_1_, f32[128,128]{1,0:T(8,128)S(1)} %add.12.rest_2_, f32[128,128]{1,0:T(8,128)S(1)} %collective-permute-done.15.rest_3_, bf16[320,256]{1,0:T(8,128)(2,1)S(1)} %get-tuple-element.50.rest_4_, ...), custom_call_target="tpu_custom_call" | custom-call | tf_op jit(solution)/shard_map/pallas_call | solution.py:43
  (9 shorter events, 0.0 us)
Async XLA Ops:
  1.3 11.1 %copy-start.4 = (f32[1,1024]{1,0:T(1,128)S(1)}, f32[1,1024]{1,0:T(1,128)}, u32[]{:S(2)}) copy-start(f32[1,1024]{1,0:T(1,128)} %weights.1) | copy-start | bytes 12292
  1.4 14.9 %collective-permute-start = (f32[240,128]{1,0:T(8,128)S(1)}, f32[240,128]{1,0:T(8,128)S(1)}, u32[]{:S(2)}, u32[]{:S(2)}) collective-permute-start(f32[240,128]{1,0:T(8,128)S(1)} %get-tuple-element.34), channel_id=1, source_target_pairs={{4,8},{12,0},{8,4},{0,12},{5,9},{13,1},{9,5},{1,13},{6,10},{14,2},... | collective-permute-start | bytes 368648 | tf_op jit(solution)/shard_map/ppermute | solution.py:700
  6.5 9.7 %collective-permute-start.1 = (f32[240,128]{1,0:T(8,128)S(1)}, f32[240,128]{1,0:T(8,128)S(1)}, u32[]{:S(2)}, u32[]{:S(2)}) collective-permute-start(f32[240,128]{1,0:T(8,128)S(1)} %get-tuple-element.35), channel_id=1, source_target_pairs={{0,4},{8,12},{4,0},{12,8},{1,5},{9,13},{5,1},{13,9},{2,6},{10,14},... | collective-permute-start | bytes 368648 | tf_op jit(solution)/shard_map/ppermute | solution.py:700
  6.5 5.9 %copy-start.3 = (f32[1,1024]{1,0:T(1,128)S(1)}, f32[1,1024]{1,0:T(1,128)}, u32[]{:S(2)}) copy-start(f32[1,1024]{1,0:T(1,128)} %values.1) | copy-start | bytes 12292
  6.5 5.9 %copy-start.2 = (s32[1,1024]{1,0:T(1,128)S(1)}, s32[1,1024]{1,0:T(1,128)}, u32[]{:S(2)}) copy-start(s32[1,1024]{1,0:T(1,128)} %cells.1) | copy-start | bytes 12292
  6.5 10.5 %collective-permute-start.2 = (f32[192,128]{1,0:T(8,128)S(1)}, f32[192,128]{1,0:T(8,128)S(1)}, u32[]{:S(2)}, u32[]{:S(2)}) collective-permute-start(f32[192,128]{1,0:T(8,128)S(1)} %get-tuple-element.36), channel_id=1, source_target_pairs={{4,8},{12,0},{8,4},{0,12},{5,9},{13,1},{9,5},{1,13},{6,10},{14,2},... | collective-permute-start | bytes 294920 | tf_op jit(solution)/shard_map/ppermute | solution.py:700
  7.4 9.6 %collective-permute-start.3 = (f32[192,128]{1,0:T(8,128)S(1)}, f32[192,128]{1,0:T(8,128)S(1)}, u32[]{:S(2)}, u32[]{:S(2)}) collective-permute-start(f32[192,128]{1,0:T(8,128)S(1)} %get-tuple-element.37), channel_id=1, source_target_pairs={{0,4},{8,12},{4,0},{12,8},{1,5},{9,13},{5,1},{13,9},{2,6},{10,14},... | collective-permute-start | bytes 294920 | tf_op jit(solution)/shard_map/ppermute | solution.py:700
  8.5 3.2 %collective-permute-start.4 = (f32[40,128]{1,0:T(8,128)S(1)}, f32[40,128]{1,0:T(8,128)S(1)}, u32[]{:S(2)}, u32[]{:S(2)}) collective-permute-start(f32[40,128]{1,0:T(8,128)S(1)} %get-tuple-element.38), channel_id=1, source_target_pairs={{0,1},{1,2},{2,3},{3,0},{4,5},{5,6},{6,7},{7,4},{8,9},{9,10},{10,1... | collective-permute-start | bytes 61448 | tf_op jit(solution)/shard_map/ppermute | solution.py:691
  11.7 1.5 %collective-permute-start.5 = (f32[40,128]{1,0:T(8,128)S(1)}, f32[40,128]{1,0:T(8,128)S(1)}, u32[]{:S(2)}, u32[]{:S(2)}) collective-permute-start(f32[40,128]{1,0:T(8,128)S(1)} %get-tuple-element.39), channel_id=1, source_target_pairs={{0,3},{1,0},{2,1},{3,2},{4,7},{5,4},{6,5},{7,6},{8,11},{9,8},{10,9... | collective-permute-start | bytes 61448 | tf_op jit(solution)/shard_map/ppermute | solution.py:691
  13.2 6.8 %collective-permute-start.6 = (f32[136,128]{1,0:T(8,128)S(1)}, f32[136,128]{1,0:T(8,128)S(1)}, u32[]{:S(2)}, u32[]{:S(2)}) collective-permute-start(f32[136,128]{1,0:T(8,128)S(1)} %get-tuple-element.40), channel_id=1, source_target_pairs={{4,8},{12,0},{8,4},{0,12},{5,9},{13,1},{9,5},{1,13},{6,10},{14,2},... | collective-permute-start | bytes 208904 | tf_op jit(solution)/shard_map/ppermute | solution.py:700
  16.2 5.4 %collective-permute-start.7 = (f32[136,128]{1,0:T(8,128)S(1)}, f32[136,128]{1,0:T(8,128)S(1)}, u32[]{:S(2)}, u32[]{:S(2)}) collective-permute-start(f32[136,128]{1,0:T(8,128)S(1)} %get-tuple-element.41), channel_id=1, source_target_pairs={{0,4},{8,12},{4,0},{12,8},{1,5},{9,13},{5,1},{13,9},{2,6},{10,14},... | collective-permute-start | bytes 208904 | tf_op jit(solution)/shard_map/ppermute | solution.py:700
  17.9 12.1 %collective-permute-start.9 = (f32[8,48,128]{2,1,0:T(8,128)S(1)}, f32[8,48,128]{2,1,0:T(8,128)S(1)}, u32[]{:S(2)}, u32[]{:S(2)}) collective-permute-start(f32[8,48,128]{2,1,0:T(8,128)S(1)} %shard_map.85.after.second.own), channel_id=1, source_target_pairs={{0,16},{16,0},{1,17},{17,1},{2,18},{18,2},{3,19},{19,3},{4,20},{20... | collective-permute-start | bytes 589832 | tf_op jit(solution)/shard_map/ppermute | solution.py:691
  19.5 9.1 %collective-permute-start.11 = (f32[8,40,128]{2,1,0:T(8,128)S(1)}, f32[8,40,128]{2,1,0:T(8,128)S(1)}, u32[]{:S(2)}, u32[]{:S(2)}) collective-permute-start(f32[8,40,128]{2,1,0:T(8,128)S(1)} %shard_map.84.after.first.own), channel_id=1, source_target_pairs={{0,16},{16,0},{1,17},{17,1},{2,18},{18,2},{3,19},{19,3},{4,20},{20... | collective-permute-start | bytes 491528 | tf_op jit(solution)/shard_map/ppermute | solution.py:691
  22.7 9.5 %collective-permute-start.8 = (f32[8,40,128]{2,1,0:T(8,128)S(1)}, f32[8,40,128]{2,1,0:T(8,128)S(1)}, u32[]{:S(2)}, u32[]{:S(2)}) collective-permute-start(f32[8,40,128]{2,1,0:T(8,128)S(1)} %shard_map.87.sides.own), channel_id=1, source_target_pairs={{0,16},{16,0},{1,17},{17,1},{2,18},{18,2},{3,19},{19,3},{4,20},{20... | collective-permute-start | bytes 491528 | tf_op jit(solution)/shard_map/ppermute | solution.py:691
  25.4 1.3 %collective-permute-start.10 = (f32[128,128]{1,0:T(8,128)S(1)}, f32[128,128]{1,0:T(8,128)S(1)}, u32[]{:S(2)}, u32[]{:S(2)}) collective-permute-start(f32[128,128]{1,0:T(8,128)S(1)} %get-tuple-element.45), channel_id=1, source_target_pairs={{0,1},{1,0},{2,3},{3,2},{4,5},{5,4},{6,7},{7,6},{8,9},{9,8},{10,11... | collective-permute-start | bytes 196616 | tf_op jit(solution)/shard_map/ppermute | solution.py:710
  29.4 0.7 %copy-start = (bf16[320,256]{1,0:T(8,128)(2,1)}, bf16[320,256]{1,0:T(8,128)(2,1)S(1)}, u32[]{:S(2)}) copy-start(bf16[320,256]{1,0:T(8,128)(2,1)S(1)} %get-tuple-element.53.rest_7_) | copy-start | bytes 491524
  32.6 1.9 %collective-permute-start.12 = (f32[136,128]{1,0:T(8,128)S(1)}, f32[136,128]{1,0:T(8,128)S(1)}, u32[]{:S(2)}, u32[]{:S(2)}) collective-permute-start(f32[136,128]{1,0:T(8,128)S(1)} %shard_map.91.after), channel_id=1, source_target_pairs={{0,1},{1,0},{2,3},{3,2},{4,5},{5,4},{6,7},{7,6},{8,9},{9,8},{10,11... | collective-permute-start | bytes 208904 | tf_op jit(solution)/shard_map/ppermute | solution.py:710
  33.1 4.3 %collective-permute-start.14 = (f32[128,128]{1,0:T(8,128)S(1)}, f32[128,128]{1,0:T(8,128)S(1)}, u32[]{:S(2)}, u32[]{:S(2)}) collective-permute-start(f32[128,128]{1,0:T(8,128)S(1)} %add.10.after), channel_id=1, source_target_pairs={{0,2},{1,3},{2,0},{3,1},{4,6},{5,7},{6,4},{7,5},{8,10},{9,11},{10,... | collective-permute-start | bytes 196616 | tf_op jit(solution)/shard_map/ppermute | solution.py:710
  34.5 7.2 %collective-permute-start.13 = (f32[136,128]{1,0:T(8,128)S(1)}, f32[136,128]{1,0:T(8,128)S(1)}, u32[]{:S(2)}, u32[]{:S(2)}) collective-permute-start(f32[136,128]{1,0:T(8,128)S(1)} %add.11.rest_0_), channel_id=1, source_target_pairs={{0,2},{1,3},{2,0},{3,1},{4,6},{5,7},{6,4},{7,5},{8,10},{9,11},{10,... | collective-permute-start | bytes 208904 | tf_op jit(solution)/shard_map/ppermute | solution.py:710
  37.4 4.3 %copy-start.1 = (bf16[320,256]{1,0:T(8,128)(2,1)S(1)}, bf16[320,256]{1,0:T(8,128)(2,1)}, u32[]{:S(2)}) copy-start(bf16[320,256]{1,0:T(8,128)(2,1)} %copy-done) | copy-start | bytes 491524
  37.4 4.3 %collective-permute-start.15 = (f32[128,128]{1,0:T(8,128)S(1)}, f32[128,128]{1,0:T(8,128)S(1)}, u32[]{:S(2)}, u32[]{:S(2)}) collective-permute-start(f32[128,128]{1,0:T(8,128)S(1)} %add.12.rest_2_), channel_id=1, source_target_pairs={{0,16},{16,0},{1,17},{17,1},{2,18},{18,2},{3,19},{19,3},{4,20},{20... | collective-permute-start | bytes 196616 | tf_op jit(solution)/shard_map/ppermute | solution.py:691

commit v6 on v5

--- a/solution.py
+++ b/solution.py
@@ -83,7 +83,7 @@
 
 
 def parted(cols):
-    return cols * 7 // 16 // 8 * 8, cols * 13 // 16 // 8 * 8
+    return cols * 3 // 8 // 8 * 8, cols * 3 // 4 // 8 * 8
 
 
 def parity(axis):
@@ -700,17 +700,16 @@
     return lax.ppermute(value, axis, pairs + [(j, i) for i, j in pairs])
 
 
-def role_sums(value):
+def role_sums(value, far_first=False):
     size = lax.axis_size("role")
     if size & (size - 1) or size == 1:
         return [(lax.psum(value, "role"), jnp.zeros_like(value))]
+    steps = [1 << i for i in range(size.bit_length() - 1)]
     stages = []
-    step = 1
-    while step < size:
-        other = lax.ppermute(value, "role", [(i, i ^ step) for i in range(size)])
+    for step in steps[::-1] if far_first else steps:
+        other = lax.ppermute(value, "role", [(k, k ^ step) for k in range(size)])
         stages.append((value, other))
         value = value + other
-        step *= 2
     return stages
 
 
@@ -870,7 +869,7 @@
             last_cross_kernel, cross, sides, theirs[-1], left_half, right_half, spread, total
         )
         facing = shift(alone, ("member",), 1)
-        grams = (*role_sums(gram)[-1], alone, facing)
+        grams = (*role_sums(gram, True)[-1], alone, facing)
         three = call(
             functools.partial(deviation_kernel, layout[-1]),
             deviations(sides),

time: 46.6 us -> 49.6 us (1.064)
  waiting for transfers between devices: 13.7 us -> 17.3 us
  local copies, waits for them, and re-layouts: 0.68 us -> 0.01 us
    ppermute x4, waiting for transfers between devices: 2.7 us -> 5.34 us  [role_sums(): other = lax.ppermute(value, 'role', [(k, k ^ step) for k in range(size)])]
    ppermute x6, starting transfers between devices: 5.27 us -> 7 us  [shift(): return lax.ppermute(value, axes if len(axes) > 1 else axes[0], pairs)]
    ppermute x6, waiting for transfers between devices: 1.6 us -> 2.97 us  [trade(): return lax.ppermute(value, axis, pairs + [(j, i) for i, j in pairs])]
    ppermute x6, starting transfers between devices: 10.2 us -> 9.33 us  [trade(): return lax.ppermute(value, axis, pairs + [(j, i) for i, j in pairs])]
    unnamed x10 -> x6, local copies, waits for them, and re-layouts: 0.68 us -> 0.01 us
    ppermute x4, starting transfers between devices: 3.41 us -> 2.76 us  [role_sums(): other = lax.ppermute(value, 'role', [(k, k ^ step) for k in range(size)])]
  transfers between devices with their start and end apart: 16 -> 16, of which waited for: 8 -> 8; matrix products, arithmetic and copies ran while one was open for 0% -> 0% of each run, Pallas kernels for 13% -> 12%
where the time goes in v6:
time: 49.6 us; the launch traced here: 49.5 us
  starting transfers between devices  19.1 us (39%)
  waiting for transfers between devices  17.3 us (35%)
  Pallas kernels  12.2 us (25%)
  between operations  0.83 us (2%)
    pallas_call x12, Pallas kernels, call(): pl.pallas_call(body, out_shape=outs, in_specs=[SMEM] * scalars + [VMEM] *...  12.2 us
    ppermute x6, starting transfers between devices, trade(): return lax.ppermute(value, axis, pairs + [(j, i) for i, j in pairs])  9.33 us
    ppermute x6, waiting for transfers between devices, shift(): return lax.ppermute(value, axes if len(axes) > 1 else axes[0], pairs)  8.98 us
    ppermute x6, starting transfers between devices, shift(): return lax.ppermute(value, axes if len(axes) > 1 else axes[0], pairs)  7 us
    ppermute x4, waiting for transfers between devices, role_sums(): other = lax.ppermute(value, 'role', [(k, k ^ step) for k in range(size)])  5.34 us
    ppermute x6, waiting for transfers between devices, trade(): return lax.ppermute(value, axis, pairs + [(j, i) for i, j in pairs])  2.97 us
    ppermute x4, starting transfers between devices, role_sums(): other = lax.ppermute(value, 'role', [(k, k ^ step) for k in range(size)])  2.76 us
  transfers between devices with their start and end apart: 16, of which 8 were waited for; matrix products, arithmetic and copies ran while one was open for 0% of the time, Pallas kernels for 12%

profile of v6, /device:TPU:0, one launch (start us, length us, event | category | flops | bytes accessed | tf_op | source)
XLA Modules:
  0.0 49.5 jit_solution(17696199410621024634)
XLA Ops:
  0.0 1.3 %shard_map.83 = (f32[8,128,128]{2,1,0:T(8,128)S(1)}, f32[3,8,128]{2,1,0:T(8,128)S(1)}, f32[208,128]{1,0:T(8,128)S(1)}, f32[208,128]{1,0:T(8,128)S(1)}, f32[192,1...) custom-call(f32[1024,128]{1,0:T(8,128)} %bitcast.2, ...), custom_call_target="tpu_custom_call" | custom-call | tf_op jit(solution)/shard_map/pallas_call | solution.py:43
  1.4 0.0 copy-start.2
  1.4 5.1 %collective-permute-start = (f32[208,128]{1,0:T(8,128)S(1)}, f32[208,128]{1,0:T(8,128)S(1)}, u32[]{:S(2)}, u32[]{:S(2)}) collective-permute-start(f32[208,128]{1,0:T(8,128)S(1)} %get-tuple-element.34), channel_id=1, source_target_pairs={{4,8},{12,0},{8,4},{0,12},{5,9},{13,1},{9,5},{1,13},{6,10},{14,2},... | collective-permute-start | bytes 319496 | tf_op jit(solution)/shard_map/ppermute | solution.py:700
  6.5 0.0 collective-permute-start.4
  6.5 0.0 copy-start.1
  6.5 0.0 collective-permute-start.1
  6.5 1.7 %collective-permute-start.5 = (f32[40,128]{1,0:T(8,128)S(1)}, f32[40,128]{1,0:T(8,128)S(1)}, u32[]{:S(2)}, u32[]{:S(2)}) collective-permute-start(f32[40,128]{1,0:T(8,128)S(1)} %get-tuple-element.39), channel_id=1, source_target_pairs={{0,3},{1,0},{2,1},{3,2},{4,7},{5,4},{6,5},{7,6},{8,11},{9,8},{10,9... | collective-permute-start | bytes 61448 | tf_op jit(solution)/shard_map/ppermute | solution.py:691
  8.3 0.6 %collective-permute-start.2 = (f32[192,128]{1,0:T(8,128)S(1)}, f32[192,128]{1,0:T(8,128)S(1)}, u32[]{:S(2)}, u32[]{:S(2)}) collective-permute-start(f32[192,128]{1,0:T(8,128)S(1)} %get-tuple-element.36), channel_id=1, source_target_pairs={{4,8},{12,0},{8,4},{0,12},{5,9},{13,1},{9,5},{1,13},{6,10},{14,2},... | collective-permute-start | bytes 294920 | tf_op jit(solution)/shard_map/ppermute | solution.py:700
  8.9 0.8 %collective-permute-done.4.left = f32[40,128]{1,0:T(8,128)S(1)} collective-permute-done((f32[40,128]{1,0:T(8,128)S(1)}, f32[40,128]{1,0:T(8,128)S(1)}, u32[]{:S(2)}, u32[]{:S(2)}) %collective-permute-start.4) | collective-permute-done | bytes 20512 | tf_op jit(solution)/shard_map/ppermute | solution.py:691
  9.7 0.3 collective-permute-start.3
  10.7 0.0 copy-done.2
  10.7 0.0 copy-done.1
  10.7 0.0 copy-done
  10.7 0.4 shard_map.82.after.weight
  11.1 0.0 collective-permute-done.5.right
  11.1 3.0 %collective-permute-start.6 = (f32[168,128]{1,0:T(8,128)S(1)}, f32[168,128]{1,0:T(8,128)S(1)}, u32[]{:S(2)}, u32[]{:S(2)}) collective-permute-start(f32[168,128]{1,0:T(8,128)S(1)} %get-tuple-element.40), channel_id=1, source_target_pairs={{4,8},{12,0},{8,4},{0,12},{5,9},{13,1},{9,5},{1,13},{6,10},{14,2},... | collective-permute-start | bytes 258056 | tf_op jit(solution)/shard_map/ppermute | solution.py:700
  14.1 0.0 collective-permute-done.refs_0_.early
  14.1 0.3 collective-permute-start.7
  14.4 0.0 collective-permute-done.1.refs_1_.late
  14.4 0.7 %shard_map.84.after.first.own = f32[8,32,128]{2,1,0:T(8,128)S(1)} custom-call(f32[128,16]{1,0:T(8,128)S(1)} %shard_map.82.after.weight, f32[8,128,128]{2,1,0:T(8,128)S(1)} %get-tuple-element.32.field, f32[3,8,128]{2,1,0:T(8,128)S(1)} %get-tuple-element.33.kept, f32[208,128]{1,0:T(8,128)S(1)} %collective-permute-done.refs_0_.early, ...), custom_call_target="tpu_custom_call" | custom-call | tf_op jit(solution)/shard_map/pallas_call | solution.py:43
  15.1 0.6 %collective-permute-done.2.refs_2_.early_next = f32[192,128]{1,0:T(8,128)S(1)} collective-permute-done((f32[192,128]{1,0:T(8,128)S(1)}, f32[192,128]{1,0:T(8,128)S(1)}, u32[]{:S(2)}, u32[]{:S(2)}) %collective-permute-start.2) | collective-permute-done | bytes 98336 | tf_op jit(solution)/shard_map/ppermute | solution.py:700
  15.7 2.3 %collective-permute-done.3.refs_3_.late_next = f32[192,128]{1,0:T(8,128)S(1)} collective-permute-done((f32[192,128]{1,0:T(8,128)S(1)}, f32[192,128]{1,0:T(8,128)S(1)}, u32[]{:S(2)}, u32[]{:S(2)}) %collective-permute-start.3) | collective-permute-done | bytes 98336 | tf_op jit(solution)/shard_map/ppermute | solution.py:700
  18.1 0.9 %shard_map.85.after.second.own = f32[8,48,128]{2,1,0:T(8,128)S(1)} custom-call(f32[8,32,128]{2,1,0:T(8,128)S(1)} %shard_map.84.after.first.own, f32[8,128,128]{2,1,0:T(8,128)S(1)} %get-tuple-element.32.field, f32[3,8,128]{2,1,0:T(8,128)S(1)} %get-tuple-element.33.kept, f32[208,128]{1,0:T(8,128)S(1)} %collective-permute-done.refs_0_.early, ...), custom_call_target="tpu_custom_call" | custom-call | tf_op jit(solution)/shard_map/pallas_call | solution.py:43
  18.9 1.6 %collective-permute-start.9 = (f32[8,48,128]{2,1,0:T(8,128)S(1)}, f32[8,48,128]{2,1,0:T(8,128)S(1)}, u32[]{:S(2)}, u32[]{:S(2)}) collective-permute-start(f32[8,48,128]{2,1,0:T(8,128)S(1)} %shard_map.85.after.second.own), channel_id=1, source_target_pairs={{0,16},{16,0},{1,17},{17,1},{2,18},{18,2},{3,19},{19,3},{4,20},{20... | collective-permute-start | bytes 589832 | tf_op jit(solution)/shard_map/ppermute | solution.py:691
  20.5 0.0 collective-permute-done.6.early_rest
  20.5 0.0 collective-permute-done.7.late_rest
  20.5 1.1 %shard_map.87.sides.own = f32[8,48,128]{2,1,0:T(8,128)S(1)} custom-call(f32[8,48,128]{2,1,0:T(8,128)S(1)} %shard_map.85.after.second.own, f32[8,128,128]{2,1,0:T(8,128)S(1)} %get-tuple-element.32.field, f32[3,8,128]{2,1,0:T(8,128)S(1)} %get-tuple-element.33.kept, f32[208,128]{1,0:T(8,128)S(1)} %collective-permute-done.refs_0_.early, ...), custom_call_target="tpu_custom_call" | custom-call | tf_op jit(solution)/shard_map/pallas_call | solution.py:43
  21.7 1.3 %collective-permute-start.8 = (f32[8,48,128]{2,1,0:T(8,128)S(1)}, f32[8,48,128]{2,1,0:T(8,128)S(1)}, u32[]{:S(2)}, u32[]{:S(2)}) collective-permute-start(f32[8,48,128]{2,1,0:T(8,128)S(1)} %shard_map.87.sides.own), channel_id=1, source_target_pairs={{0,16},{16,0},{1,17},{17,1},{2,18},{18,2},{3,19},{19,3},{4,20},{20... | collective-permute-start | bytes 589832 | tf_op jit(solution)/shard_map/ppermute | solution.py:691
  23.0 0.8 %collective-permute-start.11 = (f32[8,32,128]{2,1,0:T(8,128)S(1)}, f32[8,32,128]{2,1,0:T(8,128)S(1)}, u32[]{:S(2)}, u32[]{:S(2)}) collective-permute-start(f32[8,32,128]{2,1,0:T(8,128)S(1)} %shard_map.84.after.first.own), channel_id=1, source_target_pairs={{0,16},{16,0},{1,17},{17,1},{2,18},{18,2},{3,19},{19,3},{4,20},{20... | collective-permute-start | bytes 393224 | tf_op jit(solution)/shard_map/ppermute | solution.py:691
  23.7 1.0 %shard_map.88 = (f32[128,128]{1,0:T(8,128)S(1)}, bf16[128,384]{1,0:T(8,128)(2,1)S(1)}, bf16[128,384]{1,0:T(8,128)(2,1)S(1)}, f32[3,384,128]{2,1,0:T(8,128)S(1)}) custom-call(f32[8,32,128]{2,1,0:T(8,128)S(1)} %shard_map.84.after.first.own, f32[8,48,128]{2,1,0:T(8,128)S(1)} %shard_map.85.after.second.own, f32[8,48,128]{2,1,0:T(8,128)S(1)} %shard_map.87.sides.own, ...), custom_call_target="tpu_custom_call" | custom-call | tf_op jit(solution)/shard_map/pallas_call | solution.py:43
  24.8 0.1 collective-permute-start.10
  24.9 1.2 %collective-permute-done.10 = f32[128,128]{1,0:T(8,128)S(1)} collective-permute-done((f32[128,128]{1,0:T(8,128)S(1)}, f32[128,128]{1,0:T(8,128)S(1)}, u32[]{:S(2)}, u32[]{:S(2)}) %collective-permute-start.10) | collective-permute-done | bytes 65568 | tf_op jit(solution)/shard_map/ppermute | solution.py:710
  26.1 5.6 %collective-permute-done.11.other = f32[8,32,128]{2,1,0:T(8,128)S(1)} collective-permute-done((f32[8,32,128]{2,1,0:T(8,128)S(1)}, f32[8,32,128]{2,1,0:T(8,128)S(1)}, u32[]{:S(2)}, u32[]{:S(2)}) %collective-permute-start.11) | collective-permute-done | bytes 131104 | tf_op jit(solution)/shard_map/ppermute | solution.py:691
  31.7 0.6 %shard_map.89 = (bf16[256,256]{1,0:T(8,128)(2,1)S(1)}, bf16[256,256]{1,0:T(8,128)(2,1)S(1)}, f32[8,128]{1,0:T(8,128)S(1)}, f32[136,128]{1,0:T(8,128)S(1)}) custom-call(f32[8,32,128]{2,1,0:T(8,128)S(1)} %shard_map.84.after.first.own, f32[8,32,128]{2,1,0:T(8,128)S(1)} %collective-permute-done.11.other, f32[128,16]{1,0:T(8,128)S(1)} %shard_map.82.after.weight, ...), custom_call_target="tpu_custom_call" | custom-call | tf_op jit(solution)/shard_map/pallas_call | solution.py:43
  32.3 0.0 collective-permute-done.9.other
  32.3 0.9 %shard_map.90 = (bf16[384,256]{1,0:T(8,128)(2,1)S(1)}, bf16[384,256]{1,0:T(8,128)(2,1)S(1)}, f32[8,128]{1,0:T(8,128)S(1)}, f32[136,128]{1,0:T(8,128)S(1)}) custom-call(f32[8,48,128]{2,1,0:T(8,128)S(1)} %shard_map.85.after.second.own, f32[8,48,128]{2,1,0:T(8,128)S(1)} %collective-permute-done.9.other, f32[128,16]{1,0:T(8,128)S(1)} %shard_map.82.after.weight, ...), custom_call_target="tpu_custom_call" | custom-call | tf_op jit(solution)/shard_map/pallas_call | solution.py:43
  33.2 0.0 collective-permute-done.8.other
  33.2 0.4 shard_map.91.after
  33.6 2.5 %collective-permute-start.12 = (f32[136,128]{1,0:T(8,128)S(1)}, f32[136,128]{1,0:T(8,128)S(1)}, u32[]{:S(2)}, u32[]{:S(2)}) collective-permute-start(f32[136,128]{1,0:T(8,128)S(1)} %shard_map.91.after), channel_id=1, source_target_pairs={{0,2},{1,3},{2,0},{3,1},{4,6},{5,7},{6,4},{7,5},{8,10},{9,11},{10,... | collective-permute-start | bytes 208904 | tf_op jit(solution)/shard_map/ppermute | solution.py:710
  36.2 0.1 collective-permute-start.14
  36.3 2.3 %collective-permute-done.12 = f32[136,128]{1,0:T(8,128)S(1)} collective-permute-done((f32[136,128]{1,0:T(8,128)S(1)}, f32[136,128]{1,0:T(8,128)S(1)}, u32[]{:S(2)}, u32[]{:S(2)}) %collective-permute-start.12) | collective-permute-done | bytes 69664 | tf_op jit(solution)/shard_map/ppermute | solution.py:710
  38.6 0.1 collective-permute-start.13
  38.6 1.8 %collective-permute-done.14 = f32[128,128]{1,0:T(8,128)S(1)} collective-permute-done((f32[128,128]{1,0:T(8,128)S(1)}, f32[128,128]{1,0:T(8,128)S(1)}, u32[]{:S(2)}, u32[]{:S(2)}) %collective-permute-start.14) | collective-permute-done | bytes 65568 | tf_op jit(solution)/shard_map/ppermute | solution.py:710
  40.5 1.6 %collective-permute-start.15 = (f32[128,128]{1,0:T(8,128)S(1)}, f32[128,128]{1,0:T(8,128)S(1)}, u32[]{:S(2)}, u32[]{:S(2)}) collective-permute-start(f32[128,128]{1,0:T(8,128)S(1)} %add.12.rest_2_), channel_id=1, source_target_pairs={{0,16},{16,0},{1,17},{17,1},{2,18},{18,2},{3,19},{19,3},{4,20},{20... | collective-permute-start | bytes 196616 | tf_op jit(solution)/shard_map/ppermute | solution.py:691
  42.0 0.2 shard_map.92
  42.2 2.6 %collective-permute-done.15.rest_3_ = f32[128,128]{1,0:T(8,128)S(1)} collective-permute-done((f32[128,128]{1,0:T(8,128)S(1)}, f32[128,128]{1,0:T(8,128)S(1)}, u32[]{:S(2)}, u32[]{:S(2)}) %collective-permute-start.15) | collective-permute-done | bytes 65568 | tf_op jit(solution)/shard_map/ppermute | solution.py:691
  44.8 0.0 collective-permute-done.13.rest_1_
  44.8 4.7 %shard_map.93 = f32[1024,128]{1,0:T(8,128)} custom-call(f32[136,128]{1,0:T(8,128)S(1)} %add.11.rest_0_, f32[136,128]{1,0:T(8,128)S(1)} %collective-permute-done.13.rest_1_, f32[128,128]{1,0:T(8,128)S(1)} %add.12.rest_2_, f32[128,128]{1,0:T(8,128)S(1)} %collective-permute-done.15.rest_3_, bf16[256,256]{1,0:T(8,128)(2,1)S(1)} %get-tuple-element.50.rest_4_, ...), custom_call_target="tpu_custom_call" | custom-call | tf_op jit(solution)/shard_map/pallas_call | solution.py:43
  (5 shorter events, 0.1 us)
Async XLA Ops:
  1.4 9.3 %copy-start.2 = (f32[1,1024]{1,0:T(1,128)S(1)}, f32[1,1024]{1,0:T(1,128)}, u32[]{:S(2)}) copy-start(f32[1,1024]{1,0:T(1,128)} %weights.1) | copy-start | bytes 12292
  1.4 12.8 %collective-permute-start = (f32[208,128]{1,0:T(8,128)S(1)}, f32[208,128]{1,0:T(8,128)S(1)}, u32[]{:S(2)}, u32[]{:S(2)}) collective-permute-start(f32[208,128]{1,0:T(8,128)S(1)} %get-tuple-element.34), channel_id=1, source_target_pairs={{4,8},{12,0},{8,4},{0,12},{5,9},{13,1},{9,5},{1,13},{6,10},{14,2},... | collective-permute-start | bytes 319496 | tf_op jit(solution)/shard_map/ppermute | solution.py:700
  6.5 3.2 %collective-permute-start.4 = (f32[40,128]{1,0:T(8,128)S(1)}, f32[40,128]{1,0:T(8,128)S(1)}, u32[]{:S(2)}, u32[]{:S(2)}) collective-permute-start(f32[40,128]{1,0:T(8,128)S(1)} %get-tuple-element.38), channel_id=1, source_target_pairs={{0,1},{1,2},{2,3},{3,0},{4,5},{5,6},{6,7},{7,4},{8,9},{9,10},{10,1... | collective-permute-start | bytes 61448 | tf_op jit(solution)/shard_map/ppermute | solution.py:691
  6.5 4.2 %copy-start.1 = (f32[1,1024]{1,0:T(1,128)S(1)}, f32[1,1024]{1,0:T(1,128)}, u32[]{:S(2)}) copy-start(f32[1,1024]{1,0:T(1,128)} %values.1) | copy-start | bytes 12292
  6.5 4.2 %copy-start = (s32[1,1024]{1,0:T(1,128)S(1)}, s32[1,1024]{1,0:T(1,128)}, u32[]{:S(2)}) copy-start(s32[1,1024]{1,0:T(1,128)} %cells.1) | copy-start | bytes 12292
  6.5 7.9 %collective-permute-start.1 = (f32[208,128]{1,0:T(8,128)S(1)}, f32[208,128]{1,0:T(8,128)S(1)}, u32[]{:S(2)}, u32[]{:S(2)}) collective-permute-start(f32[208,128]{1,0:T(8,128)S(1)} %get-tuple-element.35), channel_id=1, source_target_pairs={{0,4},{8,12},{4,0},{12,8},{1,5},{9,13},{5,1},{13,9},{2,6},{10,14},... | collective-permute-start | bytes 319496 | tf_op jit(solution)/shard_map/ppermute | solution.py:700
  6.5 4.6 %collective-permute-start.5 = (f32[40,128]{1,0:T(8,128)S(1)}, f32[40,128]{1,0:T(8,128)S(1)}, u32[]{:S(2)}, u32[]{:S(2)}) collective-permute-start(f32[40,128]{1,0:T(8,128)S(1)} %get-tuple-element.39), channel_id=1, source_target_pairs={{0,3},{1,0},{2,1},{3,2},{4,7},{5,4},{6,5},{7,6},{8,11},{9,8},{10,9... | collective-permute-start | bytes 61448 | tf_op jit(solution)/shard_map/ppermute | solution.py:691
  8.3 7.5 %collective-permute-start.2 = (f32[192,128]{1,0:T(8,128)S(1)}, f32[192,128]{1,0:T(8,128)S(1)}, u32[]{:S(2)}, u32[]{:S(2)}) collective-permute-start(f32[192,128]{1,0:T(8,128)S(1)} %get-tuple-element.36), channel_id=1, source_target_pairs={{4,8},{12,0},{8,4},{0,12},{5,9},{13,1},{9,5},{1,13},{6,10},{14,2},... | collective-permute-start | bytes 294920 | tf_op jit(solution)/shard_map/ppermute | solution.py:700
  9.7 8.3 %collective-permute-start.3 = (f32[192,128]{1,0:T(8,128)S(1)}, f32[192,128]{1,0:T(8,128)S(1)}, u32[]{:S(2)}, u32[]{:S(2)}) collective-permute-start(f32[192,128]{1,0:T(8,128)S(1)} %get-tuple-element.37), channel_id=1, source_target_pairs={{0,4},{8,12},{4,0},{12,8},{1,5},{9,13},{5,1},{13,9},{2,6},{10,14},... | collective-permute-start | bytes 294920 | tf_op jit(solution)/shard_map/ppermute | solution.py:700
  11.1 9.4 %collective-permute-start.6 = (f32[168,128]{1,0:T(8,128)S(1)}, f32[168,128]{1,0:T(8,128)S(1)}, u32[]{:S(2)}, u32[]{:S(2)}) collective-permute-start(f32[168,128]{1,0:T(8,128)S(1)} %get-tuple-element.40), channel_id=1, source_target_pairs={{4,8},{12,0},{8,4},{0,12},{5,9},{13,1},{9,5},{1,13},{6,10},{14,2},... | collective-permute-start | bytes 258056 | tf_op jit(solution)/shard_map/ppermute | solution.py:700
  14.1 6.4 %collective-permute-start.7 = (f32[168,128]{1,0:T(8,128)S(1)}, f32[168,128]{1,0:T(8,128)S(1)}, u32[]{:S(2)}, u32[]{:S(2)}) collective-permute-start(f32[168,128]{1,0:T(8,128)S(1)} %get-tuple-element.41), channel_id=1, source_target_pairs={{0,4},{8,12},{4,0},{12,8},{1,5},{9,13},{5,1},{13,9},{2,6},{10,14},... | collective-permute-start | bytes 258056 | tf_op jit(solution)/shard_map/ppermute | solution.py:700
  18.9 13.4 %collective-permute-start.9 = (f32[8,48,128]{2,1,0:T(8,128)S(1)}, f32[8,48,128]{2,1,0:T(8,128)S(1)}, u32[]{:S(2)}, u32[]{:S(2)}) collective-permute-start(f32[8,48,128]{2,1,0:T(8,128)S(1)} %shard_map.85.after.second.own), channel_id=1, source_target_pairs={{0,16},{16,0},{1,17},{17,1},{2,18},{18,2},{3,19},{19,3},{4,20},{20... | collective-permute-start | bytes 589832 | tf_op jit(solution)/shard_map/ppermute | solution.py:691
  21.7 11.5 %collective-permute-start.8 = (f32[8,48,128]{2,1,0:T(8,128)S(1)}, f32[8,48,128]{2,1,0:T(8,128)S(1)}, u32[]{:S(2)}, u32[]{:S(2)}) collective-permute-start(f32[8,48,128]{2,1,0:T(8,128)S(1)} %shard_map.87.sides.own), channel_id=1, source_target_pairs={{0,16},{16,0},{1,17},{17,1},{2,18},{18,2},{3,19},{19,3},{4,20},{20... | collective-permute-start | bytes 589832 | tf_op jit(solution)/shard_map/ppermute | solution.py:691
  23.0 8.7 %collective-permute-start.11 = (f32[8,32,128]{2,1,0:T(8,128)S(1)}, f32[8,32,128]{2,1,0:T(8,128)S(1)}, u32[]{:S(2)}, u32[]{:S(2)}) collective-permute-start(f32[8,32,128]{2,1,0:T(8,128)S(1)} %shard_map.84.after.first.own), channel_id=1, source_target_pairs={{0,16},{16,0},{1,17},{17,1},{2,18},{18,2},{3,19},{19,3},{4,20},{20... | collective-permute-start | bytes 393224 | tf_op jit(solution)/shard_map/ppermute | solution.py:691
  24.8 1.3 %collective-permute-start.10 = (f32[128,128]{1,0:T(8,128)S(1)}, f32[128,128]{1,0:T(8,128)S(1)}, u32[]{:S(2)}, u32[]{:S(2)}) collective-permute-start(f32[128,128]{1,0:T(8,128)S(1)} %get-tuple-element.45), channel_id=1, source_target_pairs={{0,1},{1,0},{2,3},{3,2},{4,5},{5,4},{6,7},{7,6},{8,9},{9,8},{10,11... | collective-permute-start | bytes 196616 | tf_op jit(solution)/shard_map/ppermute | solution.py:710
  33.6 4.9 %collective-permute-start.12 = (f32[136,128]{1,0:T(8,128)S(1)}, f32[136,128]{1,0:T(8,128)S(1)}, u32[]{:S(2)}, u32[]{:S(2)}) collective-permute-start(f32[136,128]{1,0:T(8,128)S(1)} %shard_map.91.after), channel_id=1, source_target_pairs={{0,2},{1,3},{2,0},{3,1},{4,6},{5,7},{6,4},{7,5},{8,10},{9,11},{10,... | collective-permute-start | bytes 208904 | tf_op jit(solution)/shard_map/ppermute | solution.py:710
  36.2 4.3 %collective-permute-start.14 = (f32[128,128]{1,0:T(8,128)S(1)}, f32[128,128]{1,0:T(8,128)S(1)}, u32[]{:S(2)}, u32[]{:S(2)}) collective-permute-start(f32[128,128]{1,0:T(8,128)S(1)} %add.10.after), channel_id=1, source_target_pairs={{0,2},{1,3},{2,0},{3,1},{4,6},{5,7},{6,4},{7,5},{8,10},{9,11},{10,... | collective-permute-start | bytes 196616 | tf_op jit(solution)/shard_map/ppermute | solution.py:710
  38.6 6.2 %collective-permute-start.13 = (f32[136,128]{1,0:T(8,128)S(1)}, f32[136,128]{1,0:T(8,128)S(1)}, u32[]{:S(2)}, u32[]{:S(2)}) collective-permute-start(f32[136,128]{1,0:T(8,128)S(1)} %add.11.rest_0_), channel_id=1, source_target_pairs={{0,1},{1,0},{2,3},{3,2},{4,5},{5,4},{6,7},{7,6},{8,9},{9,8},{10,11... | collective-permute-start | bytes 208904 | tf_op jit(solution)/shard_map/ppermute | solution.py:710
  40.5 4.3 %collective-permute-start.15 = (f32[128,128]{1,0:T(8,128)S(1)}, f32[128,128]{1,0:T(8,128)S(1)}, u32[]{:S(2)}, u32[]{:S(2)}) collective-permute-start(f32[128,128]{1,0:T(8,128)S(1)} %add.12.rest_2_), channel_id=1, source_target_pairs={{0,16},{16,0},{1,17},{17,1},{2,18},{18,2},{3,19},{19,3},{4,20},{20... | collective-permute-start | bytes 196616 | tf_op jit(solution)/shard_map/ppermute | solution.py:691

commit v7 on v3

--- a/solution.py
+++ b/solution.py
@@ -59,8 +59,16 @@
     return lax.dot_general(a, b, (dims, ((), ())), preferred_element_type=jnp.float32)
 
 
-def dot3(a, b, dims=((1,), (0,))):
-    return dot(a[0], b[0], dims) + (dot(a[0], b[1], dims) + dot(a[1], b[0], dims))
+def by_halves(product, *operands):
+    half = operands[0].shape[0] // 2
+    parts = [product(*(o[at] for o in operands)) for at in (slice(0, half), slice(half, None))]
+    return jnp.concatenate(parts, axis=0)
+
+
+def dot3(a, b):
+    return by_halves(
+        lambda high, low: (dot(high, b[0]) + dot(low, b[0])) + dot(high, b[1]), *a
+    )
 
 
 def loop(count, body):
@@ -457,8 +465,8 @@
             if own is sides:
                 at = pl.ds(b * depth, depth)
                 left[:, at], right[:, at] = turned
-                lane = lax.broadcasted_iota(jnp.int32, (depth, local), 1)
-                spread[at] = jnp.where(lane == 0, plain, jnp.where(lane == 1, valued, mean))
+                for i, column in enumerate((plain, valued, mean)):
+                    spread[i, at] = jnp.broadcast_to(column, (depth, local))
 
         loop(rows // many, block)
 
@@ -518,7 +526,7 @@
     def block(b):
         at = pl.ds(b * depth, depth)
         value, partner = cells_of(own, b, many), cells_of(other, b, many)
-        counter = tally(total, local, value, partner, *(spread[at, i : i + 1] for i in range(3)))
+        counter = tally(total, local, value, partner, *(spread[i, at] for i in range(3)))
         total[pl.ds(0, local)] += dot_wide(
             (left[:, at], right[:, at]), wide(halves(counter)), local
         )
@@ -836,7 +844,7 @@
         half = struct(local, sided, kind=jnp.bfloat16)
         alone, left_half, right_half, spread = call(
             functools.partial(own_gram_kernel, layout),
-            (struct(local, local), half, half, struct(sided, local)),
+            (struct(local, local), half, half, struct(3, sided, local)),
             *owns,
             weight,
         )

time: 48.9 us -> 48.8 us (level)
  Pallas kernels: 13 us -> 12.2 us
  local copies, waits for them, and re-layouts: 0.02 us -> 0.68 us
    pallas_call x12, Pallas kernels: 13 us -> 12.2 us  [call(): pl.pallas_call(body, out_shape=outs, in_specs=[SMEM] * scalars + [VMEM] *...]
    unnamed x6 -> x14, local copies, waits for them, and re-layouts: 0.02 us -> 0.68 us
where the time goes in v7:
time: 48.8 us; the launch traced here: 48.7 us
  starting transfers between devices  20.3 us (42%)
  waiting for transfers between devices  14.6 us (30%)
  Pallas kernels  12.2 us (25%)
  between operations  0.86 us (2%)
  local copies, waits for them, and re-layouts  0.68 us (1%)
    pallas_call x12, Pallas kernels, call(): pl.pallas_call(body, out_shape=outs, in_specs=[SMEM] * scalars + [VMEM] *...  12.2 us
    ppermute x6, starting transfers between devices, trade(): return lax.ppermute(value, axis, pairs + [(j, i) for i, j in pairs])  9.33 us
    ppermute x6, waiting for transfers between devices, shift(): return lax.ppermute(value, axes if len(axes) > 1 else axes[0], pairs)  8.56 us
    ppermute x6, starting transfers between devices, shift(): return lax.ppermute(value, axes if len(axes) > 1 else axes[0], pairs)  7.01 us
    ppermute x4, starting transfers between devices, role_sums(): other = lax.ppermute(value, 'role', [(i, i ^ step) for i in range(size)])  3.93 us
    ppermute x6, waiting for transfers between devices, trade(): return lax.ppermute(value, axis, pairs + [(j, i) for i, j in pairs])  3.37 us
    ppermute x4, waiting for transfers between devices, role_sums(): other = lax.ppermute(value, 'role', [(i, i ^ step) for i in range(size)])  2.67 us
  transfers between devices with their start and end apart: 16, of which 7 were waited for; matrix products, arithmetic and copies ran while one was open for 0% of the time, Pallas kernels for 12%

profile of v7, /device:TPU:0, one launch (start us, length us, event | category | flops | bytes accessed | tf_op | source)
XLA Modules:
  0.0 48.7 jit_solution(5387861853816796579)
XLA Ops:
  0.0 1.3 %shard_map.82 = (f32[8,128,128]{2,1,0:T(8,128)S(1)}, f32[3,8,128]{2,1,0:T(8,128)S(1)}, f32[208,128]{1,0:T(8,128)S(1)}, f32[208,128]{1,0:T(8,128)S(1)}, f32[192,1...) custom-call(f32[1024,128]{1,0:T(8,128)} %bitcast.2, ...), custom_call_target="tpu_custom_call" | custom-call | tf_op jit(solution)/shard_map/pallas_call | solution.py:43
  1.4 5.1 %collective-permute-start = (f32[208,128]{1,0:T(8,128)S(1)}, f32[208,128]{1,0:T(8,128)S(1)}, u32[]{:S(2)}, u32[]{:S(2)}) collective-permute-start(f32[208,128]{1,0:T(8,128)S(1)} %get-tuple-element.34), channel_id=1, source_target_pairs={{4,8},{12,0},{8,4},{0,12},{5,9},{13,1},{9,5},{1,13},{6,10},{14,2},... | collective-permute-start | bytes 319496 | tf_op jit(solution)/shard_map/ppermute | solution.py:700
  6.5 0.0 collective-permute-start.4
  6.5 0.0 collective-permute-start.1
  6.5 1.7 %collective-permute-start.5 = (f32[40,128]{1,0:T(8,128)S(1)}, f32[40,128]{1,0:T(8,128)S(1)}, u32[]{:S(2)}, u32[]{:S(2)}) collective-permute-start(f32[40,128]{1,0:T(8,128)S(1)} %get-tuple-element.39), channel_id=1, source_target_pairs={{0,3},{1,0},{2,1},{3,2},{4,7},{5,4},{6,5},{7,6},{8,11},{9,8},{10,9... | collective-permute-start | bytes 61448 | tf_op jit(solution)/shard_map/ppermute | solution.py:691
  8.3 0.6 %collective-permute-start.2 = (f32[192,128]{1,0:T(8,128)S(1)}, f32[192,128]{1,0:T(8,128)S(1)}, u32[]{:S(2)}, u32[]{:S(2)}) collective-permute-start(f32[192,128]{1,0:T(8,128)S(1)} %get-tuple-element.36), channel_id=1, source_target_pairs={{4,8},{12,0},{8,4},{0,12},{5,9},{13,1},{9,5},{1,13},{6,10},{14,2},... | collective-permute-start | bytes 294920 | tf_op jit(solution)/shard_map/ppermute | solution.py:700
  8.9 0.8 %collective-permute-done.4.left = f32[40,128]{1,0:T(8,128)S(1)} collective-permute-done((f32[40,128]{1,0:T(8,128)S(1)}, f32[40,128]{1,0:T(8,128)S(1)}, u32[]{:S(2)}, u32[]{:S(2)}) %collective-permute-start.4) | collective-permute-done | bytes 20512 | tf_op jit(solution)/shard_map/ppermute | solution.py:691
  9.7 0.3 collective-permute-start.3
  10.0 0.0 collective-permute-done.5.right
  10.0 3.0 %collective-permute-start.6 = (f32[168,128]{1,0:T(8,128)S(1)}, f32[168,128]{1,0:T(8,128)S(1)}, u32[]{:S(2)}, u32[]{:S(2)}) collective-permute-start(f32[168,128]{1,0:T(8,128)S(1)} %get-tuple-element.40), channel_id=1, source_target_pairs={{4,8},{12,0},{8,4},{0,12},{5,9},{13,1},{9,5},{1,13},{6,10},{14,2},... | collective-permute-start | bytes 258056 | tf_op jit(solution)/shard_map/ppermute | solution.py:700
  13.0 0.0 collective-permute-done.refs_0_.early
  13.0 0.3 collective-permute-start.7
  14.0 0.0 collective-permute-done.1.refs_1_.late
  14.0 0.7 %shard_map.83.refs_4_.first.own = f32[8,32,128]{2,1,0:T(8,128)S(1)} custom-call(f32[8,128,128]{2,1,0:T(8,128)S(1)} %get-tuple-element.32.field, f32[3,8,128]{2,1,0:T(8,128)S(1)} %get-tuple-element.33.kept, f32[208,128]{1,0:T(8,128)S(1)} %collective-permute-done.refs_0_.early, f32[208,128]{1,0:T(8,128)S(1)} %collective-permute-done.1.refs_1_.late), custom_call_target="tpu_custom_call" | custom-call | tf_op jit(solution)/shard_map/pallas_call | solution.py:43
  14.6 0.0 copy-start.4
  14.6 0.0 copy-start.5
  14.7 0.0 copy-start.6
  14.7 1.0 %collective-permute-done.2.refs_2_.early_next = f32[192,128]{1,0:T(8,128)S(1)} collective-permute-done((f32[192,128]{1,0:T(8,128)S(1)}, f32[192,128]{1,0:T(8,128)S(1)}, u32[]{:S(2)}, u32[]{:S(2)}) %collective-permute-start.2) | collective-permute-done | bytes 98336 | tf_op jit(solution)/shard_map/ppermute | solution.py:700
  15.7 2.3 %collective-permute-done.3.refs_3_.late_next = f32[192,128]{1,0:T(8,128)S(1)} collective-permute-done((f32[192,128]{1,0:T(8,128)S(1)}, f32[192,128]{1,0:T(8,128)S(1)}, u32[]{:S(2)}, u32[]{:S(2)}) %collective-permute-start.3) | collective-permute-done | bytes 98336 | tf_op jit(solution)/shard_map/ppermute | solution.py:700
  18.0 0.9 %shard_map.84.after.second.own = f32[8,48,128]{2,1,0:T(8,128)S(1)} custom-call(f32[8,128,128]{2,1,0:T(8,128)S(1)} %get-tuple-element.32.field, f32[3,8,128]{2,1,0:T(8,128)S(1)} %get-tuple-element.33.kept, f32[208,128]{1,0:T(8,128)S(1)} %collective-permute-done.refs_0_.early, f32[208,128]{1,0:T(8,128)S(1)} %collective-permute-done.1.refs_1_.late, ...), custom_call_target="tpu_custom_call" | custom-call | tf_op jit(solution)/shard_map/pallas_call | solution.py:43
  18.9 1.6 %collective-permute-start.9 = (f32[8,48,128]{2,1,0:T(8,128)S(1)}, f32[8,48,128]{2,1,0:T(8,128)S(1)}, u32[]{:S(2)}, u32[]{:S(2)}) collective-permute-start(f32[8,48,128]{2,1,0:T(8,128)S(1)} %shard_map.84.after.second.own), channel_id=1, source_target_pairs={{0,16},{16,0},{1,17},{17,1},{2,18},{18,2},{3,19},{19,3},{4,20},{20... | collective-permute-start | bytes 589832 | tf_op jit(solution)/shard_map/ppermute | solution.py:691
  20.5 0.4 shard_map.85.after.weight
  20.9 0.0 collective-permute-done.6.early_rest
  20.9 0.0 collective-permute-done.7.late_rest
  20.9 1.1 %shard_map.87.sides.own = f32[8,48,128]{2,1,0:T(8,128)S(1)} custom-call(f32[128,16]{1,0:T(8,128)S(1)} %shard_map.85.after.weight, f32[8,128,128]{2,1,0:T(8,128)S(1)} %get-tuple-element.32.field, f32[3,8,128]{2,1,0:T(8,128)S(1)} %get-tuple-element.33.kept, f32[208,128]{1,0:T(8,128)S(1)} %collective-permute-done.refs_0_.early, ...), custom_call_target="tpu_custom_call" | custom-call | tf_op jit(solution)/shard_map/pallas_call | solution.py:43
  22.1 0.9 %collective-permute-start.8 = (f32[8,48,128]{2,1,0:T(8,128)S(1)}, f32[8,48,128]{2,1,0:T(8,128)S(1)}, u32[]{:S(2)}, u32[]{:S(2)}) collective-permute-start(f32[8,48,128]{2,1,0:T(8,128)S(1)} %shard_map.87.sides.own), channel_id=1, source_target_pairs={{0,16},{16,0},{1,17},{17,1},{2,18},{18,2},{3,19},{19,3},{4,20},{20... | collective-permute-start | bytes 589832 | tf_op jit(solution)/shard_map/ppermute | solution.py:691
  23.0 1.2 %collective-permute-start.11 = (f32[8,32,128]{2,1,0:T(8,128)S(1)}, f32[8,32,128]{2,1,0:T(8,128)S(1)}, u32[]{:S(2)}, u32[]{:S(2)}) collective-permute-start(f32[8,32,128]{2,1,0:T(8,128)S(1)} %shard_map.83.refs_4_.first.own), channel_id=1, source_target_pairs={{0,16},{16,0},{1,17},{17,1},{2,18},{18,2},{3,19},{19,3},{4,20},{20... | collective-permute-start | bytes 393224 | tf_op jit(solution)/shard_map/ppermute | solution.py:691
  24.2 1.0 %shard_map.88 = (f32[128,128]{1,0:T(8,128)S(1)}, bf16[128,384]{1,0:T(8,128)(2,1)S(1)}, bf16[128,384]{1,0:T(8,128)(2,1)S(1)}, f32[3,384,128]{2,1,0:T(8,128)S(1)}) custom-call(f32[8,32,128]{2,1,0:T(8,128)S(1)} %shard_map.83.refs_4_.first.own, f32[8,48,128]{2,1,0:T(8,128)S(1)} %shard_map.84.after.second.own, f32[8,48,128]{2,1,0:T(8,128)S(1)} %shard_map.87.sides.own, ...), custom_call_target="tpu_custom_call" | custom-call | tf_op jit(solution)/shard_map/pallas_call | solution.py:43
  25.2 0.1 collective-permute-start.10
  25.3 1.2 %collective-permute-done.10 = f32[128,128]{1,0:T(8,128)S(1)} collective-permute-done((f32[128,128]{1,0:T(8,128)S(1)}, f32[128,128]{1,0:T(8,128)S(1)}, u32[]{:S(2)}, u32[]{:S(2)}) %collective-permute-start.10) | collective-permute-done | bytes 65568 | tf_op jit(solution)/shard_map/ppermute | solution.py:710
  26.5 5.1 %collective-permute-done.11.other = f32[8,32,128]{2,1,0:T(8,128)S(1)} collective-permute-done((f32[8,32,128]{2,1,0:T(8,128)S(1)}, f32[8,32,128]{2,1,0:T(8,128)S(1)}, u32[]{:S(2)}, u32[]{:S(2)}) %collective-permute-start.11) | collective-permute-done | bytes 131104 | tf_op jit(solution)/shard_map/ppermute | solution.py:691
  31.7 0.6 %shard_map.89 = (bf16[256,256]{1,0:T(8,128)(2,1)S(1)}, bf16[256,256]{1,0:T(8,128)(2,1)S(1)}, f32[8,128]{1,0:T(8,128)S(1)}, f32[136,128]{1,0:T(8,128)S(1)}) custom-call(f32[8,32,128]{2,1,0:T(8,128)S(1)} %shard_map.83.refs_4_.first.own, f32[8,32,128]{2,1,0:T(8,128)S(1)} %collective-permute-done.11.other, f32[128,16]{1,0:T(8,128)S(1)} %shard_map.85.after.weight, ...), custom_call_target="tpu_custom_call" | custom-call | tf_op jit(solution)/shard_map/pallas_call | solution.py:43
  32.3 0.0 copy-start
  32.3 0.6 %copy-done = bf16[256,256]{1,0:T(8,128)(2,1)} copy-done((bf16[256,256]{1,0:T(8,128)(2,1)}, bf16[256,256]{1,0:T(8,128)(2,1)S(1)}, u32[]{:S(2)}) %copy-start) | copy-done | bytes 131096
  33.0 0.0 collective-permute-done.9.other
  33.0 0.9 %shard_map.90 = (bf16[384,256]{1,0:T(8,128)(2,1)S(1)}, bf16[384,256]{1,0:T(8,128)(2,1)S(1)}, f32[8,128]{1,0:T(8,128)S(1)}, f32[136,128]{1,0:T(8,128)S(1)}) custom-call(f32[8,48,128]{2,1,0:T(8,128)S(1)} %shard_map.84.after.second.own, f32[8,48,128]{2,1,0:T(8,128)S(1)} %collective-permute-done.9.other, f32[128,16]{1,0:T(8,128)S(1)} %shard_map.85.after.weight, ...), custom_call_target="tpu_custom_call" | custom-call | tf_op jit(solution)/shard_map/pallas_call | solution.py:43
  33.8 0.0 collective-permute-done.8.other
  33.8 0.4 shard_map.91.after
  34.3 0.1 collective-permute-start.12
  34.4 2.5 %collective-permute-start.14 = (f32[128,128]{1,0:T(8,128)S(1)}, f32[128,128]{1,0:T(8,128)S(1)}, u32[]{:S(2)}, u32[]{:S(2)}) collective-permute-start(f32[128,128]{1,0:T(8,128)S(1)} %add.10.after), channel_id=1, source_target_pairs={{0,2},{1,3},{2,0},{3,1},{4,6},{5,7},{6,4},{7,5},{8,10},{9,11},{10,... | collective-permute-start | bytes 196616 | tf_op jit(solution)/shard_map/ppermute | solution.py:710
  36.9 1.2 %collective-permute-start.13 = (f32[136,128]{1,0:T(8,128)S(1)}, f32[136,128]{1,0:T(8,128)S(1)}, u32[]{:S(2)}, u32[]{:S(2)}) collective-permute-start(f32[136,128]{1,0:T(8,128)S(1)} %add.11.rest_0_), channel_id=1, source_target_pairs={{0,2},{1,3},{2,0},{3,1},{4,6},{5,7},{6,4},{7,5},{8,10},{9,11},{10,... | collective-permute-start | bytes 208904 | tf_op jit(solution)/shard_map/ppermute | solution.py:710
  38.2 1.4 %collective-permute-done.14 = f32[128,128]{1,0:T(8,128)S(1)} collective-permute-done((f32[128,128]{1,0:T(8,128)S(1)}, f32[128,128]{1,0:T(8,128)S(1)}, u32[]{:S(2)}, u32[]{:S(2)}) %collective-permute-start.14) | collective-permute-done | bytes 65568 | tf_op jit(solution)/shard_map/ppermute | solution.py:710
  39.6 0.0 copy-start.1
  39.6 1.6 %collective-permute-start.15 = (f32[128,128]{1,0:T(8,128)S(1)}, f32[128,128]{1,0:T(8,128)S(1)}, u32[]{:S(2)}, u32[]{:S(2)}) collective-permute-start(f32[128,128]{1,0:T(8,128)S(1)} %add.12.rest_2_), channel_id=1, source_target_pairs={{0,16},{16,0},{1,17},{17,1},{2,18},{18,2},{3,19},{19,3},{4,20},{20... | collective-permute-start | bytes 196616 | tf_op jit(solution)/shard_map/ppermute | solution.py:691
  41.2 0.2 shard_map.92
  41.4 2.6 %collective-permute-done.15.rest_3_ = f32[128,128]{1,0:T(8,128)S(1)} collective-permute-done((f32[128,128]{1,0:T(8,128)S(1)}, f32[128,128]{1,0:T(8,128)S(1)}, u32[]{:S(2)}, u32[]{:S(2)}) %collective-permute-start.15) | collective-permute-done | bytes 65568 | tf_op jit(solution)/shard_map/ppermute | solution.py:691
  44.0 0.0 collective-permute-done.13.rest_1_
  44.0 4.7 %shard_map.93 = f32[1024,128]{1,0:T(8,128)} custom-call(f32[136,128]{1,0:T(8,128)S(1)} %add.11.rest_0_, f32[136,128]{1,0:T(8,128)S(1)} %collective-permute-done.13.rest_1_, f32[128,128]{1,0:T(8,128)S(1)} %add.12.rest_2_, f32[128,128]{1,0:T(8,128)S(1)} %collective-permute-done.15.rest_3_, bf16[256,256]{1,0:T(8,128)(2,1)S(1)} %copy-done.1, ...), custom_call_target="tpu_custom_call" | custom-call | tf_op jit(solution)/shard_map/pallas_call | solution.py:43
  (13 shorter events, 0.1 us)
Async XLA Ops:
  1.4 11.7 %collective-permute-start = (f32[208,128]{1,0:T(8,128)S(1)}, f32[208,128]{1,0:T(8,128)S(1)}, u32[]{:S(2)}, u32[]{:S(2)}) collective-permute-start(f32[208,128]{1,0:T(8,128)S(1)} %get-tuple-element.34), channel_id=1, source_target_pairs={{4,8},{12,0},{8,4},{0,12},{5,9},{13,1},{9,5},{1,13},{6,10},{14,2},... | collective-permute-start | bytes 319496 | tf_op jit(solution)/shard_map/ppermute | solution.py:700
  6.5 3.2 %collective-permute-start.4 = (f32[40,128]{1,0:T(8,128)S(1)}, f32[40,128]{1,0:T(8,128)S(1)}, u32[]{:S(2)}, u32[]{:S(2)}) collective-permute-start(f32[40,128]{1,0:T(8,128)S(1)} %get-tuple-element.38), channel_id=1, source_target_pairs={{0,1},{1,2},{2,3},{3,0},{4,5},{5,6},{6,7},{7,4},{8,9},{9,10},{10,1... | collective-permute-start | bytes 61448 | tf_op jit(solution)/shard_map/ppermute | solution.py:691
  6.5 7.5 %collective-permute-start.1 = (f32[208,128]{1,0:T(8,128)S(1)}, f32[208,128]{1,0:T(8,128)S(1)}, u32[]{:S(2)}, u32[]{:S(2)}) collective-permute-start(f32[208,128]{1,0:T(8,128)S(1)} %get-tuple-element.35), channel_id=1, source_target_pairs={{0,4},{8,12},{4,0},{12,8},{1,5},{9,13},{5,1},{13,9},{2,6},{10,14},... | collective-permute-start | bytes 319496 | tf_op jit(solution)/shard_map/ppermute | solution.py:700
  6.5 3.5 %collective-permute-start.5 = (f32[40,128]{1,0:T(8,128)S(1)}, f32[40,128]{1,0:T(8,128)S(1)}, u32[]{:S(2)}, u32[]{:S(2)}) collective-permute-start(f32[40,128]{1,0:T(8,128)S(1)} %get-tuple-element.39), channel_id=1, source_target_pairs={{0,3},{1,0},{2,1},{3,2},{4,7},{5,4},{6,5},{7,6},{8,11},{9,8},{10,9... | collective-permute-start | bytes 61448 | tf_op jit(solution)/shard_map/ppermute | solution.py:691
  8.3 7.5 %collective-permute-start.2 = (f32[192,128]{1,0:T(8,128)S(1)}, f32[192,128]{1,0:T(8,128)S(1)}, u32[]{:S(2)}, u32[]{:S(2)}) collective-permute-start(f32[192,128]{1,0:T(8,128)S(1)} %get-tuple-element.36), channel_id=1, source_target_pairs={{4,8},{12,0},{8,4},{0,12},{5,9},{13,1},{9,5},{1,13},{6,10},{14,2},... | collective-permute-start | bytes 294920 | tf_op jit(solution)/shard_map/ppermute | solution.py:700
  9.7 8.3 %collective-permute-start.3 = (f32[192,128]{1,0:T(8,128)S(1)}, f32[192,128]{1,0:T(8,128)S(1)}, u32[]{:S(2)}, u32[]{:S(2)}) collective-permute-start(f32[192,128]{1,0:T(8,128)S(1)} %get-tuple-element.37), channel_id=1, source_target_pairs={{0,4},{8,12},{4,0},{12,8},{1,5},{9,13},{5,1},{13,9},{2,6},{10,14},... | collective-permute-start | bytes 294920 | tf_op jit(solution)/shard_map/ppermute | solution.py:700
  10.0 10.9 %collective-permute-start.6 = (f32[168,128]{1,0:T(8,128)S(1)}, f32[168,128]{1,0:T(8,128)S(1)}, u32[]{:S(2)}, u32[]{:S(2)}) collective-permute-start(f32[168,128]{1,0:T(8,128)S(1)} %get-tuple-element.40), channel_id=1, source_target_pairs={{4,8},{12,0},{8,4},{0,12},{5,9},{13,1},{9,5},{1,13},{6,10},{14,2},... | collective-permute-start | bytes 258056 | tf_op jit(solution)/shard_map/ppermute | solution.py:700
  13.0 7.9 %collective-permute-start.7 = (f32[168,128]{1,0:T(8,128)S(1)}, f32[168,128]{1,0:T(8,128)S(1)}, u32[]{:S(2)}, u32[]{:S(2)}) collective-permute-start(f32[168,128]{1,0:T(8,128)S(1)} %get-tuple-element.41), channel_id=1, source_target_pairs={{0,4},{8,12},{4,0},{12,8},{1,5},{9,13},{5,1},{13,9},{2,6},{10,14},... | collective-permute-start | bytes 258056 | tf_op jit(solution)/shard_map/ppermute | solution.py:700
  14.6 5.9 %copy-start.4 = (s32[1,1024]{1,0:T(1,128)S(1)}, s32[1,1024]{1,0:T(1,128)}, u32[]{:S(2)}) copy-start(s32[1,1024]{1,0:T(1,128)} %cells.1) | copy-start | bytes 12292
  14.6 5.9 %copy-start.5 = (f32[1,1024]{1,0:T(1,128)S(1)}, f32[1,1024]{1,0:T(1,128)}, u32[]{:S(2)}) copy-start(f32[1,1024]{1,0:T(1,128)} %values.1) | copy-start | bytes 12292
  14.7 5.9 %copy-start.6 = (f32[1,1024]{1,0:T(1,128)S(1)}, f32[1,1024]{1,0:T(1,128)}, u32[]{:S(2)}) copy-start(f32[1,1024]{1,0:T(1,128)} %weights.1) | copy-start | bytes 12292
  18.9 14.0 %collective-permute-start.9 = (f32[8,48,128]{2,1,0:T(8,128)S(1)}, f32[8,48,128]{2,1,0:T(8,128)S(1)}, u32[]{:S(2)}, u32[]{:S(2)}) collective-permute-start(f32[8,48,128]{2,1,0:T(8,128)S(1)} %shard_map.84.after.second.own), channel_id=1, source_target_pairs={{0,16},{16,0},{1,17},{17,1},{2,18},{18,2},{3,19},{19,3},{4,20},{20... | collective-permute-start | bytes 589832 | tf_op jit(solution)/shard_map/ppermute | solution.py:691
  22.1 11.8 %collective-permute-start.8 = (f32[8,48,128]{2,1,0:T(8,128)S(1)}, f32[8,48,128]{2,1,0:T(8,128)S(1)}, u32[]{:S(2)}, u32[]{:S(2)}) collective-permute-start(f32[8,48,128]{2,1,0:T(8,128)S(1)} %shard_map.87.sides.own), channel_id=1, source_target_pairs={{0,16},{16,0},{1,17},{17,1},{2,18},{18,2},{3,19},{19,3},{4,20},{20... | collective-permute-start | bytes 589832 | tf_op jit(solution)/shard_map/ppermute | solution.py:691
  23.0 8.7 %collective-permute-start.11 = (f32[8,32,128]{2,1,0:T(8,128)S(1)}, f32[8,32,128]{2,1,0:T(8,128)S(1)}, u32[]{:S(2)}, u32[]{:S(2)}) collective-permute-start(f32[8,32,128]{2,1,0:T(8,128)S(1)} %shard_map.83.refs_4_.first.own), channel_id=1, source_target_pairs={{0,16},{16,0},{1,17},{17,1},{2,18},{18,2},{3,19},{19,3},{4,20},{20... | collective-permute-start | bytes 393224 | tf_op jit(solution)/shard_map/ppermute | solution.py:691
  25.2 1.3 %collective-permute-start.10 = (f32[128,128]{1,0:T(8,128)S(1)}, f32[128,128]{1,0:T(8,128)S(1)}, u32[]{:S(2)}, u32[]{:S(2)}) collective-permute-start(f32[128,128]{1,0:T(8,128)S(1)} %get-tuple-element.45), channel_id=1, source_target_pairs={{0,1},{1,0},{2,3},{3,2},{4,5},{5,4},{6,7},{7,6},{8,9},{9,8},{10,11... | collective-permute-start | bytes 196616 | tf_op jit(solution)/shard_map/ppermute | solution.py:710
  32.3 0.7 %copy-start = (bf16[256,256]{1,0:T(8,128)(2,1)}, bf16[256,256]{1,0:T(8,128)(2,1)S(1)}, u32[]{:S(2)}) copy-start(bf16[256,256]{1,0:T(8,128)(2,1)S(1)} %get-tuple-element.50.rest_4_) | copy-start | bytes 393220
  33.0 0.9 %copy-start.2 = (bf16[256,256]{1,0:T(8,128)(2,1)}, bf16[256,256]{1,0:T(8,128)(2,1)S(1)}, u32[]{:S(2)}) copy-start(bf16[256,256]{1,0:T(8,128)(2,1)S(1)} %get-tuple-element.53.rest_7_) | copy-start | bytes 393220
  34.3 2.6 %collective-permute-start.12 = (f32[136,128]{1,0:T(8,128)S(1)}, f32[136,128]{1,0:T(8,128)S(1)}, u32[]{:S(2)}, u32[]{:S(2)}) collective-permute-start(f32[136,128]{1,0:T(8,128)S(1)} %shard_map.91.after), channel_id=1, source_target_pairs={{0,1},{1,0},{2,3},{3,2},{4,5},{5,4},{6,7},{7,6},{8,9},{9,8},{10,11... | collective-permute-start | bytes 208904 | tf_op jit(solution)/shard_map/ppermute | solution.py:710
  34.4 5.2 %collective-permute-start.14 = (f32[128,128]{1,0:T(8,128)S(1)}, f32[128,128]{1,0:T(8,128)S(1)}, u32[]{:S(2)}, u32[]{:S(2)}) collective-permute-start(f32[128,128]{1,0:T(8,128)S(1)} %add.10.after), channel_id=1, source_target_pairs={{0,2},{1,3},{2,0},{3,1},{4,6},{5,7},{6,4},{7,5},{8,10},{9,11},{10,... | collective-permute-start | bytes 196616 | tf_op jit(solution)/shard_map/ppermute | solution.py:710
  36.9 7.0 %collective-permute-start.13 = (f32[136,128]{1,0:T(8,128)S(1)}, f32[136,128]{1,0:T(8,128)S(1)}, u32[]{:S(2)}, u32[]{:S(2)}) collective-permute-start(f32[136,128]{1,0:T(8,128)S(1)} %add.11.rest_0_), channel_id=1, source_target_pairs={{0,2},{1,3},{2,0},{3,1},{4,6},{5,7},{6,4},{7,5},{8,10},{9,11},{10,... | collective-permute-start | bytes 208904 | tf_op jit(solution)/shard_map/ppermute | solution.py:710
  39.6 4.4 %copy-start.1 = (bf16[256,256]{1,0:T(8,128)(2,1)S(1)}, bf16[256,256]{1,0:T(8,128)(2,1)}, u32[]{:S(2)}) copy-start(bf16[256,256]{1,0:T(8,128)(2,1)} %copy-done) | copy-start | bytes 393220
  39.6 4.3 %copy-start.3 = (bf16[256,256]{1,0:T(8,128)(2,1)S(1)}, bf16[256,256]{1,0:T(8,128)(2,1)}, u32[]{:S(2)}) copy-start(bf16[256,256]{1,0:T(8,128)(2,1)} %copy-done.2) | copy-start | bytes 393220
  39.6 4.3 %collective-permute-start.15 = (f32[128,128]{1,0:T(8,128)S(1)}, f32[128,128]{1,0:T(8,128)S(1)}, u32[]{:S(2)}, u32[]{:S(2)}) collective-permute-start(f32[128,128]{1,0:T(8,128)S(1)} %add.12.rest_2_), channel_id=1, source_target_pairs={{0,16},{16,0},{1,17},{17,1},{2,18},{18,2},{3,19},{19,3},{4,20},{20... | collective-permute-start | bytes 196616 | tf_op jit(solution)/shard_map/ppermute | solution.py:691

commit v8 on v5

--- a/solution.py
+++ b/solution.py
@@ -83,7 +83,7 @@
 
 
 def parted(cols):
-    return cols * 7 // 16 // 8 * 8, cols * 13 // 16 // 8 * 8
+    return cols * 3 // 8 // 8 * 8, cols * 3 // 4 // 8 * 8
 
 
 def parity(axis):
@@ -447,7 +447,7 @@
     loop(rows // many, block)
 
 
-def own_gram_kernel(layout, first, second, sides, weight, total, left, right, spread):
+def own_gram_kernel(layout, first, second, sides, weight, total):
     local = total.shape[0]
     total[...] = jnp.zeros_like(total)
     for pieces, own in zip(layout, (first, second, sides)):
@@ -459,16 +459,28 @@
             value = cells_of(own, b, many)
             mean = lane_mean(value)
             deviation = value - mean
-            plain, valued = cell_weights(rows, pieces, weight, b, many)
+            plain, _ = cell_weights(rows, pieces, weight, b, many)
             turned = halves((deviation * plain).T)
             total[...] += dot_wide(turned, wide(halves(deviation)), local)
-            if own is sides:
-                at = pl.ds(b * depth, depth)
-                left[:, at], right[:, at] = turned
-                for i, column in enumerate((plain, valued, mean)):
-                    spread[i, at] = jnp.broadcast_to(column, (depth, local))
 
         loop(rows // many, block)
+
+
+def prepare_kernel(pieces, own, weight, after, left, right, spread):
+    rows, size, local = own.shape
+    many = grouping(rows)
+    depth = many * size
+
+    def block(b):
+        value = cells_of(own, b, many)
+        mean = lane_mean(value)
+        plain, valued = cell_weights(rows, pieces, weight, b, many)
+        at = pl.ds(b * depth, depth)
+        left[:, at], right[:, at] = halves(((value - mean) * plain).T)
+        for i, column in enumerate((plain, valued, mean)):
+            spread[i, at] = jnp.broadcast_to(column, (depth, local))
+
+    loop(rows // many, block)
 
 
 def tally(total, local, value, partner, plain, valued, mean_own):
@@ -841,14 +853,18 @@
     if pair:
         sided = rows * sides.shape[1]
         half = struct(local, sided, kind=jnp.bfloat16)
-        alone, left_half, right_half, spread = call(
-            functools.partial(own_gram_kernel, layout),
-            (struct(local, local), half, half, struct(3, sided, local)),
-            *owns,
-            weight,
+        alone = call(
+            functools.partial(own_gram_kernel, layout), struct(local, local), *owns, weight
         )
         stages = role_sums(alone)
         started = sum(stages[0])
+        left_half, right_half, spread = call(
+            functools.partial(prepare_kernel, layout[-1]),
+            (half, half, struct(3, sided, local)),
+            sides,
+            weight,
+            started,
+        )
         cross = struct(local + 8, local)
         total = ()
         for i in range(2):

time: 46.6 us -> 48.1 us (1.032)
  starting transfers between devices: 18.8 us -> 20.3 us
  local copies, waits for them, and re-layouts: 0.68 us -> 0.01 us
    ppermute x6, starting transfers between devices: 5.27 us -> 7 us  [shift(): return lax.ppermute(value, axes if len(axes) > 1 else axes[0], pairs)]
    ppermute x6, waiting for transfers between devices: 1.6 us -> 2.97 us  [trade(): return lax.ppermute(value, axis, pairs + [(j, i) for i, j in pairs])]
    ppermute x6, waiting for transfers between devices: 9.39 us -> 8.41 us  [shift(): return lax.ppermute(value, axes if len(axes) > 1 else axes[0], pairs)]
    ppermute x6, starting transfers between devices: 10.2 us -> 9.33 us  [trade(): return lax.ppermute(value, axis, pairs + [(j, i) for i, j in pairs])]
    unnamed x10 -> x6, local copies, waits for them, and re-layouts: 0.68 us -> 0.01 us
    ppermute x4, starting transfers between devices: 3.41 us -> 3.93 us  [role_sums(): other = lax.ppermute(value, 'role', [(i, i ^ step) for i in range(size)])]
    pallas_call x12 -> x13, Pallas kernels: 12.4 us -> 12.8 us  [call(): pl.pallas_call(body, out_shape=outs, in_specs=[SMEM] * scalars + [VMEM] *...]
  transfers between devices with their start and end apart: 16 -> 16, of which waited for: 8 -> 7; matrix products, arithmetic and copies ran while one was open for 0% -> 0% of each run, Pallas kernels for 13% -> 13%
where the time goes in v8:
time: 48.1 us; the launch traced here: 48 us
  starting transfers between devices  20.3 us (42%)
  waiting for transfers between devices  14.1 us (29%)
  Pallas kernels  12.8 us (27%)
  between operations  0.82 us (2%)
    pallas_call x13, Pallas kernels, call(): pl.pallas_call(body, out_shape=outs, in_specs=[SMEM] * scalars + [VMEM] *...  12.8 us
    ppermute x6, starting transfers between devices, trade(): return lax.ppermute(value, axis, pairs + [(j, i) for i, j in pairs])  9.33 us
    ppermute x6, waiting for transfers between devices, shift(): return lax.ppermute(value, axes if len(axes) > 1 else axes[0], pairs)  8.41 us
    ppermute x6, starting transfers between devices, shift(): return lax.ppermute(value, axes if len(axes) > 1 else axes[0], pairs)  7 us
    ppermute x4, starting transfers between devices, role_sums(): other = lax.ppermute(value, 'role', [(i, i ^ step) for i in range(size)])  3.93 us
    ppermute x6, waiting for transfers between devices, trade(): return lax.ppermute(value, axis, pairs + [(j, i) for i, j in pairs])  2.97 us
    ppermute x4, waiting for transfers between devices, role_sums(): other = lax.ppermute(value, 'role', [(i, i ^ step) for i in range(size)])  2.67 us
  transfers between devices with their start and end apart: 16, of which 7 were waited for; matrix products, arithmetic and copies ran while one was open for 0% of the time, Pallas kernels for 13%

profile of v8, /device:TPU:0, one launch (start us, length us, event | category | flops | bytes accessed | tf_op | source)
XLA Modules:
  0.0 48.0 jit_solution(17551989530450888643)
XLA Ops:
  0.0 1.3 %shard_map.83 = (f32[8,128,128]{2,1,0:T(8,128)S(1)}, f32[3,8,128]{2,1,0:T(8,128)S(1)}, f32[208,128]{1,0:T(8,128)S(1)}, f32[208,128]{1,0:T(8,128)S(1)}, f32[192,1...) custom-call(f32[1024,128]{1,0:T(8,128)} %bitcast.2, ...), custom_call_target="tpu_custom_call" | custom-call | tf_op jit(solution)/shard_map/pallas_call | solution.py:43
  1.4 0.0 copy-start.2
  1.4 5.1 %collective-permute-start = (f32[208,128]{1,0:T(8,128)S(1)}, f32[208,128]{1,0:T(8,128)S(1)}, u32[]{:S(2)}, u32[]{:S(2)}) collective-permute-start(f32[208,128]{1,0:T(8,128)S(1)} %get-tuple-element.33), channel_id=1, source_target_pairs={{4,8},{12,0},{8,4},{0,12},{5,9},{13,1},{9,5},{1,13},{6,10},{14,2},... | collective-permute-start | bytes 319496 | tf_op jit(solution)/shard_map/ppermute | solution.py:712
  6.5 0.0 collective-permute-start.4
  6.5 0.0 collective-permute-start.1
  6.5 1.7 %collective-permute-start.5 = (f32[40,128]{1,0:T(8,128)S(1)}, f32[40,128]{1,0:T(8,128)S(1)}, u32[]{:S(2)}, u32[]{:S(2)}) collective-permute-start(f32[40,128]{1,0:T(8,128)S(1)} %get-tuple-element.38), channel_id=1, source_target_pairs={{0,3},{1,0},{2,1},{3,2},{4,7},{5,4},{6,5},{7,6},{8,11},{9,8},{10,9... | collective-permute-start | bytes 61448 | tf_op jit(solution)/shard_map/ppermute | solution.py:703
  8.3 0.6 %collective-permute-start.2 = (f32[192,128]{1,0:T(8,128)S(1)}, f32[192,128]{1,0:T(8,128)S(1)}, u32[]{:S(2)}, u32[]{:S(2)}) collective-permute-start(f32[192,128]{1,0:T(8,128)S(1)} %get-tuple-element.35), channel_id=1, source_target_pairs={{4,8},{12,0},{8,4},{0,12},{5,9},{13,1},{9,5},{1,13},{6,10},{14,2},... | collective-permute-start | bytes 294920 | tf_op jit(solution)/shard_map/ppermute | solution.py:712
  8.9 0.8 %collective-permute-done.4.left = f32[40,128]{1,0:T(8,128)S(1)} collective-permute-done((f32[40,128]{1,0:T(8,128)S(1)}, f32[40,128]{1,0:T(8,128)S(1)}, u32[]{:S(2)}, u32[]{:S(2)}) %collective-permute-start.4) | collective-permute-done | bytes 20512 | tf_op jit(solution)/shard_map/ppermute | solution.py:703
  9.7 0.3 collective-permute-start.3
  10.7 0.0 copy-done.2
  10.7 0.0 copy-done.1
  10.7 0.0 copy-done
  10.7 0.4 shard_map.82.after.weight
  11.1 0.0 collective-permute-done.5.right
  11.1 3.0 %collective-permute-start.6 = (f32[168,128]{1,0:T(8,128)S(1)}, f32[168,128]{1,0:T(8,128)S(1)}, u32[]{:S(2)}, u32[]{:S(2)}) collective-permute-start(f32[168,128]{1,0:T(8,128)S(1)} %get-tuple-element.39), channel_id=1, source_target_pairs={{4,8},{12,0},{8,4},{0,12},{5,9},{13,1},{9,5},{1,13},{6,10},{14,2},... | collective-permute-start | bytes 258056 | tf_op jit(solution)/shard_map/ppermute | solution.py:712
  14.1 0.0 collective-permute-done.refs_0_.early
  14.1 0.3 collective-permute-start.7
  14.4 0.0 collective-permute-done.1.refs_1_.late
  14.4 0.7 %shard_map.84.after.first.own = f32[8,32,128]{2,1,0:T(8,128)S(1)} custom-call(f32[128,16]{1,0:T(8,128)S(1)} %shard_map.82.after.weight, f32[8,128,128]{2,1,0:T(8,128)S(1)} %get-tuple-element.31.field, f32[3,8,128]{2,1,0:T(8,128)S(1)} %get-tuple-element.32.kept, f32[208,128]{1,0:T(8,128)S(1)} %collective-permute-done.refs_0_.early, ...), custom_call_target="tpu_custom_call" | custom-call | tf_op jit(solution)/shard_map/pallas_call | solution.py:43
  15.1 0.6 %collective-permute-done.2.refs_2_.early_next = f32[192,128]{1,0:T(8,128)S(1)} collective-permute-done((f32[192,128]{1,0:T(8,128)S(1)}, f32[192,128]{1,0:T(8,128)S(1)}, u32[]{:S(2)}, u32[]{:S(2)}) %collective-permute-start.2) | collective-permute-done | bytes 98336 | tf_op jit(solution)/shard_map/ppermute | solution.py:712
  15.7 2.3 %collective-permute-done.3.refs_3_.late_next = f32[192,128]{1,0:T(8,128)S(1)} collective-permute-done((f32[192,128]{1,0:T(8,128)S(1)}, f32[192,128]{1,0:T(8,128)S(1)}, u32[]{:S(2)}, u32[]{:S(2)}) %collective-permute-start.3) | collective-permute-done | bytes 98336 | tf_op jit(solution)/shard_map/ppermute | solution.py:712
  18.1 0.9 %shard_map.85.after.second.own = f32[8,48,128]{2,1,0:T(8,128)S(1)} custom-call(f32[8,32,128]{2,1,0:T(8,128)S(1)} %shard_map.84.after.first.own, f32[8,128,128]{2,1,0:T(8,128)S(1)} %get-tuple-element.31.field, f32[3,8,128]{2,1,0:T(8,128)S(1)} %get-tuple-element.32.kept, f32[208,128]{1,0:T(8,128)S(1)} %collective-permute-done.refs_0_.early, ...), custom_call_target="tpu_custom_call" | custom-call | tf_op jit(solution)/shard_map/pallas_call | solution.py:43
  18.9 1.6 %collective-permute-start.10 = (f32[8,48,128]{2,1,0:T(8,128)S(1)}, f32[8,48,128]{2,1,0:T(8,128)S(1)}, u32[]{:S(2)}, u32[]{:S(2)}) collective-permute-start(f32[8,48,128]{2,1,0:T(8,128)S(1)} %shard_map.85.after.second.own), channel_id=1, source_target_pairs={{0,16},{16,0},{1,17},{17,1},{2,18},{18,2},{3,19},{19,3},{4,20},{20... | collective-permute-start | bytes 589832 | tf_op jit(solution)/shard_map/ppermute | solution.py:703
  20.5 0.0 collective-permute-done.6.early_rest
  20.5 0.0 collective-permute-done.7.late_rest
  20.5 1.1 %shard_map.87.sides.own = f32[8,48,128]{2,1,0:T(8,128)S(1)} custom-call(f32[8,48,128]{2,1,0:T(8,128)S(1)} %shard_map.85.after.second.own, f32[8,128,128]{2,1,0:T(8,128)S(1)} %get-tuple-element.31.field, f32[3,8,128]{2,1,0:T(8,128)S(1)} %get-tuple-element.32.kept, f32[208,128]{1,0:T(8,128)S(1)} %collective-permute-done.refs_0_.early, ...), custom_call_target="tpu_custom_call" | custom-call | tf_op jit(solution)/shard_map/pallas_call | solution.py:43
  21.7 1.3 %collective-permute-start.8 = (f32[8,48,128]{2,1,0:T(8,128)S(1)}, f32[8,48,128]{2,1,0:T(8,128)S(1)}, u32[]{:S(2)}, u32[]{:S(2)}) collective-permute-start(f32[8,48,128]{2,1,0:T(8,128)S(1)} %shard_map.87.sides.own), channel_id=1, source_target_pairs={{0,16},{16,0},{1,17},{17,1},{2,18},{18,2},{3,19},{19,3},{4,20},{20... | collective-permute-start | bytes 589832 | tf_op jit(solution)/shard_map/ppermute | solution.py:703
  23.0 0.8 %collective-permute-start.11 = (f32[8,32,128]{2,1,0:T(8,128)S(1)}, f32[8,32,128]{2,1,0:T(8,128)S(1)}, u32[]{:S(2)}, u32[]{:S(2)}) collective-permute-start(f32[8,32,128]{2,1,0:T(8,128)S(1)} %shard_map.84.after.first.own), channel_id=1, source_target_pairs={{0,16},{16,0},{1,17},{17,1},{2,18},{18,2},{3,19},{19,3},{4,20},{20... | collective-permute-start | bytes 393224 | tf_op jit(solution)/shard_map/ppermute | solution.py:703
  23.7 1.1 %shard_map.88 = f32[128,128]{1,0:T(8,128)S(1)} custom-call(f32[8,32,128]{2,1,0:T(8,128)S(1)} %shard_map.84.after.first.own, f32[8,48,128]{2,1,0:T(8,128)S(1)} %shard_map.85.after.second.own, f32[8,48,128]{2,1,0:T(8,128)S(1)} %shard_map.87.sides.own, f32[128,16]{1,0:T(8,128)S(1)} %shard_map.82.after.weight), custom_call_target="tpu_custom_call" | custom-call | tf_op jit(solution)/shard_map/pallas_call | solution.py:43
  24.8 0.1 collective-permute-start.9
  24.9 1.2 %collective-permute-done.9 = f32[128,128]{1,0:T(8,128)S(1)} collective-permute-done((f32[128,128]{1,0:T(8,128)S(1)}, f32[128,128]{1,0:T(8,128)S(1)}, u32[]{:S(2)}, u32[]{:S(2)}) %collective-permute-start.9) | collective-permute-done | bytes 65568 | tf_op jit(solution)/shard_map/ppermute | solution.py:722
  26.1 0.6 %shard_map.89 = (bf16[128,384]{1,0:T(8,128)(2,1)S(1)}, bf16[128,384]{1,0:T(8,128)(2,1)S(1)}, f32[3,384,128]{2,1,0:T(8,128)S(1)}) custom-call(f32[8,48,128]{2,1,0:T(8,128)S(1)} %shard_map.87.sides.own, f32[128,16]{1,0:T(8,128)S(1)} %shard_map.82.after.weight, f32[128,128]{1,0:T(8,128)S(1)} %add.10.after), custom_call_target="tpu_custom_call" | custom-call | tf_op jit(solution)/shard_map/pallas_call | solution.py:43
  26.7 5.0 %collective-permute-done.11.other = f32[8,32,128]{2,1,0:T(8,128)S(1)} collective-permute-done((f32[8,32,128]{2,1,0:T(8,128)S(1)}, f32[8,32,128]{2,1,0:T(8,128)S(1)}, u32[]{:S(2)}, u32[]{:S(2)}) %collective-permute-start.11) | collective-permute-done | bytes 131104 | tf_op jit(solution)/shard_map/ppermute | solution.py:703
  31.7 0.6 %shard_map.90 = (bf16[256,256]{1,0:T(8,128)(2,1)S(1)}, bf16[256,256]{1,0:T(8,128)(2,1)S(1)}, f32[8,128]{1,0:T(8,128)S(1)}, f32[136,128]{1,0:T(8,128)S(1)}) custom-call(f32[8,32,128]{2,1,0:T(8,128)S(1)} %shard_map.84.after.first.own, f32[8,32,128]{2,1,0:T(8,128)S(1)} %collective-permute-done.11.other, f32[128,16]{1,0:T(8,128)S(1)} %shard_map.82.after.weight, ...), custom_call_target="tpu_custom_call" | custom-call | tf_op jit(solution)/shard_map/pallas_call | solution.py:43
  32.3 0.0 collective-permute-done.10.other
  32.3 0.8 %shard_map.91 = (bf16[384,256]{1,0:T(8,128)(2,1)S(1)}, bf16[384,256]{1,0:T(8,128)(2,1)S(1)}, f32[8,128]{1,0:T(8,128)S(1)}, f32[136,128]{1,0:T(8,128)S(1)}) custom-call(f32[8,48,128]{2,1,0:T(8,128)S(1)} %shard_map.85.after.second.own, f32[8,48,128]{2,1,0:T(8,128)S(1)} %collective-permute-done.10.other, f32[128,16]{1,0:T(8,128)S(1)} %shard_map.82.after.weight, ...), custom_call_target="tpu_custom_call" | custom-call | tf_op jit(solution)/shard_map/pallas_call | solution.py:43
  33.2 0.0 collective-permute-done.8.other
  33.2 0.4 shard_map.92.after
  33.6 0.1 collective-permute-start.12
  33.7 2.5 %collective-permute-start.14 = (f32[128,128]{1,0:T(8,128)S(1)}, f32[128,128]{1,0:T(8,128)S(1)}, u32[]{:S(2)}, u32[]{:S(2)}) collective-permute-start(f32[128,128]{1,0:T(8,128)S(1)} %add.10.after), channel_id=1, source_target_pairs={{0,2},{1,3},{2,0},{3,1},{4,6},{5,7},{6,4},{7,5},{8,10},{9,11},{10,... | collective-permute-start | bytes 196616 | tf_op jit(solution)/shard_map/ppermute | solution.py:722
  36.2 0.0 collective-permute-done.12
  36.3 1.2 %collective-permute-start.13 = (f32[136,128]{1,0:T(8,128)S(1)}, f32[136,128]{1,0:T(8,128)S(1)}, u32[]{:S(2)}, u32[]{:S(2)}) collective-permute-start(f32[136,128]{1,0:T(8,128)S(1)} %add.11.rest_0_), channel_id=1, source_target_pairs={{0,2},{1,3},{2,0},{3,1},{4,6},{5,7},{6,4},{7,5},{8,10},{9,11},{10,... | collective-permute-start | bytes 208904 | tf_op jit(solution)/shard_map/ppermute | solution.py:722
  37.5 1.4 %collective-permute-done.14 = f32[128,128]{1,0:T(8,128)S(1)} collective-permute-done((f32[128,128]{1,0:T(8,128)S(1)}, f32[128,128]{1,0:T(8,128)S(1)}, u32[]{:S(2)}, u32[]{:S(2)}) %collective-permute-start.14) | collective-permute-done | bytes 65568 | tf_op jit(solution)/shard_map/ppermute | solution.py:722
  38.9 1.6 %collective-permute-start.15 = (f32[128,128]{1,0:T(8,128)S(1)}, f32[128,128]{1,0:T(8,128)S(1)}, u32[]{:S(2)}, u32[]{:S(2)}) collective-permute-start(f32[128,128]{1,0:T(8,128)S(1)} %add.12.rest_2_), channel_id=1, source_target_pairs={{0,16},{16,0},{1,17},{17,1},{2,18},{18,2},{3,19},{19,3},{4,20},{20... | collective-permute-start | bytes 196616 | tf_op jit(solution)/shard_map/ppermute | solution.py:703
  40.5 0.2 shard_map.93
  40.7 2.6 %collective-permute-done.15.rest_3_ = f32[128,128]{1,0:T(8,128)S(1)} collective-permute-done((f32[128,128]{1,0:T(8,128)S(1)}, f32[128,128]{1,0:T(8,128)S(1)}, u32[]{:S(2)}, u32[]{:S(2)}) %collective-permute-start.15) | collective-permute-done | bytes 65568 | tf_op jit(solution)/shard_map/ppermute | solution.py:703
  43.3 0.0 collective-permute-done.13.rest_1_
  43.3 4.7 %shard_map.94 = f32[1024,128]{1,0:T(8,128)} custom-call(f32[136,128]{1,0:T(8,128)S(1)} %add.11.rest_0_, f32[136,128]{1,0:T(8,128)S(1)} %collective-permute-done.13.rest_1_, f32[128,128]{1,0:T(8,128)S(1)} %add.12.rest_2_, f32[128,128]{1,0:T(8,128)S(1)} %collective-permute-done.15.rest_3_, bf16[256,256]{1,0:T(8,128)(2,1)S(1)} %get-tuple-element.48.rest_4_, ...), custom_call_target="tpu_custom_call" | custom-call | tf_op jit(solution)/shard_map/pallas_call | solution.py:43
  (6 shorter events, 0.1 us)
Async XLA Ops:
  1.4 9.3 %copy-start.2 = (f32[1,1024]{1,0:T(1,128)S(1)}, f32[1,1024]{1,0:T(1,128)}, u32[]{:S(2)}) copy-start(f32[1,1024]{1,0:T(1,128)} %weights.1) | copy-start | bytes 12292
  1.4 12.8 %collective-permute-start = (f32[208,128]{1,0:T(8,128)S(1)}, f32[208,128]{1,0:T(8,128)S(1)}, u32[]{:S(2)}, u32[]{:S(2)}) collective-permute-start(f32[208,128]{1,0:T(8,128)S(1)} %get-tuple-element.33), channel_id=1, source_target_pairs={{4,8},{12,0},{8,4},{0,12},{5,9},{13,1},{9,5},{1,13},{6,10},{14,2},... | collective-permute-start | bytes 319496 | tf_op jit(solution)/shard_map/ppermute | solution.py:712
  6.5 3.2 %collective-permute-start.4 = (f32[40,128]{1,0:T(8,128)S(1)}, f32[40,128]{1,0:T(8,128)S(1)}, u32[]{:S(2)}, u32[]{:S(2)}) collective-permute-start(f32[40,128]{1,0:T(8,128)S(1)} %get-tuple-element.37), channel_id=1, source_target_pairs={{0,1},{1,2},{2,3},{3,0},{4,5},{5,6},{6,7},{7,4},{8,9},{9,10},{10,1... | collective-permute-start | bytes 61448 | tf_op jit(solution)/shard_map/ppermute | solution.py:703
  6.5 4.2 %copy-start.1 = (f32[1,1024]{1,0:T(1,128)S(1)}, f32[1,1024]{1,0:T(1,128)}, u32[]{:S(2)}) copy-start(f32[1,1024]{1,0:T(1,128)} %values.1) | copy-start | bytes 12292
  6.5 4.2 %copy-start = (s32[1,1024]{1,0:T(1,128)S(1)}, s32[1,1024]{1,0:T(1,128)}, u32[]{:S(2)}) copy-start(s32[1,1024]{1,0:T(1,128)} %cells.1) | copy-start | bytes 12292
  6.5 7.9 %collective-permute-start.1 = (f32[208,128]{1,0:T(8,128)S(1)}, f32[208,128]{1,0:T(8,128)S(1)}, u32[]{:S(2)}, u32[]{:S(2)}) collective-permute-start(f32[208,128]{1,0:T(8,128)S(1)} %get-tuple-element.34), channel_id=1, source_target_pairs={{0,4},{8,12},{4,0},{12,8},{1,5},{9,13},{5,1},{13,9},{2,6},{10,14},... | collective-permute-start | bytes 319496 | tf_op jit(solution)/shard_map/ppermute | solution.py:712
  6.5 4.6 %collective-permute-start.5 = (f32[40,128]{1,0:T(8,128)S(1)}, f32[40,128]{1,0:T(8,128)S(1)}, u32[]{:S(2)}, u32[]{:S(2)}) collective-permute-start(f32[40,128]{1,0:T(8,128)S(1)} %get-tuple-element.38), channel_id=1, source_target_pairs={{0,3},{1,0},{2,1},{3,2},{4,7},{5,4},{6,5},{7,6},{8,11},{9,8},{10,9... | collective-permute-start | bytes 61448 | tf_op jit(solution)/shard_map/ppermute | solution.py:703
  8.3 7.5 %collective-permute-start.2 = (f32[192,128]{1,0:T(8,128)S(1)}, f32[192,128]{1,0:T(8,128)S(1)}, u32[]{:S(2)}, u32[]{:S(2)}) collective-permute-start(f32[192,128]{1,0:T(8,128)S(1)} %get-tuple-element.35), channel_id=1, source_target_pairs={{4,8},{12,0},{8,4},{0,12},{5,9},{13,1},{9,5},{1,13},{6,10},{14,2},... | collective-permute-start | bytes 294920 | tf_op jit(solution)/shard_map/ppermute | solution.py:712
  9.7 8.3 %collective-permute-start.3 = (f32[192,128]{1,0:T(8,128)S(1)}, f32[192,128]{1,0:T(8,128)S(1)}, u32[]{:S(2)}, u32[]{:S(2)}) collective-permute-start(f32[192,128]{1,0:T(8,128)S(1)} %get-tuple-element.36), channel_id=1, source_target_pairs={{0,4},{8,12},{4,0},{12,8},{1,5},{9,13},{5,1},{13,9},{2,6},{10,14},... | collective-permute-start | bytes 294920 | tf_op jit(solution)/shard_map/ppermute | solution.py:712
  11.1 9.4 %collective-permute-start.6 = (f32[168,128]{1,0:T(8,128)S(1)}, f32[168,128]{1,0:T(8,128)S(1)}, u32[]{:S(2)}, u32[]{:S(2)}) collective-permute-start(f32[168,128]{1,0:T(8,128)S(1)} %get-tuple-element.39), channel_id=1, source_target_pairs={{4,8},{12,0},{8,4},{0,12},{5,9},{13,1},{9,5},{1,13},{6,10},{14,2},... | collective-permute-start | bytes 258056 | tf_op jit(solution)/shard_map/ppermute | solution.py:712
  14.1 6.4 %collective-permute-start.7 = (f32[168,128]{1,0:T(8,128)S(1)}, f32[168,128]{1,0:T(8,128)S(1)}, u32[]{:S(2)}, u32[]{:S(2)}) collective-permute-start(f32[168,128]{1,0:T(8,128)S(1)} %get-tuple-element.40), channel_id=1, source_target_pairs={{0,4},{8,12},{4,0},{12,8},{1,5},{9,13},{5,1},{13,9},{2,6},{10,14},... | collective-permute-start | bytes 258056 | tf_op jit(solution)/shard_map/ppermute | solution.py:712
  18.9 13.4 %collective-permute-start.10 = (f32[8,48,128]{2,1,0:T(8,128)S(1)}, f32[8,48,128]{2,1,0:T(8,128)S(1)}, u32[]{:S(2)}, u32[]{:S(2)}) collective-permute-start(f32[8,48,128]{2,1,0:T(8,128)S(1)} %shard_map.85.after.second.own), channel_id=1, source_target_pairs={{0,16},{16,0},{1,17},{17,1},{2,18},{18,2},{3,19},{19,3},{4,20},{20... | collective-permute-start | bytes 589832 | tf_op jit(solution)/shard_map/ppermute | solution.py:703
  21.7 11.5 %collective-permute-start.8 = (f32[8,48,128]{2,1,0:T(8,128)S(1)}, f32[8,48,128]{2,1,0:T(8,128)S(1)}, u32[]{:S(2)}, u32[]{:S(2)}) collective-permute-start(f32[8,48,128]{2,1,0:T(8,128)S(1)} %shard_map.87.sides.own), channel_id=1, source_target_pairs={{0,16},{16,0},{1,17},{17,1},{2,18},{18,2},{3,19},{19,3},{4,20},{20... | collective-permute-start | bytes 589832 | tf_op jit(solution)/shard_map/ppermute | solution.py:703
  23.0 8.7 %collective-permute-start.11 = (f32[8,32,128]{2,1,0:T(8,128)S(1)}, f32[8,32,128]{2,1,0:T(8,128)S(1)}, u32[]{:S(2)}, u32[]{:S(2)}) collective-permute-start(f32[8,32,128]{2,1,0:T(8,128)S(1)} %shard_map.84.after.first.own), channel_id=1, source_target_pairs={{0,16},{16,0},{1,17},{17,1},{2,18},{18,2},{3,19},{19,3},{4,20},{20... | collective-permute-start | bytes 393224 | tf_op jit(solution)/shard_map/ppermute | solution.py:703
  24.8 1.3 %collective-permute-start.9 = (f32[128,128]{1,0:T(8,128)S(1)}, f32[128,128]{1,0:T(8,128)S(1)}, u32[]{:S(2)}, u32[]{:S(2)}) collective-permute-start(f32[128,128]{1,0:T(8,128)S(1)} %shard_map.88), channel_id=1, source_target_pairs={{0,1},{1,0},{2,3},{3,2},{4,5},{5,4},{6,7},{7,6},{8,9},{9,8},{10,11... | collective-permute-start | bytes 196616 | tf_op jit(solution)/shard_map/ppermute | solution.py:722
  33.6 2.6 %collective-permute-start.12 = (f32[136,128]{1,0:T(8,128)S(1)}, f32[136,128]{1,0:T(8,128)S(1)}, u32[]{:S(2)}, u32[]{:S(2)}) collective-permute-start(f32[136,128]{1,0:T(8,128)S(1)} %shard_map.92.after), channel_id=1, source_target_pairs={{0,1},{1,0},{2,3},{3,2},{4,5},{5,4},{6,7},{7,6},{8,9},{9,8},{10,11... | collective-permute-start | bytes 208904 | tf_op jit(solution)/shard_map/ppermute | solution.py:722
  33.7 5.2 %collective-permute-start.14 = (f32[128,128]{1,0:T(8,128)S(1)}, f32[128,128]{1,0:T(8,128)S(1)}, u32[]{:S(2)}, u32[]{:S(2)}) collective-permute-start(f32[128,128]{1,0:T(8,128)S(1)} %add.10.after), channel_id=1, source_target_pairs={{0,2},{1,3},{2,0},{3,1},{4,6},{5,7},{6,4},{7,5},{8,10},{9,11},{10,... | collective-permute-start | bytes 196616 | tf_op jit(solution)/shard_map/ppermute | solution.py:722
  36.3 7.0 %collective-permute-start.13 = (f32[136,128]{1,0:T(8,128)S(1)}, f32[136,128]{1,0:T(8,128)S(1)}, u32[]{:S(2)}, u32[]{:S(2)}) collective-permute-start(f32[136,128]{1,0:T(8,128)S(1)} %add.11.rest_0_), channel_id=1, source_target_pairs={{0,2},{1,3},{2,0},{3,1},{4,6},{5,7},{6,4},{7,5},{8,10},{9,11},{10,... | collective-permute-start | bytes 208904 | tf_op jit(solution)/shard_map/ppermute | solution.py:722
  38.9 4.3 %collective-permute-start.15 = (f32[128,128]{1,0:T(8,128)S(1)}, f32[128,128]{1,0:T(8,128)S(1)}, u32[]{:S(2)}, u32[]{:S(2)}) collective-permute-start(f32[128,128]{1,0:T(8,128)S(1)} %add.12.rest_2_), channel_id=1, source_target_pairs={{0,16},{16,0},{1,17},{17,1},{2,18},{18,2},{3,19},{19,3},{4,20},{20... | collective-permute-start | bytes 196616 | tf_op jit(solution)/shard_map/ppermute | solution.py:703
